TPU v7x, 256 devices: a whole 4x4x8 slice. The times are simulated.
256 devices in a mesh: seq: 32 (over x, z), mlp: 8 (over y, core).
Axes of the slice: x: 4, y: 4, z: 8, core: 2. Of those that a mesh axis runs over, the one named last changes fastest.
Arguments:
- queries: bfloat16 [1024, 2560], P(('seq', 'mlp')), may hold values from -8 to 8
- new_kv: bfloat16 [1024, 512], P(('seq', 'mlp')), may hold values from -5 to 5
- kv_cache: bfloat16 [4352, 128, 512], P(('seq', 'mlp')), may hold values from -4 to 4, as said below
- lengths: int32 [256], replicated, may hold values from 256 to 16384, as said below
- page_table: int32 [256, 128], replicated, may hold values from -1 to 4351, as said below
- residual: bfloat16 [1024, 2560], P('seq', 'mlp'), may hold values from -3 to 3
- out_weight: bfloat16 [2560, 2560], P(None, 'mlp'), may hold values from -0.125 to 0.125
- norm_gain: float32 [2560], replicated, may hold values from 0.1 to 1.9
- gate_weight: bfloat16 [2560, 3840], P(None, 'mlp'), may hold values from -0.125 to 0.125
- up_weight: bfloat16 [2560, 3840], P(None, 'mlp'), may hold values from -0.125 to 0.125
- down_weight: bfloat16 [3840, 2560], P('mlp'), may hold values from -0.09375 to 0.09375
- next_gain: float32 [2560], replicated, may hold values from 0.1 to 1.9
- qkv_weight: bfloat16 [2560, 3072], P(None, 'mlp'), may hold values from -0.125 to 0.125
Outputs:
- attended: bfloat16 [1024, 2560], P(('seq', 'mlp'))
- residual_out: bfloat16 [1024, 2560], P('seq', 'mlp')
- next_qkv: bfloat16 [1024, 3072], P('seq', 'mlp')
Inputs may be any that keep to these rules, and one draw needn't show every extreme that they name: `lengths`: lengths have a heavy tail; at least one request has exactly 16384. page_table[r, p] is a slot exactly for the pages p holding positions max(0, lengths[r] - 2047) to lengths[r] - 1, and -1 elsewhere. Slots d * 17 to d * 17 + 16 lie on device d of seq+mlp. All pages of request r lie in consecutive slots of ONE device, whose mlp index is r modulo 8; a device may hold the pages of several requests or of none. No slot holds two pages; some device of every mlp index has all 17 slots in use. `kv_cache`: unused slots hold arbitrary values.
All inputs are finite; a program needn't handle non-finite values.
Results may differ from a plain program's by a relative error of at most 0.011.
Values may be sent and summed in bfloat16 or wider, within the bound.
No kernel may reach another device: no remote copies, remote signals or barrier semaphores. Data moves between devices by JAX's collectives and lax.ppermute only.
A program may use at most 64 MiB of HBM per device.

v0:
```python
import jax
import jax.numpy as jnp
from jax import lax
from jax.sharding import PartitionSpec as P

WINDOW = 2048


NEG_FILL = -1e30


def combine_parts(first, second):
    first_max, first_sum, first_acc = first
    second_max, second_sum, second_acc = second
    peak = jnp.maximum(first_max, second_max)
    first_factor = jnp.exp(first_max - peak)
    second_factor = jnp.exp(second_max - peak)
    return (
        peak,
        first_sum * first_factor + second_sum * second_factor,
        first_acc * first_factor[..., None] + second_acc * second_factor[..., None],
    )


def rms_norm(values, gain):
    floats = values.astype(jnp.float32)
    scaled = floats * lax.rsqrt(jnp.mean(floats * floats, axis=-1, keepdims=True) + 1e-06)
    return (scaled * gain).astype(jnp.bfloat16)


def shards(
    queries,
    new_kv,
    kv_cache,
    lengths,
    page_table,
    residual,
    out_weight,
    norm_gain,
    gate_weight,
    up_weight,
    down_weight,
    next_gain,
    qkv_weight,
):
    seq_count = lax.axis_size("seq")
    mlp_count = lax.axis_size("mlp")
    seq_place = lax.axis_index("seq")
    device = seq_place * mlp_count + lax.axis_index("mlp")
    slot_count = kv_cache.shape[0]
    page_len = kv_cache.shape[1]
    head_dim = kv_cache.shape[2] // 2
    token_count = queries.shape[0]
    width = queries.shape[1]
    head_count = width // head_dim
    request_total, page_count = page_table.shape
    scale = head_dim ** (-0.5)
    local_slot = page_table - device * slot_count
    inside = (local_slot >= 0) & (local_slot < slot_count)
    target = jnp.where(inside, local_slot, slot_count).reshape(-1)
    owners = jnp.broadcast_to(
        jnp.arange(request_total, dtype=jnp.int32)[:, None], page_table.shape
    ).reshape(-1)
    page_numbers = jnp.broadcast_to(
        jnp.arange(page_count, dtype=jnp.int32)[None, :], page_table.shape
    ).reshape(-1)
    slot_request = jnp.zeros((slot_count,), jnp.int32).at[target].set(owners, mode="drop")
    slot_page = jnp.zeros((slot_count,), jnp.int32).at[target].set(page_numbers, mode="drop")
    slot_used = jnp.zeros((slot_count,), jnp.bool_).at[target].set(True, mode="drop")
    column_rows = lax.all_gather(queries, "seq", axis=0, tiled=True)
    column_queries = column_rows.reshape(seq_count, token_count, head_count, head_dim)
    slot_column = slot_request // mlp_count
    slot_queries = column_queries[slot_column]
    cache_keys = kv_cache[:, :, :head_dim]
    cache_values = kv_cache[:, :, head_dim:]
    scores = (
        jnp.einsum("sqhd,skd->sqhk", slot_queries, cache_keys, preferred_element_type=jnp.float32)
        * scale
    )
    positions = slot_page[:, None] * page_len + jnp.arange(page_len, dtype=jnp.int32)[None, :]
    slot_length = lengths[slot_request]
    offsets = jnp.arange(token_count, dtype=jnp.int32)
    valid = (
        slot_used[:, None, None]
        & (positions[:, None, :] < slot_length[:, None, None])
        & (
            positions[:, None, :]
            >= slot_length[:, None, None] + offsets[None, :, None] - (WINDOW - 1)
        )
    )
    valid = valid[:, :, None, :]
    page_max = jnp.max(jnp.where(valid, scores, NEG_FILL), axis=-1)
    weights = jnp.where(valid, jnp.exp(scores - page_max[..., None]), 0.0)
    page_sum = jnp.sum(weights, axis=-1)
    page_acc = jnp.einsum(
        "sqhk,skd->sqhd",
        weights.astype(jnp.bfloat16),
        cache_values,
        preferred_element_type=jnp.float32,
    )
    member = (slot_column[None, :] == jnp.arange(seq_count, dtype=jnp.int32)[:, None]) & slot_used[
        None, :
    ]
    request_max = jnp.max(jnp.where(member[:, :, None, None], page_max[None], NEG_FILL), axis=1)
    rescale = jnp.exp(page_max - request_max[slot_column])
    member_float = member.astype(jnp.float32)
    request_sum = jnp.einsum(
        "rs,sqh->rqh", member_float, rescale * page_sum, precision=lax.Precision.HIGHEST
    )
    request_acc = jnp.einsum(
        "rs,sqhd->rqhd",
        member_float,
        rescale[..., None] * page_acc,
        precision=lax.Precision.HIGHEST,
    )
    got_max, got_sum, got_acc = (
        lax.all_to_all(request_max, "seq", split_axis=0, concat_axis=0, tiled=True),
        lax.all_to_all(request_sum, "seq", split_axis=0, concat_axis=0, tiled=True),
        lax.all_to_all(request_acc, "seq", split_axis=0, concat_axis=0, tiled=True),
    )
    peak = jnp.max(got_max, axis=0)
    factor = jnp.exp(got_max - peak[None])
    own_part = (
        peak,
        jnp.sum(factor * got_sum, axis=0),
        jnp.sum(factor[..., None] * got_acc, axis=0),
    )
    own_queries = queries.reshape(token_count, head_count, head_dim)
    new_keys = new_kv[:, :head_dim]
    new_values = new_kv[:, head_dim:]
    new_scores = (
        jnp.einsum("qhd,kd->qhk", own_queries, new_keys, preferred_element_type=jnp.float32) * scale
    )
    causal = (offsets[:, None] >= offsets[None, :])[:, None, :]
    new_max = jnp.max(jnp.where(causal, new_scores, NEG_FILL), axis=-1)
    new_weights = jnp.where(causal, jnp.exp(new_scores - new_max[..., None]), 0.0)
    new_sum = jnp.sum(new_weights, axis=-1)
    new_acc = jnp.einsum(
        "qhk,kd->qhd",
        new_weights.astype(jnp.bfloat16),
        new_values,
        preferred_element_type=jnp.float32,
    )
    final_max, final_sum, final_acc = combine_parts(own_part, (new_max, new_sum, new_acc))
    attended = (final_acc / final_sum[..., None]).reshape(token_count, width).astype(jnp.bfloat16)
    attention_out = jnp.dot(
        lax.all_gather(attended, "mlp", axis=0, tiled=True),
        out_weight,
        preferred_element_type=jnp.float32,
    )
    stream = (residual.astype(jnp.float32) + attention_out).astype(jnp.bfloat16)
    whole_stream = lax.all_gather(stream, "mlp", axis=1, tiled=True)
    normed = rms_norm(whole_stream, norm_gain)
    gate = jnp.dot(normed, gate_weight, preferred_element_type=jnp.float32)
    upward = jnp.dot(normed, up_weight, preferred_element_type=jnp.float32)
    hidden = (jax.nn.gelu(gate, approximate=True) * upward).astype(jnp.bfloat16)
    partial_down = jnp.dot(hidden, down_weight, preferred_element_type=jnp.float32)
    column_width = stream.shape[1]
    column_start = lax.axis_index("mlp") * column_width
    down_total = lax.psum(partial_down, "mlp")
    full_after = (whole_stream.astype(jnp.float32) + down_total).astype(jnp.bfloat16)
    shard_after = lax.dynamic_slice_in_dim(full_after, column_start, column_width, 1)
    normed_next = rms_norm(full_after, next_gain)
    next_qkv = jnp.dot(normed_next, qkv_weight, preferred_element_type=jnp.float32).astype(
        jnp.bfloat16
    )
    return (attended, shard_after, next_qkv)


def solution(mesh):
    return jax.shard_map(
        shards,
        mesh=mesh,
        in_specs=(
            P(("seq", "mlp"), None),
            P(("seq", "mlp"), None),
            P(("seq", "mlp"), None, None),
            P(),
            P(),
            P("seq", "mlp"),
            P(None, "mlp"),
            P(),
            P(None, "mlp"),
            P(None, "mlp"),
            P("mlp", None),
            P(),
            P(None, "mlp"),
        ),
        out_specs=(P(("seq", "mlp"), None), P("seq", "mlp"), P("seq", "mlp")),
        check_vma=False,
    )
```

profile of v0, /device:TPU:1, one launch (start us, length us, event | category | flops | bytes accessed | tf_op | source)
XLA Modules:
  0.0 616.1 jit_solution(3208878940347870312)
XLA Ops:
  7.2 1.1 and_select_fusion
  8.3 0.1 compare_select_fusion
  8.5 120.0 %scatter_custom_fusion = s32[17]{0:T(128)S(1)} fusion(s32[32768]{0:T(1024)S(1)} %bitcast.70, s32[32768]{0:T(1024)S(1)} %iota_bitcast_fusion.1, s32[]{:T(128)} %constant.28.clone.1), kind=kCustom, calls=%fused_computation.111 | custom fusion | bytes 72 | tf_op jit(solution)/shard_map/scatter | solution.py:67
  128.5 1.4 gather_fusion
  129.9 0.1 add_add_fusion
  130.0 120.0 %scatter_custom_fusion.2 = s32[17]{0:T(128)S(1)} fusion(s32[32768]{0:T(1024)S(1)} %bitcast.71, s32[32768]{0:T(1024)S(1)} %iota_bitcast_fusion, s32[]{:T(128)} %constant.28.clone.1), kind=kCustom, calls=%fused_computation.109 | custom fusion | bytes 72 | tf_op jit(solution)/shard_map/scatter | solution.py:68
  250.1 136.5 %scatter_custom_fusion.1 = pred[17]{0:T(512)(128)(4,1)S(1)} fusion(s32[32768]{0:T(1024)S(1)} %bitcast.72, pred[32768]{0:T(1024)(128)(4,1)S(1)} %broadcast.184, pred[]{:T(512)} %constant.20.clone.1), kind=kCustom, calls=%fused_computation.104 | custom fusion | bytes 18 | tf_op jit(solution)/shard_map/scatter | solution.py:69
  386.6 0.1 compare_and_fusion.1
  386.7 42.3 %all-gather = bf16[32,4,2560]{2,1,0:T(4,128)(2,1)S(1)} all-gather(bf16[1,4,2560]{2,1,0:T(4,128)(2,1)} %bitcast.74), channel_id=1, replica_groups=mesh['seq'=32,'mlp'=8] {'seq'}, dimensions={0}, use_global_device_ids=true | all-gather | bytes 675840 | tf_op jit(solution)/shard_map/all_gather | solution.py:70
  428.9 0.1 copy.49
  429.0 1.4 reshape.237
  430.4 2.7 gather_fusion.1
  433.1 0.1 compare_and_fusion
  433.2 2.0 select_reduce_fusion
  435.2 0.2 copy.50
  435.4 0.4 fusion.13
  435.9 0.1 fusion.43
  436.0 0.3 select_reduce_fusion.1
  436.2 0.7 copy.51
  436.9 1.4 gather_fusion.2
  438.4 0.2 fusion.37
  438.6 0.7 copy.58
  439.4 5.5 all-to-all-start.2
  444.8 2.7 convolution_multiply_fusion
  447.5 6.2 %all-to-all-done.2 = f32[32,4,10]{2,1,0:T(4,128)S(1)} async-done(((f32[32,4,10]{2,1,0:T(4,128)}), f32[32,4,10]{2,1,0:T(4,128)S(1)}, u32[]{:S(2)}, u32[]{:S(2)}) %all-to-all-start.2) | async-done | bytes 5152 | tf_op jit(solution)/shard_map/all_to_all | solution.py:118
  453.7 4.0 all-to-all-start
  457.7 2.3 fusion.11
  460.1 1.9 copy.55
  462.0 4.4 all-to-all-done
  466.4 4.9 all-to-all-start.1
  471.4 0.2 select_reduce_fusion.2
  471.6 0.1 fusion.46
  471.8 0.3 copy.52
  472.1 19.2 %all-to-all-done.1 = f32[32,4,10,256]{3,1,2,0:T(4,128)} async-done(((f32[32,4,10,256]{3,1,2,0:T(4,128)}), f32[32,4,10,256]{3,1,2,0:T(4,128)}, u32[]{:S(2)}, u32[]{:S(2)}) %all-to-all-start.1) | async-done | bytes 1310752 | tf_op jit(solution)/shard_map/all_to_all | solution.py:119
  491.3 1.7 multiply_reduce_fusion
  493.0 0.3 fusion.3
  493.3 29.2 %all-gather.1 = bf16[8,4,2560]{2,1,0:T(4,128)(2,1)S(1)} all-gather(bf16[1,4,2560]{2,1,0:T(4,128)(2,1)S(1)} %reshape.292), channel_id=1, replica_groups=mesh['seq'=32,'mlp'=8] {'mlp'}, dimensions={0}, use_global_device_ids=true | all-gather | bytes 184320 | tf_op jit(solution)/shard_map/all_gather | solution.py:147
  522.6 2.0 fusion.10
  524.6 12.8 %all-gather.2 = bf16[8,320,32]{1,2,0:T(8,128)(2,1)S(1)} all-gather(bf16[1,320,32]{1,2,0:T(8,128)(2,1)S(1)} %fusion.10), channel_id=1, replica_groups=mesh['seq'=32,'mlp'=8] {'mlp'}, dimensions={0}, use_global_device_ids=true | all-gather | bytes 184320 | tf_op jit(solution)/shard_map/all_gather | solution.py:152
  537.5 0.1 reshape.298
  537.6 0.1 fusion.18
  537.8 2.5 fusion.74
  540.3 3.8 fusion.9
  544.1 0.6 copy.63
  544.7 60.1 %all-reduce.2.cloned.1.call-done = f32[32,2560]{1,0:T(8,128)} async-done(((f32[32,2560]{1,0:T(8,128)}), f32[32,2560]{1,0:T(8,128)}) %all-reduce.2.cloned.1.call-update) | async-done | bytes 327696 | tf_op jit(solution)/shard_map/psum | solution.py:160
  604.8 1.1 fusion.15
  605.9 0.7 constant_dynamic-slice_fusion
  606.6 2.6 convolution_convert_fusion
  (33 shorter events, 0.6 us)
Async XLA Ops:
  7.2 533.1 %copy-start = (bf16[480,2560]{1,0:T(8,128)(2,1)S(1)}, bf16[480,2560]{1,0:T(8,128)(2,1)}, u32[]{:S(2)}) copy-start(bf16[480,2560]{1,0:T(8,128)(2,1)} %param.23) | copy-start | bytes 7372804
  439.4 14.3 %all-to-all-start.2 = ((f32[32,4,10]{2,1,0:T(4,128)}), f32[32,4,10]{2,1,0:T(4,128)S(1)}, u32[]{:S(2)}, u32[]{:S(2)}) async-start(f32[32,4,10]{2,1,0:T(4,128)} %copy.58), calls=%async_computation.2 | async-start | bytes 131072 | tf_op jit(solution)/shard_map/all_to_all | solution.py:118
  453.7 12.7 %all-to-all-start = ((f32[32,4,10]{2,1,0:T(4,128)}), f32[32,4,10]{2,1,0:T(4,128)S(1)}, u32[]{:S(2)}, u32[]{:S(2)}) async-start(f32[32,4,10]{2,1,0:T(4,128)} %copy.51), calls=%async_computation | async-start | bytes 131072 | tf_op jit(solution)/shard_map/all_to_all | solution.py:117
  462.0 9.4 %copy-start.1 = (bf16[4,2560]{1,0:T(4,128)(2,1)S(1)}, bf16[4,2560]{1,0:T(4,128)(2,1)}, u32[]{:S(2)}) copy-start(bf16[4,2560]{1,0:T(4,128)(2,1)} %param.13) | copy-start | bytes 61444
  462.0 9.4 %copy-start.5 = (bf16[4,512]{1,0:T(4,128)(2,1)S(1)}, bf16[4,512]{1,0:T(4,128)(2,1)}, u32[]{:S(2)}) copy-start(bf16[4,512]{1,0:T(4,128)(2,1)} %param.14) | copy-start | bytes 12292
  466.4 24.9 %all-to-all-start.1 = ((f32[32,4,10,256]{3,1,2,0:T(4,128)}), f32[32,4,10,256]{3,1,2,0:T(4,128)}, u32[]{:S(2)}, u32[]{:S(2)}) async-start(f32[32,4,10,256]{3,1,2,0:T(4,128)} %copy.55), calls=%async_computation.1 | async-start | bytes 2621440 | tf_op jit(solution)/shard_map/all_to_all | solution.py:119
  471.3 51.3 %copy-start.3 = (bf16[32,320]{1,0:T(8,128)(2,1)S(1)}, bf16[32,320]{1,0:T(8,128)(2,1)}, u32[]{:S(2)}) copy-start(bf16[32,320]{1,0:T(8,128)(2,1)} %param.18) | copy-start | bytes 61444
  471.3 133.5 %all-reduce.2.cloned.1.call-start = ((), (), s32[]{:S(2)}) async-start(), calls=%async_computation.3 | async-start | bytes 655360 | tf_op jit(solution)/shard_map/psum | solution.py:160
  522.6 15.2 %copy-start.2 = (f32[2560]{0:T(1024)S(1)}, f32[2560]{0:T(1024)}, u32[]{:S(2)}) copy-start(f32[2560]{0:T(1024)} %param.20) | copy-start | bytes 30724
  540.2 66.4 %copy-start.4 = (f32[2560]{0:T(1024)S(1)}, f32[2560]{0:T(1024)}, u32[]{:S(2)}) copy-start(f32[2560]{0:T(1024)} %param.24) | copy-start | bytes 30724
Sparse Core Ops, SparseCore 0:
  544.2 60.5 all-reduce.1
where the time goes:
time: 618 us; the launch traced here: 616 us
  local copies, waits for them, and re-layouts  389 us (63%)
  waiting for transfers between devices  89.9 us (15%)
  blocking collectives  84.3 us (14%)
  matrix products  18.6 us (3%)
  starting transfers between devices  14.4 us (2%)
  between operations  14.3 us (2%)
    scatter x1, local copies, waits for them, and re-layouts, shards(): jnp.zeros((slot_count,), jnp.bool_).at[target].set(True, mode='drop')  136 us
    scatter x1, local copies, waits for them, and re-layouts, shards(): jnp.zeros((slot_count,), jnp.int32).at[target].set(owners, mode='drop')  120 us
    scatter x1, local copies, waits for them, and re-layouts, shards(): jnp.zeros((slot_count,), jnp.int32).at[target]  120 us
    psum x1, waiting for transfers between devices, shards(): down_total = lax.psum(partial_down, 'mlp')  60.1 us
    all_gather x1, blocking collectives, shards(): column_rows = lax.all_gather(queries, 'seq', axis=0, tiled=True)  42.3 us
    all_gather x1, blocking collectives, shards(): lax.all_gather(attended, 'mlp', axis=0, tiled=True)  29.2 us
    all_to_all x1, waiting for transfers between devices, shards(): lax.all_to_all(request_acc, 'seq', split_axis=0, concat_axis=0, tiled=True)  19.2 us
    all_gather x1, blocking collectives, shards(): whole_stream = lax.all_gather(stream, 'mlp', axis=1, tiled=True)  12.8 us
  transfers between devices with their start and end apart: 4, of which 4 were waited for; matrix products, arithmetic and copies ran while one was open for 1% of the time, Pallas kernels for 0%

commit v1 on v0

v1 whole, which is shorter than its diff:
```python
import jax
import jax.numpy as jnp
from jax import lax
from jax.experimental import pallas as pl
from jax.experimental.pallas import tpu as pltpu
from jax.sharding import PartitionSpec as P

WINDOW = 2048
NEG_FILL = -1e30


def attend_pages(code_ref, length_ref, rows_ref, cache_ref, out_ref, max_ref, sum_ref, acc_ref):
    slot_count, page_len, kv_width = cache_ref.shape
    head_dim = kv_width // 2
    token_count = out_ref.shape[1]
    query_rows = out_ref.shape[2] // head_dim * token_count
    page_count = 128
    scale = head_dim ** (-0.5)
    token = lax.broadcasted_iota(jnp.int32, (query_rows, page_len), 0) % token_count
    lane = lax.broadcasted_iota(jnp.int32, (query_rows, page_len), 1)
    contract_last = (((1,), (1,)), ((), ()))
    for slot in range(slot_count):
        code = code_ref[slot]
        entry = jnp.maximum(code - 1, 0)
        source = entry // page_count
        page = entry % page_count
        length = jnp.where(code > 0, length_ref[source], 0)
        query = rows_ref[source, :query_rows, :]
        scores = (
            lax.dot_general(
                query, cache_ref[slot, :, :head_dim], contract_last, preferred_element_type=jnp.float32
            )
            * scale
        )
        position = page * page_len + lane
        valid = (position < length) & (position >= length + token - (WINDOW - 1))
        peak = jnp.max(jnp.where(valid, scores, NEG_FILL), axis=1, keepdims=True)
        weights = jnp.where(valid, jnp.exp(scores - peak), 0.0)
        max_ref[slot] = jnp.broadcast_to(peak, (query_rows, 128))
        sum_ref[slot] = jnp.broadcast_to(jnp.sum(weights, axis=1, keepdims=True), (query_rows, 128))
        acc_ref[slot] = jnp.dot(
            weights.astype(jnp.bfloat16),
            cache_ref[slot, :, head_dim:],
            preferred_element_type=jnp.float32,
        )
    last = slot_count
    for slot in range(slot_count):
        code = code_ref[slot]
        entry = jnp.maximum(code - 1, 0)
        source = entry // page_count
        before = code_ref[max(slot - 1, 0)]
        after = code_ref[min(slot + 1, slot_count - 1)]
        same_before = (before > 0) & ((before - 1) // page_count == source) & (slot > 0)
        same_after = (after > 0) & ((after - 1) // page_count == source) & (slot < slot_count - 1)
        used = code > 0

        @pl.when(used & jnp.logical_not(same_before))
        def _():
            query = rows_ref[source, :query_rows, :]
            fresh = rows_ref[source, query_rows:, :]
            scores = (
                lax.dot_general(query, fresh, contract_last, preferred_element_type=jnp.float32) * scale
            )
            row_token = lax.broadcasted_iota(jnp.int32, scores.shape, 0) % token_count
            column = lax.broadcasted_iota(jnp.int32, scores.shape, 1)
            valid = column <= row_token
            peak = jnp.max(jnp.where(valid, scores, NEG_FILL), axis=1, keepdims=True)
            weights = jnp.where(valid, jnp.exp(scores - peak), 0.0)
            total = jnp.sum(weights, axis=1, keepdims=True)
            rounded = weights.astype(jnp.bfloat16).astype(jnp.float32)
            acc = jnp.zeros((query_rows, head_dim), jnp.float32)
            for new in range(token_count):
                value = fresh[token_count + new : token_count + new + 1, :].astype(jnp.float32)
                acc = acc + rounded[:, new : new + 1] * value
            max_ref[last] = jnp.broadcast_to(peak, (query_rows, 128))
            sum_ref[last] = jnp.broadcast_to(total, (query_rows, 128))
            acc_ref[last] = acc

        @pl.when(used)
        def _():
            old_max = max_ref[last]
            page_max = max_ref[slot]
            peak = jnp.maximum(old_max, page_max)
            old_factor = jnp.exp(old_max - peak)
            page_factor = jnp.exp(page_max - peak)
            max_ref[last] = peak
            sum_ref[last] = sum_ref[last] * old_factor + sum_ref[slot] * page_factor
            acc_ref[last] = acc_ref[last] * jnp.concatenate([old_factor, old_factor], axis=1) + acc_ref[
                slot
            ] * jnp.concatenate([page_factor, page_factor], axis=1)

        @pl.when(used & jnp.logical_not(same_after))
        def _():
            total = sum_ref[last]
            result = acc_ref[last] / jnp.concatenate([total, total], axis=1)
            for head in range(query_rows // token_count):
                out_ref[source, :, head * head_dim : (head + 1) * head_dim] = result[
                    head * token_count : (head + 1) * token_count, :
                ].astype(jnp.bfloat16)


def feed_forward(stream_ref, gain_ref, gate_ref, up_ref, down_ref, keep_ref, send_ref, core_ref=None):
    parts, rows, width = stream_ref.shape
    square = jnp.zeros((rows, 1), jnp.float32)
    for part in range(parts):
        floats = stream_ref[part].astype(jnp.float32)
        square = square + jnp.sum(floats * floats, axis=1, keepdims=True)
    factor = lax.rsqrt(square / (parts * width) + 1e-06)
    gate = jnp.zeros((rows, gate_ref.shape[2]), jnp.float32)
    upward = jnp.zeros((rows, up_ref.shape[2]), jnp.float32)
    for part in range(parts):
        normed = (stream_ref[part].astype(jnp.float32) * factor * gain_ref[part]).astype(jnp.bfloat16)
        gate = gate + jnp.dot(normed, gate_ref[part], preferred_element_type=jnp.float32)
        upward = upward + jnp.dot(normed, up_ref[part], preferred_element_type=jnp.float32)
    hidden = (jax.nn.gelu(gate, approximate=True) * upward).astype(jnp.bfloat16)
    partial = jnp.dot(hidden, down_ref[...], preferred_element_type=jnp.float32)
    half = partial.shape[1] // 2
    keep_ref[...] = partial[:, :half]
    send_ref[...] = partial[:, half:]


def rms_norm(values, gain):
    floats = values.astype(jnp.float32)
    scaled = floats * lax.rsqrt(jnp.mean(floats * floats, axis=-1, keepdims=True) + 1e-06)
    return (scaled * gain).astype(jnp.bfloat16)


def spread(block, axis):
    copies = jnp.broadcast_to(block[None], (lax.axis_size(axis),) + block.shape)
    return lax.all_to_all(copies, axis, split_axis=0, concat_axis=0, tiled=True)


def shards(
    queries,
    new_kv,
    kv_cache,
    lengths,
    page_table,
    residual,
    out_weight,
    norm_gain,
    gate_weight,
    up_weight,
    down_weight,
    next_gain,
    qkv_weight,
):
    seq_count = lax.axis_size("seq")
    mlp_count = lax.axis_size("mlp")
    seq_place = lax.axis_index("seq")
    mlp_place = lax.axis_index("mlp")
    device = seq_place * mlp_count + mlp_place
    slot_count, page_len, kv_width = kv_cache.shape
    head_dim = kv_width // 2
    token_count, width = queries.shape
    head_count = width // head_dim
    page_count = page_table.shape[1]
    bf16 = jnp.bfloat16

    own_rows = jnp.concatenate(
        [
            queries.reshape(token_count, head_count, head_dim).transpose(1, 0, 2).reshape(-1, head_dim),
            new_kv[:, :head_dim],
            new_kv[:, head_dim:],
        ],
        axis=0,
    )
    column_rows = spread(own_rows, "seq")

    column_table = lax.dynamic_index_in_dim(
        page_table.reshape(seq_count, mlp_count, page_count), mlp_place, 1, keepdims=False
    )
    column_lengths = lax.dynamic_index_in_dim(
        lengths.reshape(seq_count, mlp_count), mlp_place, 1, keepdims=False
    )
    entry = (
        jnp.arange(seq_count, dtype=jnp.int32)[:, None] * page_count
        + jnp.arange(page_count, dtype=jnp.int32)[None, :]
        + 1
    )
    slots = device * slot_count + jnp.arange(slot_count, dtype=jnp.int32)
    codes = jnp.max(
        jnp.where(column_table[None] == slots[:, None, None], entry[None], 0), axis=(1, 2)
    )
    own_table = lax.dynamic_index_in_dim(column_table, seq_place, 0, keepdims=False)
    holder = jnp.max(own_table) // (slot_count * mlp_count)

    smem = pl.BlockSpec(memory_space=pltpu.SMEM)
    vmem = pl.BlockSpec(memory_space=pltpu.VMEM)
    query_rows = token_count * head_count
    held = pl.pallas_call(
        attend_pages,
        out_shape=jax.ShapeDtypeStruct((seq_count, token_count, width), bf16),
        in_specs=[smem, smem, vmem, vmem],
        out_specs=vmem,
        scratch_shapes=[
            pltpu.VMEM((slot_count + 1, query_rows, 128), jnp.float32),
            pltpu.VMEM((slot_count + 1, query_rows, 128), jnp.float32),
            pltpu.VMEM((slot_count + 1, query_rows, head_dim), jnp.float32),
        ],
        name="attend_pages",
    )(codes, column_lengths, column_rows, kv_cache)
    returned = lax.all_to_all(held, "seq", split_axis=0, concat_axis=0, tiled=True)
    attended = lax.dynamic_index_in_dim(returned, holder, 0, keepdims=False)

    rows = spread(attended, "mlp").reshape(mlp_count * token_count, width)
    attention_out = jnp.dot(rows, out_weight, preferred_element_type=jnp.float32)
    stream = (residual.astype(jnp.float32) + attention_out).astype(bf16)
    streams = spread(stream, "mlp")

    row_count, part_width = stream.shape
    hidden_count = gate_weight.shape[1]
    half = width // 2
    low, high = pl.pallas_call(
        feed_forward,
        out_shape=[jax.ShapeDtypeStruct((row_count, half), jnp.float32)] * 2,
        in_specs=[vmem] * 5,
        out_specs=[vmem] * 2,
        name="feed_forward",
    )(
        streams,
        norm_gain.reshape(mlp_count, 1, part_width),
        gate_weight.reshape(mlp_count, part_width, hidden_count),
        up_weight.reshape(mlp_count, part_width, hidden_count),
        down_weight,
    )
    is_high = mlp_place % 2 == 1
    keep = jnp.where(is_high, high, low)
    send = jnp.where(is_high, low, high).astype(bf16)
    pair = [(i, i ^ 1) for i in range(mlp_count)]
    chip_half = keep + lax.ppermute(send, "mlp", pair).astype(jnp.float32)
    chip_send = chip_half.astype(bf16)
    total_half = chip_half
    for shift in (2, 6, 4):
        got = lax.ppermute(chip_send, "mlp", [(i, (i + shift) % mlp_count) for i in range(mlp_count)])
        total_half = total_half + got.astype(jnp.float32)
    whole_stream = streams.transpose(1, 0, 2).reshape(row_count, width)
    stream_half = jnp.where(is_high, whole_stream[:, half:], whole_stream[:, :half])
    after_half = (stream_half.astype(jnp.float32) + total_half).astype(bf16)
    other_half = lax.ppermute(after_half, "mlp", pair)
    full_after = jnp.concatenate(
        [jnp.where(is_high, other_half, after_half), jnp.where(is_high, after_half, other_half)], axis=1
    )
    shard_after = lax.dynamic_slice_in_dim(full_after, mlp_place * part_width, part_width, 1)
    normed_next = rms_norm(full_after, next_gain)
    next_qkv = jnp.dot(normed_next, qkv_weight, preferred_element_type=jnp.float32).astype(bf16)
    return (attended, shard_after, next_qkv)


def solution(mesh):
    return jax.shard_map(
        shards,
        mesh=mesh,
        in_specs=(
            P(("seq", "mlp"), None),
            P(("seq", "mlp"), None),
            P(("seq", "mlp"), None, None),
            P(),
            P(),
            P("seq", "mlp"),
            P(None, "mlp"),
            P(),
            P(None, "mlp"),
            P(None, "mlp"),
            P("mlp", None),
            P(),
            P(None, "mlp"),
        ),
        out_specs=(P(("seq", "mlp"), None), P("seq", "mlp"), P("seq", "mlp")),
        check_vma=False,
    )
```

time: 618 us -> 123 us (0.20)
  local copies, waits for them, and re-layouts: 389 us -> 17.2 us
  blocking collectives: 84.3 us -> 14.8 us
  waiting for transfers between devices: 89.9 us -> 33.9 us
  starting transfers between devices: 14.4 us -> 31.2 us
  matrix products: 18.6 us -> 3.08 us
  Pallas kernels: 0 us -> 13.3 us
  between operations: 14.3 us -> 2.78 us
    scatter x3 -> x0, local copies, waits for them, and re-layouts: 377 us -> none  [the longest x1 136 us: shards(): jnp.zeros((slot_count,), jnp.bool_).at[target].set(True, mode='drop')]
    all_gather x3 -> x0, blocking collectives: 84.3 us -> none  [the longest x1 42.3 us: shards(): column_rows = lax.all_gather(queries, 'seq', axis=0, tiled=True)]
    psum x1 -> x0, waiting for transfers between devices: 60.1 us -> none  [shards(): down_total = lax.psum(partial_down, 'mlp')]
    all_to_all x0 -> x1, blocking collectives: none -> 14.8 us  [spread(): return lax.all_to_all(copies, axis, split_axis=0, concat_axis=0, tiled=True)]
    dot_general x9 -> x1, matrix products: 15.9 us -> 2.01 us  [shards(): jnp.dot(rows, out_weight, preferred_element_type=jnp.float32)]
    pallas_call x0 -> x2, Pallas kernels: none -> 13.3 us  [the longest x1 7.65 us: shards(): pl.pallas_call(attend_pages, out_shape=jax.ShapeDtypeStruct((seq_count, t...]
    all_to_all x3, starting transfers between devices: 14.4 us -> 24.7 us  [the longest x2 16.1 us: spread(): return lax.all_to_all(copies, axis, split_axis=0, concat_axis=0, tiled=True)]
    unnamed x15 -> x18, local copies, waits for them, and re-layouts: 0.74 us -> 10.3 us
  transfers between devices with their start and end apart: 4 -> 8, of which waited for: 4 -> 5; matrix products, arithmetic and copies ran while one was open for 1% -> 12% of each run, Pallas kernels for 0% -> 0%
where the time goes in v1:
time: 123 us; the launch traced here: 122 us
  waiting for transfers between devices  33.9 us (28%)
  starting transfers between devices  31.2 us (25%)
  local copies, waits for them, and re-layouts  17.2 us (14%)
  blocking collectives  14.8 us (12%)
  Pallas kernels  13.3 us (11%)
  other arithmetic  6.2 us (5%)
  matrix products  3.08 us (3%)
  between operations  2.78 us (2%)
    all_to_all x2, waiting for transfers between devices, spread(): return lax.all_to_all(copies, axis, split_axis=0, concat_axis=0, tiled=True)  16.4 us
    all_to_all x2, starting transfers between devices, spread(): return lax.all_to_all(copies, axis, split_axis=0, concat_axis=0, tiled=True)  16.1 us
    all_to_all x1, blocking collectives, spread(): return lax.all_to_all(copies, axis, split_axis=0, concat_axis=0, tiled=True)  14.8 us
    all_to_all x1, waiting for transfers between devices, shards(): lax.all_to_all(held, 'seq', split_axis=0, concat_axis=0, tiled=True)  13.4 us
    unnamed x18, local copies, waits for them, and re-layouts  10.3 us
    all_to_all x1, starting transfers between devices, shards(): lax.all_to_all(held, 'seq', split_axis=0, concat_axis=0, tiled=True)  8.6 us
    pallas_call x1, Pallas kernels, shards(): pl.pallas_call(attend_pages, out_shape=jax.ShapeDtypeStruct((seq_count, t...  7.65 us
    pallas_call x1, Pallas kernels, shards(): pl.pallas_call(feed_forward, out_shape=[jax.ShapeDtypeStruct((row_count,...  5.6 us
  transfers between devices with their start and end apart: 8, of which 5 were waited for; matrix products, arithmetic and copies ran while one was open for 12% of the time, Pallas kernels for 0%

profile of v1, /device:TPU:1, one launch (start us, length us, event | category | flops | bytes accessed | tf_op | source)
XLA Modules:
  0.0 122.4 jit_solution(8954532577394526646)
XLA Ops:
  0.6 0.0 copy-start
  0.6 0.0 copy-start.7
  0.7 0.8 fusion.11
  1.5 0.7 reshape.79
  2.3 0.9 broadcast_in_dim.20
  3.2 11.9 %all-to-all-start = ((bf16[32,48,256]{2,1,0:T(8,128)(2,1)}), bf16[32,48,256]{2,1,0:T(8,128)(2,1)S(1)}, u32[]{:S(2)}, u32[]{:S(2)}) async-start(bf16[32,48,256]{2,1,0:T(8,128)(2,1)} %broadcast_in_dim.20), calls=%async_computation | async-start | bytes 1572864 | tf_op jit(solution)/shard_map/all_to_all | solution.py:130
  15.1 0.0 copy-done.7
  15.1 0.1 reshape.78
  15.2 0.7 dynamic-slice_reduce_fusion.length_ref
  15.9 0.9 constant_dynamic-slice_fusion.1
  16.8 0.1 add_add_fusion
  16.9 1.0 select_reduce_fusion.code_ref
  17.9 16.4 %all-to-all-done.rows_ref = bf16[32,48,256]{2,1,0:T(8,128)(2,1)S(1)} async-done(((bf16[32,48,256]{2,1,0:T(8,128)(2,1)}), bf16[32,48,256]{2,1,0:T(8,128)(2,1)S(1)}, u32[]{:S(2)}, u32[]{:S(2)}) %all-to-all-start) | async-done | bytes 786464 | tf_op jit(solution)/shard_map/all_to_all | solution.py:130
  34.4 0.9 copy-done.1
  35.2 7.7 %attend_pages.1 = bf16[32,4,2560]{2,1,0:T(4,128)(2,1)} custom-call(s32[17]{0:T(128)} %select_reduce_fusion.code_ref, s32[32]{0:T(128)} %dynamic-slice_reduce_fusion.length_ref, bf16[32,48,256]{2,1,0:T(8,128)(2,1)} %copy-done.1, bf16[17,128,512]{2,1,0:T(8,128)(2,1)} %cache_ref.1), custom_call_target="tpu_custom_call" | custom-call | tf_op jit(solution)/shard_map/attend_pages/pallas_call | solution.py:191
  42.9 8.6 %all-to-all-start.1 = ((bf16[32,4,2560]{2,1,0:T(4,128)(2,1)}), bf16[32,4,2560]{2,1,0:T(4,128)(2,1)S(1)}, u32[]{:S(2)}, u32[]{:S(2)}) async-start(bf16[32,4,2560]{2,1,0:T(4,128)(2,1)} %attend_pages.1), calls=%async_computation.1 | async-start | bytes 1310720 | tf_op jit(solution)/shard_map/all_to_all | solution.py:203
  51.5 1.3 %fusion.9 = s32[]{:T(128)} fusion(s32[32,8,128]{2,1,0:T(8,128)} %bitcast.17, s32[]{:T(128)S(6)} %select_n.65, s32[]{:T(128)S(6)} %select_n.66), kind=kLoop, calls=%fused_computation.28 | loop fusion | flops 127 | bytes 524 | tf_op jit(solution)/shard_map/reduce_max | solution.py:186
  54.8 13.4 %all-to-all-done.1 = bf16[32,4,2560]{2,1,0:T(4,128)(2,1)S(1)} async-done(((bf16[32,4,2560]{2,1,0:T(4,128)(2,1)}), bf16[32,4,2560]{2,1,0:T(4,128)(2,1)S(1)}, u32[]{:S(2)}, u32[]{:S(2)}) %all-to-all-start.1) | async-done | bytes 655392 | tf_op jit(solution)/shard_map/all_to_all | solution.py:203
  68.2 0.0 copy-start.3
  68.3 14.8 %all_to_all.20 = bf16[8,4,2560]{2,1,0:T(4,128)(2,1)S(1)} all-to-all(bf16[8,4,2560]{2,1,0:T(4,128)(2,1)S(1)} %broadcast_in_dim.21), channel_id=1, replica_groups=mesh['seq'=32,'mlp'=8] {'mlp'}, dimensions={0} | all-to-all | bytes 327680 | tf_op jit(solution)/shard_map/all_to_all | solution.py:130
  83.1 0.0 copy-done.4
  83.1 2.0 %fusion = bf16[32,320]{1,0:T(8,128)(2,1)S(1)} fusion(bf16[32,2560]{1,0:T(8,128)(2,1)S(1)} %reshape.81, bf16[2560,320]{0,1:T(8,128)(2,1)} %param.19, bf16[32,320]{1,0:T(8,128)(2,1)S(1)} %copy-done.4), kind=kOutput, calls=%fused_computation.1 | convolution fusion | flops 52459520 | bytes 1843200 | tf_op jit(solution)/shard_map/dot_general | solution.py:207
  85.2 0.7 broadcast_in_dim.22
  85.9 4.2 %all-to-all-start.3 = ((bf16[8,32,320]{2,1,0:T(8,128)(2,1)}), bf16[8,32,320]{2,1,0:T(8,128)(2,1)S(1)}, u32[]{:S(2)}, u32[]{:S(2)}) async-start(bf16[8,32,320]{2,1,0:T(8,128)(2,1)} %broadcast_in_dim.22), calls=%async_computation.3 | async-start | bytes 393216 | tf_op jit(solution)/shard_map/all_to_all | solution.py:130
  90.1 4.4 %copy.28 = bf16[2560,480]{1,0:T(8,128)(2,1)} copy(bf16[2560,480]{0,1:T(8,128)(2,1)} %param.21) | data formatting | bytes 4915200 | tf_op args[8]
  94.4 4.4 %copy.29 = bf16[2560,480]{1,0:T(8,128)(2,1)} copy(bf16[2560,480]{0,1:T(8,128)(2,1)} %param.22) | data formatting | bytes 4915200 | tf_op args[9]
  98.8 0.7 reshape.83.gain_ref
  99.5 0.0 all-to-all-done.3.stream_ref
  99.5 0.7 copy-done.2
  100.2 5.6 %feed_forward.1 = (f32[32,1280]{1,0:T(8,128)}, f32[32,1280]{1,0:T(8,128)}) custom-call(bf16[8,32,320]{2,1,0:T(8,128)(2,1)} %copy-done.2, f32[8,1,320]{2,1,0:T(1,128)} %reshape.83.gain_ref, bf16[8,320,480]{2,1,0:T(8,128)(2,1)} %bitcast.11, bf16[8,320,480]{2,1,0:T(8,128)(2,1)} %bitcast.12, bf16[480,2560]{1,0:T(8,128)(2,1)} %down_ref.1), custom_call_target="tpu_custom_call" | custom-call | tf_op jit(solution)/shard_map/feed_forward/pallas_call | solution.py:214
  105.8 0.9 select_convert_fusion
  106.7 0.2 collective-permute-start
  106.9 1.2 collective-permute-done
  108.1 0.9 fusion.8
  109.0 1.5 %collective-permute-start.1 = (bf16[32,1280]{1,0:T(8,128)(2,1)S(1)}, bf16[32,1280]{1,0:T(8,128)(2,1)S(1)}, u32[]{:S(2)}, u32[]{:S(2)}) collective-permute-start(bf16[32,1280]{1,0:T(8,128)(2,1)S(1)} %fusion.8), channel_id=1, source_target_pairs={{0,2},{1,3},{2,4},{3,5},{4,6},{5,7},{6,0},{7,1},{8,10},{9,11},{10,... | collective-permute-start | bytes 245768 | tf_op jit(solution)/shard_map/ppermute | solution.py:235
  110.5 1.3 %collective-permute-start.2 = (bf16[32,1280]{1,0:T(8,128)(2,1)S(1)}, bf16[32,1280]{1,0:T(8,128)(2,1)S(1)}, u32[]{:S(2)}, u32[]{:S(2)}) collective-permute-start(bf16[32,1280]{1,0:T(8,128)(2,1)S(1)} %fusion.8), channel_id=1, source_target_pairs={{0,6},{1,7},{2,0},{3,1},{4,2},{5,3},{6,4},{7,5},{8,14},{9,15},{10,... | collective-permute-start | bytes 245768 | tf_op jit(solution)/shard_map/ppermute | solution.py:235
  111.8 1.7 %collective-permute-start.3 = (bf16[32,1280]{1,0:T(8,128)(2,1)S(1)}, bf16[32,1280]{1,0:T(8,128)(2,1)S(1)}, u32[]{:S(2)}, u32[]{:S(2)}) collective-permute-start(bf16[32,1280]{1,0:T(8,128)(2,1)S(1)} %fusion.8), channel_id=1, source_target_pairs={{0,4},{1,5},{2,6},{3,7},{4,0},{5,1},{6,2},{7,3},{8,12},{9,13},{10,... | collective-permute-start | bytes 245768 | tf_op jit(solution)/shard_map/ppermute | solution.py:235
  113.5 1.0 copy.27
  114.5 0.2 reshape.82
  114.7 0.0 collective-permute-done.1
  114.7 0.0 collective-permute-done.2
  114.7 2.0 %collective-permute-done.3 = bf16[32,1280]{1,0:T(8,128)(2,1)S(1)} collective-permute-done((bf16[32,1280]{1,0:T(8,128)(2,1)S(1)}, bf16[32,1280]{1,0:T(8,128)(2,1)S(1)}, u32[]{:S(2)}, u32[]{:S(2)}) %collective-permute-start.3) | collective-permute-done | bytes 81952 | tf_op jit(solution)/shard_map/ppermute | solution.py:235
  116.6 1.0 add_convert_fusion
  117.6 1.9 %collective-permute-start.4 = (bf16[32,1280]{1,0:T(8,128)(2,1)S(1)}, bf16[32,1280]{1,0:T(8,128)(2,1)S(1)}, u32[]{:S(2)}, u32[]{:S(2)}) collective-permute-start(bf16[32,1280]{1,0:T(8,128)(2,1)S(1)} %add_convert_fusion), channel_id=1, source_target_pairs={{0,1},{1,0},{2,3},{3,2},{4,5},{5,4},{6,7},{7,6},{8,9},{9,8},{10,11... | collective-permute-start | bytes 245768 | tf_op jit(solution)/shard_map/ppermute | solution.py:240
  119.5 0.9 collective-permute-done.4
  120.5 0.1 fusion.1
  120.6 0.7 fusion.7
  121.4 1.1 convolution_convert_fusion
  (19 shorter events, 0.2 us)
Async XLA Ops:
  0.6 120.7 %copy-start = (bf16[2560,384]{1,0:T(8,128)(2,1)S(1)}, bf16[2560,384]{1,0:T(8,128)(2,1)}, u32[]{:S(2)}) copy-start(bf16[2560,384]{1,0:T(8,128)(2,1)} %param.25) | copy-start | bytes 5898244
  0.6 14.5 %copy-start.7 = (s32[256]{0:T(256)S(1)}, s32[256]{0:T(256)}, u32[]{:S(2)}) copy-start(s32[256]{0:T(256)} %param.16) | copy-start | bytes 3076
  3.2 31.1 %all-to-all-start = ((bf16[32,48,256]{2,1,0:T(8,128)(2,1)}), bf16[32,48,256]{2,1,0:T(8,128)(2,1)S(1)}, u32[]{:S(2)}, u32[]{:S(2)}) async-start(bf16[32,48,256]{2,1,0:T(8,128)(2,1)} %broadcast_in_dim.20), calls=%async_computation | async-start | bytes 1572864 | tf_op jit(solution)/shard_map/all_to_all | solution.py:130
  34.4 0.9 copy-start.1
  42.9 40.2 %copy-start.4 = (bf16[32,320]{1,0:T(8,128)(2,1)S(1)}, bf16[32,320]{1,0:T(8,128)(2,1)}, u32[]{:S(2)}) copy-start(bf16[32,320]{1,0:T(8,128)(2,1)} %param.18) | copy-start | bytes 61444
  42.9 25.3 %all-to-all-start.1 = ((bf16[32,4,2560]{2,1,0:T(4,128)(2,1)}), bf16[32,4,2560]{2,1,0:T(4,128)(2,1)S(1)}, u32[]{:S(2)}, u32[]{:S(2)}) async-start(bf16[32,4,2560]{2,1,0:T(4,128)(2,1)} %attend_pages.1), calls=%async_computation.1 | async-start | bytes 1310720 | tf_op jit(solution)/shard_map/all_to_all | solution.py:203
  68.2 26.2 %copy-start.3 = (bf16[4,2560]{1,0:T(4,128)(2,1)}, bf16[4,2560]{1,0:T(4,128)(2,1)S(1)}, u32[]{:S(2)}) copy-start(bf16[4,2560]{1,0:T(4,128)(2,1)S(1)} %dynamic-slice_bitcast_fusion) | copy-start | bytes 61444
  85.9 13.6 %all-to-all-start.3 = ((bf16[8,32,320]{2,1,0:T(8,128)(2,1)}), bf16[8,32,320]{2,1,0:T(8,128)(2,1)S(1)}, u32[]{:S(2)}, u32[]{:S(2)}) async-start(bf16[8,32,320]{2,1,0:T(8,128)(2,1)} %broadcast_in_dim.22), calls=%async_computation.3 | async-start | bytes 393216 | tf_op jit(solution)/shard_map/all_to_all | solution.py:130
  94.4 4.4 %copy-start.6 = (f32[2560]{0:T(1024)S(1)}, f32[2560]{0:T(1024)}, u32[]{:S(2)}) copy-start(f32[2560]{0:T(1024)} %param.20) | copy-start | bytes 30724
  99.5 0.7 copy-start.2
  105.8 15.6 %copy-start.5 = (f32[2560]{0:T(1024)S(1)}, f32[2560]{0:T(1024)}, u32[]{:S(2)}) copy-start(f32[2560]{0:T(1024)} %param.24) | copy-start | bytes 30724
  106.7 1.4 %collective-permute-start = (bf16[32,1280]{1,0:T(8,128)(2,1)S(1)}, bf16[32,1280]{1,0:T(8,128)(2,1)S(1)}, u32[]{:S(2)}, u32[]{:S(2)}) collective-permute-start(bf16[32,1280]{1,0:T(8,128)(2,1)S(1)} %select_convert_fusion), channel_id=1, source_target_pairs={{0,1},{1,0},{2,3},{3,2},{4,5},{5,4},{6,7},{7,6},{8,9},{9,8},{10,11... | collective-permute-start | bytes 245768 | tf_op jit(solution)/shard_map/ppermute | solution.py:231
  109.0 5.6 %collective-permute-start.1 = (bf16[32,1280]{1,0:T(8,128)(2,1)S(1)}, bf16[32,1280]{1,0:T(8,128)(2,1)S(1)}, u32[]{:S(2)}, u32[]{:S(2)}) collective-permute-start(bf16[32,1280]{1,0:T(8,128)(2,1)S(1)} %fusion.8), channel_id=1, source_target_pairs={{0,2},{1,3},{2,4},{3,5},{4,6},{5,7},{6,0},{7,1},{8,10},{9,11},{10,... | collective-permute-start | bytes 245768 | tf_op jit(solution)/shard_map/ppermute | solution.py:235
  110.5 4.2 %collective-permute-start.2 = (bf16[32,1280]{1,0:T(8,128)(2,1)S(1)}, bf16[32,1280]{1,0:T(8,128)(2,1)S(1)}, u32[]{:S(2)}, u32[]{:S(2)}) collective-permute-start(bf16[32,1280]{1,0:T(8,128)(2,1)S(1)} %fusion.8), channel_id=1, source_target_pairs={{0,6},{1,7},{2,0},{3,1},{4,2},{5,3},{6,4},{7,5},{8,14},{9,15},{10,... | collective-permute-start | bytes 245768 | tf_op jit(solution)/shard_map/ppermute | solution.py:235
  111.8 4.8 %collective-permute-start.3 = (bf16[32,1280]{1,0:T(8,128)(2,1)S(1)}, bf16[32,1280]{1,0:T(8,128)(2,1)S(1)}, u32[]{:S(2)}, u32[]{:S(2)}) collective-permute-start(bf16[32,1280]{1,0:T(8,128)(2,1)S(1)} %fusion.8), channel_id=1, source_target_pairs={{0,4},{1,5},{2,6},{3,7},{4,0},{5,1},{6,2},{7,3},{8,12},{9,13},{10,... | collective-permute-start | bytes 245768 | tf_op jit(solution)/shard_map/ppermute | solution.py:235
  117.6 2.8 %collective-permute-start.4 = (bf16[32,1280]{1,0:T(8,128)(2,1)S(1)}, bf16[32,1280]{1,0:T(8,128)(2,1)S(1)}, u32[]{:S(2)}, u32[]{:S(2)}) collective-permute-start(bf16[32,1280]{1,0:T(8,128)(2,1)S(1)} %add_convert_fusion), channel_id=1, source_target_pairs={{0,1},{1,0},{2,3},{3,2},{4,5},{5,4},{6,7},{7,6},{8,9},{9,8},{10,11... | collective-permute-start | bytes 245768 | tf_op jit(solution)/shard_map/ppermute | solution.py:240

commit v2 on v1

v2 whole, which is shorter than its diff:
```python
import jax
import jax.numpy as jnp
from jax import lax
from jax.experimental import pallas as pl
from jax.experimental.pallas import tpu as pltpu
from jax.sharding import PartitionSpec as P

WINDOW = 2048
NEG_FILL = -1e30
LAST = (((1,), (1,)), ((), ()))
F32 = jnp.float32
BF16 = jnp.bfloat16


def head_major(values, head_dim):
    width = values.shape[1]
    return jnp.concatenate(
        [values[:, start : start + head_dim] for start in range(0, width, head_dim)], axis=0
    )


def put_heads(column, token_count, lanes):
    lane = lax.broadcasted_iota(jnp.int32, (token_count, lanes), 1)
    placed = jnp.zeros((token_count, lanes), F32)
    for head in range(column.shape[0] // token_count):
        part = column[head * token_count : (head + 1) * token_count, :]
        placed = jnp.where(lane == head, part, placed)
    return placed


def send_queries(queries_ref, out_ref):
    rows = head_major(queries_ref[...].astype(F32), out_ref.shape[2]).astype(BF16)
    for place in range(out_ref.shape[0]):
        out_ref[place] = rows


def attend_new(queries_ref, new_ref, max_ref, sum_ref, acc_ref):
    token_count, width = queries_ref.shape
    head_dim = new_ref.shape[1] // 2
    query = head_major(queries_ref[...].astype(F32), head_dim).astype(BF16)
    scores = lax.dot_general(
        query, new_ref[:, :head_dim], LAST, preferred_element_type=F32
    ) * head_dim ** (-0.5)
    token = lax.broadcasted_iota(jnp.int32, scores.shape, 0) % token_count
    column = lax.broadcasted_iota(jnp.int32, scores.shape, 1)
    valid = column <= token
    peak = jnp.max(jnp.where(valid, scores, NEG_FILL), axis=1, keepdims=True)
    weights = jnp.where(valid, jnp.exp(scores - peak), 0.0)
    rounded = weights.astype(BF16).astype(F32)
    values = new_ref[:, head_dim:].astype(F32)
    acc = jnp.zeros((query.shape[0], head_dim), F32)
    for new in range(token_count):
        acc = acc + rounded[:, new : new + 1] * values[new : new + 1, :]
    max_ref[...] = put_heads(peak, token_count, max_ref.shape[1])
    sum_ref[...] = put_heads(jnp.sum(weights, axis=1, keepdims=True), token_count, sum_ref.shape[1])
    for head in range(width // head_dim):
        acc_ref[:, head * head_dim : (head + 1) * head_dim] = acc[
            head * token_count : (head + 1) * token_count, :
        ]


def attend_pages(
    code_ref, length_ref, rows_ref, far_ref, out_ref, max_ref, sum_ref, acc_ref, cache_ref, copied
):
    slot_count, page_len, kv_width = cache_ref.shape
    head_dim = kv_width // 2
    token_count = out_ref.shape[1]
    width = out_ref.shape[2] - 128
    query_rows = rows_ref.shape[1]
    head_count = width // head_dim
    page_count = 128
    scale = head_dim ** (-0.5)
    copies = [
        pltpu.make_async_copy(far_ref.at[slot], cache_ref.at[slot], copied.at[slot])
        for slot in range(slot_count)
    ]
    for copy in copies:
        copy.start()
    token = lax.broadcasted_iota(jnp.int32, (query_rows, page_len), 0) % token_count
    lane = lax.broadcasted_iota(jnp.int32, (query_rows, page_len), 1)
    for slot in range(slot_count):
        code = code_ref[slot]
        entry = jnp.maximum(code - 1, 0)
        source = entry // page_count
        page = entry % page_count
        length = jnp.where(code > 0, length_ref[source], 0)
        copies[slot].wait()
        scores = (
            lax.dot_general(
                rows_ref[source], cache_ref[slot, :, :head_dim], LAST, preferred_element_type=F32
            )
            * scale
        )
        position = page * page_len + lane
        valid = (position < length) & (position >= length + token - (WINDOW - 1))
        peak = jnp.max(jnp.where(valid, scores, NEG_FILL), axis=1, keepdims=True)
        weights = jnp.where(valid, jnp.exp(scores - peak), 0.0)
        max_ref[slot] = jnp.broadcast_to(peak, (query_rows, 128))
        sum_ref[slot] = jnp.broadcast_to(jnp.sum(weights, axis=1, keepdims=True), (query_rows, 128))
        acc_ref[slot] = jnp.dot(
            weights.astype(BF16), cache_ref[slot, :, head_dim:], preferred_element_type=F32
        )
    last = slot_count
    for slot in range(slot_count):
        code = code_ref[slot]
        source = jnp.maximum(code - 1, 0) // page_count
        before = code_ref[max(slot - 1, 0)]
        after = code_ref[min(slot + 1, slot_count - 1)]
        same_before = (before > 0) & ((before - 1) // page_count == source) & (slot > 0)
        same_after = (after > 0) & ((after - 1) // page_count == source) & (slot < slot_count - 1)
        used = code > 0

        @pl.when(used & jnp.logical_not(same_before))
        def _():
            max_ref[last] = max_ref[slot]
            sum_ref[last] = sum_ref[slot]
            acc_ref[last] = acc_ref[slot]

        @pl.when(used & same_before)
        def _():
            old_max = max_ref[last]
            page_max = max_ref[slot]
            peak = jnp.maximum(old_max, page_max)
            old_factor = jnp.exp(old_max - peak)
            page_factor = jnp.exp(page_max - peak)
            max_ref[last] = peak
            sum_ref[last] = sum_ref[last] * old_factor + sum_ref[slot] * page_factor
            acc_ref[last] = acc_ref[last] * jnp.concatenate([old_factor, old_factor], axis=1) + acc_ref[
                slot
            ] * jnp.concatenate([page_factor, page_factor], axis=1)

        @pl.when(used & jnp.logical_not(same_after))
        def _():
            total = sum_ref[last]
            result = acc_ref[last] / jnp.concatenate([total, total], axis=1)
            for head in range(head_count):
                out_ref[source, :, head * head_dim : (head + 1) * head_dim] = result[
                    head * token_count : (head + 1) * token_count, :
                ].astype(BF16)
            whole = put_heads((max_ref[last] + jnp.log(total))[:, :1], token_count, 128)
            high = whole.astype(BF16).astype(F32)
            middle = (whole - high).astype(BF16).astype(F32)
            low = whole - high - middle
            lanes = lax.broadcasted_iota(jnp.int32, whole.shape, 1)
            packed = jnp.where(
                lanes < 16,
                high,
                jnp.where(lanes < 32, pltpu.roll(middle, 16, 1), pltpu.roll(low, 32, 1)),
            )
            out_ref[source, :, width:] = packed.astype(BF16)


def merge_new(holder_ref, got_ref, max_ref, sum_ref, acc_ref, attended_ref, spread_ref):
    token_count, width = attended_ref.shape
    holder = holder_ref[0]
    packed = got_ref[holder, :, width:].astype(F32)
    cached = packed + pltpu.roll(packed, 128 - 16, 1) + pltpu.roll(packed, 128 - 32, 1)
    new_max = max_ref[...]
    peak = jnp.maximum(cached, new_max)
    cached_factor = jnp.exp(cached - peak)
    new_factor = jnp.exp(new_max - peak)
    inverse = 1.0 / (cached_factor + new_factor * sum_ref[...])
    cached_factor = cached_factor * inverse
    new_factor = new_factor * inverse
    head_dim = 256
    for head in range(width // head_dim):
        span = slice(head * head_dim, (head + 1) * head_dim)
        rows = (
            got_ref[holder, :, span].astype(F32) * cached_factor[:, head : head + 1]
            + acc_ref[:, span] * new_factor[:, head : head + 1]
        ).astype(BF16)
        attended_ref[:, span] = rows
        for place in range(spread_ref.shape[0]):
            spread_ref[place, :, span] = rows


def project_out(rows_ref, weight_ref, residual_ref, out_ref):
    places, token_count, width = rows_ref.shape
    rows = jnp.concatenate([rows_ref[place].astype(F32) for place in range(places)], axis=0).astype(BF16)
    attention_out = lax.dot_general(rows, weight_ref[...], LAST, preferred_element_type=F32)
    stream = (residual_ref[...].astype(F32) + attention_out).astype(BF16)
    for place in range(places):
        out_ref[place] = stream


def feed_forward(
    core_ref,
    stream_ref,
    gain_ref,
    gate_far,
    up_far,
    down_far,
    keep_ref,
    send_ref,
    stream_half_ref,
    whole_ref,
    halves_ref,
    gate_ref,
    up_ref,
    down_ref,
    copied,
):
    parts, rows, width = stream_ref.shape
    total = parts * width
    half = total // 2
    chunks = copied.shape[0] // 3
    step = gate_ref.shape[0] // chunks
    copies = []
    for chunk in range(chunks):
        span = pl.ds(chunk * step, step)
        for far, near_ref in ((gate_far, gate_ref), (up_far, up_ref), (down_far, down_ref)):
            copies.append(pltpu.make_async_copy(far.at[span], near_ref.at[span], copied.at[len(copies)]))
            copies[-1].start()
    for part in range(parts):
        whole_ref[:, part * width : (part + 1) * width] = stream_ref[part].astype(F32)
    whole = whole_ref[...]
    square = jnp.sum(whole * whole, axis=1, keepdims=True)
    normed = (whole * lax.rsqrt(square / total + 1e-06) * gain_ref[...]).astype(BF16)
    core = core_ref[0]

    @pl.when(core == 0)
    def _():
        stream_half_ref[...] = whole_ref[:, :half]

    @pl.when(core == 1)
    def _():
        stream_half_ref[...] = whole_ref[:, half:]

    partial = jnp.zeros((rows, total), F32)
    for chunk in range(chunks):
        span = slice(chunk * step, (chunk + 1) * step)
        copies[3 * chunk].wait()
        gate = lax.dot_general(normed, gate_ref[span, :], LAST, preferred_element_type=F32)
        copies[3 * chunk + 1].wait()
        upward = lax.dot_general(normed, up_ref[span, :], LAST, preferred_element_type=F32)
        hidden = (jax.nn.gelu(gate, approximate=True) * upward).astype(BF16)
        copies[3 * chunk + 2].wait()
        partial = partial + jnp.dot(hidden, down_ref[span, :], preferred_element_type=F32)
    halves_ref[0] = partial[:, :half]
    halves_ref[1] = partial[:, half:]
    keep_ref[...] = halves_ref[core]
    send_ref[...] = halves_ref[1 - core].astype(BF16)


def add_pair(keep_ref, got_ref, send_ref):
    send_ref[...] = (keep_ref[...] + got_ref[...].astype(F32)).astype(BF16)


def add_chips(keep_ref, got_ref, first_ref, second_ref, third_ref, stream_ref, out_ref):
    total = keep_ref[...] + got_ref[...].astype(F32)
    total = total + first_ref[...].astype(F32) + second_ref[...].astype(F32) + third_ref[...].astype(F32)
    out_ref[...] = (stream_ref[...] + total).astype(BF16)


def project_next(place_ref, own_ref, other_ref, gain_ref, weight_ref, shard_ref, out_ref, whole_ref):
    rows, half = own_ref.shape
    core = place_ref[0] % 2

    @pl.when(core == 0)
    def _():
        whole_ref[:, :half] = own_ref[...].astype(F32)
        whole_ref[:, half:] = other_ref[...].astype(F32)

    @pl.when(core == 1)
    def _():
        whole_ref[:, half:] = own_ref[...].astype(F32)
        whole_ref[:, :half] = other_ref[...].astype(F32)

    part = shard_ref.shape[1]
    for place in range(2 * half // part):

        @pl.when(place_ref[0] == place)
        def _():
            shard_ref[...] = whole_ref[:, place * part : (place + 1) * part].astype(BF16)

    whole = whole_ref[...]
    square = jnp.sum(whole * whole, axis=1, keepdims=True)
    normed = (whole * lax.rsqrt(square / (2 * half) + 1e-06) * gain_ref[...]).astype(BF16)
    out_ref[...] = jnp.dot(normed, weight_ref[...], preferred_element_type=F32).astype(BF16)


SMEM = pl.BlockSpec(memory_space=pltpu.SMEM)
VMEM = pl.BlockSpec(memory_space=pltpu.VMEM)
FAR = pl.BlockSpec(memory_space=pl.ANY)


def near(array):
    return pltpu.with_memory_space_constraint(array, pltpu.VMEM)


def call(body, outs, scalars, arrays, far=(), scratch=(), copies=0):
    scratch_shapes = [pltpu.VMEM(shape, dtype) for shape, dtype in scratch]
    if copies:
        scratch_shapes.append(pltpu.SemaphoreType.DMA((copies,)))
    return pl.pallas_call(
        body,
        out_shape=[
            pltpu.VMEM(shape, dtype) if stays else jax.ShapeDtypeStruct(shape, dtype)
            for shape, dtype, stays in outs
        ],
        in_specs=[SMEM] * len(scalars) + [VMEM] * len(arrays) + [FAR] * len(far),
        out_specs=[VMEM] * len(outs),
        scratch_shapes=scratch_shapes,
        name=body.__name__,
    )(*scalars, *[near(array) for array in arrays], *far)


def exchange(copies, axis):
    return lax.all_to_all(copies, axis, split_axis=0, concat_axis=0, tiled=True)


def shards(
    queries,
    new_kv,
    kv_cache,
    lengths,
    page_table,
    residual,
    out_weight,
    norm_gain,
    gate_weight,
    up_weight,
    down_weight,
    next_gain,
    qkv_weight,
):
    seq_count = lax.axis_size("seq")
    mlp_count = lax.axis_size("mlp")
    seq_place = lax.axis_index("seq")
    mlp_place = lax.axis_index("mlp")
    device = seq_place * mlp_count + mlp_place
    slot_count, page_len, kv_width = kv_cache.shape
    head_dim = kv_width // 2
    token_count, width = queries.shape
    query_rows = token_count * (width // head_dim)
    page_count = page_table.shape[1]
    row_count, part_width = residual.shape
    half = width // 2

    (sent,) = call(send_queries, [((seq_count, query_rows, head_dim), BF16, True)], [], [queries])
    column_rows = exchange(sent, "seq")

    column_table = lax.dynamic_index_in_dim(
        page_table.reshape(seq_count, mlp_count, page_count), mlp_place, 1, keepdims=False
    )
    column_lengths = lax.dynamic_index_in_dim(
        lengths.reshape(seq_count, mlp_count), mlp_place, 1, keepdims=False
    )
    entry = (
        jnp.arange(seq_count, dtype=jnp.int32)[:, None] * page_count
        + jnp.arange(page_count, dtype=jnp.int32)[None, :]
        + 1
    )
    slots = device * slot_count + jnp.arange(slot_count, dtype=jnp.int32)
    codes = jnp.max(
        jnp.where(column_table[None] == slots[:, None, None], entry[None], 0), axis=(1, 2)
    )
    own_table = lax.dynamic_index_in_dim(column_table, seq_place, 0, keepdims=False)
    holder = (jnp.max(own_table) // (slot_count * mlp_count)).reshape(1)

    new_max, new_sum, new_acc = call(
        attend_new,
        [((token_count, 128), F32, True)] * 2 + [((token_count, width), F32, True)],
        [],
        [queries, new_kv],
    )
    (held,) = call(
        attend_pages,
        [((seq_count, token_count, width + 128), BF16, True)],
        [codes, column_lengths],
        [column_rows],
        [kv_cache],
        [
            ((slot_count + 1, query_rows, 128), F32),
            ((slot_count + 1, query_rows, 128), F32),
            ((slot_count + 1, query_rows, head_dim), F32),
            (kv_cache.shape, BF16),
        ],
        slot_count,
    )
    returned = exchange(held, "seq")
    attended, spread = call(
        merge_new,
        [((token_count, width), BF16, False), ((mlp_count, token_count, width), BF16, True)],
        [holder],
        [returned, new_max, new_sum, new_acc],
    )
    rows = exchange(spread, "mlp")
    (streams,) = call(
        project_out,
        [((mlp_count, row_count, part_width), BF16, True)],
        [],
        [rows, out_weight.T, residual],
    )
    streams = exchange(streams, "mlp")

    core = (mlp_place % 2).astype(jnp.int32).reshape(1)
    keep, send, stream_half = call(
        feed_forward,
        [((row_count, half), F32, True), ((row_count, half), BF16, True), ((row_count, half), F32, True)],
        [core],
        [streams, norm_gain.reshape(1, width)],
        [gate_weight.T, up_weight.T, down_weight],
        [
            ((row_count, width), F32),
            ((2, row_count, half), F32),
            (gate_weight.shape[::-1], BF16),
            (up_weight.shape[::-1], BF16),
            (down_weight.shape, BF16),
        ],
        9,
    )
    pair = [(i, i ^ 1) for i in range(mlp_count)]
    got = lax.ppermute(send, "mlp", pair)
    (chip_half,) = call(add_pair, [((row_count, half), BF16, True)], [], [keep, got])
    others = [
        lax.ppermute(chip_half, "mlp", [(i, (i + shift) % mlp_count) for i in range(mlp_count)])
        for shift in (2, 6, 4)
    ]
    (after_half,) = call(
        add_chips, [((row_count, half), BF16, True)], [], [keep, got, *others, stream_half]
    )
    other_half = lax.ppermute(after_half, "mlp", pair)
    shard_after, next_qkv = call(
        project_next,
        [((row_count, part_width), BF16, False), ((row_count, qkv_weight.shape[1]), BF16, False)],
        [mlp_place.astype(jnp.int32).reshape(1)],
        [after_half, other_half, next_gain.reshape(1, width), qkv_weight],
        scratch=[((row_count, width), F32)],
    )
    return (attended, shard_after, next_qkv)


def solution(mesh):
    return jax.shard_map(
        shards,
        mesh=mesh,
        in_specs=(
            P(("seq", "mlp"), None),
            P(("seq", "mlp"), None),
            P(("seq", "mlp"), None, None),
            P(),
            P(),
            P("seq", "mlp"),
            P(None, "mlp"),
            P(),
            P(None, "mlp"),
            P(None, "mlp"),
            P("mlp", None),
            P(),
            P(None, "mlp"),
        ),
        out_specs=(P(("seq", "mlp"), None), P("seq", "mlp"), P("seq", "mlp")),
        check_vma=False,
    )
```

time: 123 us -> 115 us (0.935)
  local copies, waits for them, and re-layouts: 17.2 us -> 5.26 us
  waiting for transfers between devices: 33.9 us -> 40.5 us
  Pallas kernels: 13.3 us -> 19.3 us
  other arithmetic: 6.2 us -> 1.72 us
  matrix products: 3.08 us -> 0 us
    unnamed x18 -> x16, local copies, waits for them, and re-layouts: 10.3 us -> 3.76 us
    pallas_call x2 -> x9, Pallas kernels: 13.3 us -> 19.3 us  [call(): pl.pallas_call(body, out_shape=[pltpu.VMEM(shape, dtype) if stays else ja...]
    all_to_all x3, waiting for transfers between devices: 29.9 us -> 33.9 us  [exchange(): return lax.all_to_all(copies, axis, split_axis=0, concat_axis=0, tiled=True)]
    dot_general x2 -> x0, matrix products: 3.08 us -> none  [the longest x1 2.01 us: shards(): jnp.dot(rows, out_weight, preferred_element_type=jnp.float32)]
    convert_element_type x3 -> x0, other arithmetic: 2.88 us -> none  [the longest x1 0.99 us: shards(): after_half = (stream_half.astype(jnp.float32) + total_half).astype(bf16)]
    ppermute x4, waiting for transfers between devices: 3.13 us -> 5.71 us  [the longest x3 4.79 us: shards(): lax.ppermute(chip_half, 'mlp', [(i, (i + shift) % mlp_count) for i in ran...]
    broadcast_in_dim x3 -> x0, local copies, waits for them, and re-layouts: 1.68 us -> none  [spread(): copies = jnp.broadcast_to(block[None], (lax.axis_size(axis),) + block.shape)]
    reshape x5 -> x2, local copies, waits for them, and re-layouts: 1.63 us -> 0.02 us  [the longest x1 0.01 us: shards(): norm_gain.reshape(1, width)]
  transfers between devices with their start and end apart: 8 -> 8, of which waited for: 5 -> 7; matrix products, arithmetic and copies ran while one was open for 12% -> 3% of each run, Pallas kernels for 0% -> 0%
where the time goes in v2:
time: 115 us
  waiting for transfers between devices  40.5 us (35%)
  starting transfers between devices  30.4 us (26%)
  Pallas kernels  19.3 us (17%)
  blocking collectives  14.9 us (13%)
  local copies, waits for them, and re-layouts  5.26 us (5%)
  between operations  2.73 us (2%)
  other arithmetic  1.72 us (1%)
    all_to_all x3, waiting for transfers between devices, exchange(): return lax.all_to_all(copies, axis, split_axis=0, concat_axis=0, tiled=True)  33.9 us
    all_to_all x3, starting transfers between devices, exchange(): return lax.all_to_all(copies, axis, split_axis=0, concat_axis=0, tiled=True)  24.4 us
    pallas_call x9, Pallas kernels, call(): pl.pallas_call(body, out_shape=[pltpu.VMEM(shape, dtype) if stays else ja...  19.3 us
    all_to_all x1, blocking collectives, exchange(): return lax.all_to_all(copies, axis, split_axis=0, concat_axis=0, tiled=True)  14.9 us
    ppermute x3, waiting for transfers between devices, shards(): lax.ppermute(chip_half, 'mlp', [(i, (i + shift) % mlp_count) for i in ran...  4.79 us
    unnamed x16, local copies, waits for them, and re-layouts  3.76 us
    ppermute x3, starting transfers between devices, shards(): lax.ppermute(chip_half, 'mlp', [(i, (i + shift) % mlp_count) for i in ran...  2.76 us
  transfers between devices with their start and end apart: 8, of which 7 were waited for; matrix products, arithmetic and copies ran while one was open for 3% of the time, Pallas kernels for 0%

profile of v2, /device:TPU:1, one launch (start us, length us, event | category | flops | bytes accessed | tf_op | source)
XLA Modules:
  0.0 114.7 jit_solution(122793407661576210)
XLA Ops:
  0.6 0.0 copy-start
  0.6 0.0 copy-start.3
  0.7 0.8 copy-done.3
  1.4 0.9 send_queries.1
  2.3 11.9 %all-to-all-start = ((bf16[32,40,256]{2,1,0:T(8,128)(2,1)}), bf16[32,40,256]{2,1,0:T(8,128)(2,1)S(1)}, u32[]{:S(2)}, u32[]{:S(2)}) async-start(bf16[32,40,256]{2,1,0:T(8,128)(2,1)} %send_queries.1), calls=%async_computation | async-start | bytes 1310720 | tf_op jit(solution)/shard_map/all_to_all | solution.py:309
  14.2 0.8 reshape.62
  14.9 0.7 dynamic-slice_reduce_fusion.length_ref
  15.7 0.0 copy-done
  15.7 0.1 add_add_fusion
  15.8 1.0 select_reduce_fusion.code_ref
  16.8 0.0 copy-start.5
  16.8 0.0 copy-start.4
  16.8 13.8 %all-to-all-done.rows_ref = bf16[32,40,256]{2,1,0:T(8,128)(2,1)S(1)} async-done(((bf16[32,40,256]{2,1,0:T(8,128)(2,1)}), bf16[32,40,256]{2,1,0:T(8,128)(2,1)S(1)}, u32[]{:S(2)}, u32[]{:S(2)}) %all-to-all-start) | async-done | bytes 655392 | tf_op jit(solution)/shard_map/all_to_all | solution.py:309
  30.6 9.5 %attend_pages.1 = bf16[32,4,2688]{2,1,0:T(4,128)(2,1)} custom-call(s32[17]{0:T(128)} %select_reduce_fusion.code_ref, s32[32]{0:T(128)} %dynamic-slice_reduce_fusion.length_ref, bf16[32,40,256]{2,1,0:T(8,128)(2,1)S(1)} %all-to-all-done.rows_ref, bf16[17,128,512]{2,1,0:T(8,128)(2,1)} %far_ref.1), custom_call_target="tpu_custom_call" | custom-call | tf_op jit(solution)/shard_map/attend_pages/pallas_call | solution.py:295
  40.1 0.0 copy-start.6
  40.1 8.4 %all-to-all-start.1 = ((bf16[32,4,2688]{2,1,0:T(4,128)(2,1)}), bf16[32,4,2688]{2,1,0:T(4,128)(2,1)S(1)}, u32[]{:S(2)}, u32[]{:S(2)}) async-start(bf16[32,4,2688]{2,1,0:T(4,128)(2,1)} %attend_pages.1), calls=%async_computation.1 | async-start | bytes 1376256 | tf_op jit(solution)/shard_map/all_to_all | solution.py:309
  48.5 0.6 fusion
  51.1 0.0 copy-done.5
  51.1 0.3 attend_new.1
  51.4 14.2 %all-to-all-done.1.got_ref = bf16[32,4,2688]{2,1,0:T(4,128)(2,1)S(1)} async-done(((bf16[32,4,2688]{2,1,0:T(4,128)(2,1)}), bf16[32,4,2688]{2,1,0:T(4,128)(2,1)S(1)}, u32[]{:S(2)}, u32[]{:S(2)}) %all-to-all-start.1) | async-done | bytes 688160 | tf_op jit(solution)/shard_map/all_to_all | solution.py:309
  65.6 0.8 merge_new.1
  66.4 14.9 %all_to_all.20.rows_ref = bf16[8,4,2560]{2,1,0:T(4,128)(2,1)S(1)} all-to-all(bf16[8,4,2560]{2,1,0:T(4,128)(2,1)S(1)} %get-tuple-element.17), channel_id=1, replica_groups=mesh['seq'=32,'mlp'=8] {'mlp'}, dimensions={0} | all-to-all | bytes 327680 | tf_op jit(solution)/shard_map/all_to_all | solution.py:309
  81.3 0.0 copy-done.4
  81.3 0.0 copy-start.2
  81.3 1.4 %copy-done.2 = bf16[2560,320]{0,1:T(8,128)(2,1)S(1)} copy-done((bf16[2560,320]{0,1:T(8,128)(2,1)S(1)}, bf16[2560,320]{0,1:T(8,128)(2,1)}, u32[]{:S(2)}) %copy-start.2) | copy-done | bytes 1638424
  82.8 1.3 %project_out.1 = bf16[8,32,320]{2,1,0:T(8,128)(2,1)} custom-call(bf16[8,4,2560]{2,1,0:T(4,128)(2,1)S(1)} %all_to_all.20.rows_ref, bf16[320,2560]{1,0:T(8,128)(2,1)S(1)} %bitcast.10, bf16[32,320]{1,0:T(8,128)(2,1)S(1)} %copy-done.4), custom_call_target="tpu_custom_call" | custom-call | tf_op jit(solution)/shard_map/project_out/pallas_call | solution.py:295
  84.0 4.2 %all-to-all-start.3 = ((bf16[8,32,320]{2,1,0:T(8,128)(2,1)}), bf16[8,32,320]{2,1,0:T(8,128)(2,1)S(1)}, u32[]{:S(2)}, u32[]{:S(2)}) async-start(bf16[8,32,320]{2,1,0:T(8,128)(2,1)} %project_out.1), calls=%async_computation.3 | async-start | bytes 393216 | tf_op jit(solution)/shard_map/all_to_all | solution.py:309
  88.2 0.0 copy-done.6
  88.3 5.9 %all-to-all-done.3.stream_ref = bf16[8,32,320]{2,1,0:T(8,128)(2,1)S(1)} async-done(((bf16[8,32,320]{2,1,0:T(8,128)(2,1)}), bf16[8,32,320]{2,1,0:T(8,128)(2,1)S(1)}, u32[]{:S(2)}, u32[]{:S(2)}) %all-to-all-start.3) | async-done | bytes 163872 | tf_op jit(solution)/shard_map/all_to_all | solution.py:309
  94.1 0.0 copy-start.7
  94.1 5.1 %feed_forward.1 = (f32[32,1280]{1,0:T(8,128)S(1)}, bf16[32,1280]{1,0:T(8,128)(2,1)S(1)}, f32[32,1280]{1,0:T(8,128)S(1)}) custom-call(s32[1]{0:T(128)} %bitcast.4.core_ref, bf16[8,32,320]{2,1,0:T(8,128)(2,1)S(1)} %all-to-all-done.3.stream_ref, f32[1,2560]{1,0:T(1,128)S(1)} %reshape.65.gain_ref, bf16[480,2560]{1,0:T(8,128)(2,1)} %bitcast.11, ...), custom_call_target="tpu_custom_call" | custom-call | tf_op jit(solution)/shard_map/feed_forward/pallas_call | solution.py:295
  99.3 1.0 collective-permute-start
  100.3 0.9 collective-permute-done.got_ref
  101.2 0.4 collective-permute-start.1
  101.6 2.4 %collective-permute-start.2 = (bf16[32,1280]{1,0:T(8,128)(2,1)S(1)}, bf16[32,1280]{1,0:T(8,128)(2,1)S(1)}, u32[]{:S(2)}, u32[]{:S(2)}) collective-permute-start(bf16[32,1280]{1,0:T(8,128)(2,1)S(1)} %add_pair.1), channel_id=1, source_target_pairs={{0,6},{1,7},{2,0},{3,1},{4,2},{5,3},{6,4},{7,5},{8,14},{9,15},{10,... | collective-permute-start | bytes 245768 | tf_op jit(solution)/shard_map/ppermute | solution.py:417
  104.0 0.0 collective-permute-start.3
  104.0 2.2 %collective-permute-done.1.first_ref = bf16[32,1280]{1,0:T(8,128)(2,1)S(1)} collective-permute-done((bf16[32,1280]{1,0:T(8,128)(2,1)S(1)}, bf16[32,1280]{1,0:T(8,128)(2,1)S(1)}, u32[]{:S(2)}, u32[]{:S(2)}) %collective-permute-start.1) | collective-permute-done | bytes 81952 | tf_op jit(solution)/shard_map/ppermute | solution.py:417
  106.2 0.0 collective-permute-done.2.second_ref
  106.2 2.6 %collective-permute-done.3.third_ref = bf16[32,1280]{1,0:T(8,128)(2,1)S(1)} collective-permute-done((bf16[32,1280]{1,0:T(8,128)(2,1)S(1)}, bf16[32,1280]{1,0:T(8,128)(2,1)S(1)}, u32[]{:S(2)}, u32[]{:S(2)}) %collective-permute-start.3) | collective-permute-done | bytes 81952 | tf_op jit(solution)/shard_map/ppermute | solution.py:417
  108.8 0.1 add_chips.1.own_ref
  108.9 2.2 %collective-permute-start.4 = (bf16[32,1280]{1,0:T(8,128)(2,1)S(1)}, bf16[32,1280]{1,0:T(8,128)(2,1)S(1)}, u32[]{:S(2)}, u32[]{:S(2)}) collective-permute-start(bf16[32,1280]{1,0:T(8,128)(2,1)S(1)} %add_chips.1.own_ref), channel_id=1, source_target_pairs={{0,1},{1,0},{2,3},{3,2},{4,5},{5,4},{6,7},{7,6},{8,9},{9,8},{10,11... | collective-permute-start | bytes 245768 | tf_op jit(solution)/shard_map/ppermute | solution.py:423
  111.0 0.0 copy-done.7
  111.0 0.9 collective-permute-done.4.other_ref
  111.9 0.0 copy-start.1
  111.9 1.5 %copy-done.1 = bf16[2560,384]{1,0:T(8,128)(2,1)S(1)} copy-done((bf16[2560,384]{1,0:T(8,128)(2,1)S(1)}, bf16[2560,384]{1,0:T(8,128)(2,1)}, u32[]{:S(2)}) %copy-start.1) | copy-done | bytes 1966104
  113.5 1.2 %project_next.1 = (bf16[32,320]{1,0:T(8,128)(2,1)}, bf16[32,384]{1,0:T(8,128)(2,1)}) custom-call(s32[1]{0:T(128)} %bitcast.3.place_ref, bf16[32,1280]{1,0:T(8,128)(2,1)S(1)} %add_chips.1.own_ref, bf16[32,1280]{1,0:T(8,128)(2,1)S(1)} %collective-permute-done.4.other_ref, f32[1,2560]{1,0:T(1,128)S(1)} %reshape.66.gain_ref, bf16[2560,384]{1,0:T(8,128)(2,1)S(1)} %copy-done.1), custom_call_target="tpu_custom_call" | custom-call | tf_op jit(solution)/shard_map/project_next/pallas_call | solution.py:295
  (6 shorter events, 0.1 us)
Async XLA Ops:
  0.6 15.0 %copy-start = (s32[256,128]{1,0:T(8,128)S(1)}, s32[256,128]{1,0:T(8,128)}, u32[]{:S(2)}) copy-start(s32[256,128]{1,0:T(8,128)} %param.17) | copy-start | bytes 393220
  0.6 0.8 copy-start.3
  2.3 28.3 %all-to-all-start = ((bf16[32,40,256]{2,1,0:T(8,128)(2,1)}), bf16[32,40,256]{2,1,0:T(8,128)(2,1)S(1)}, u32[]{:S(2)}, u32[]{:S(2)}) async-start(bf16[32,40,256]{2,1,0:T(8,128)(2,1)} %send_queries.1), calls=%async_computation | async-start | bytes 1310720 | tf_op jit(solution)/shard_map/all_to_all | solution.py:309
  16.8 34.3 %copy-start.5 = (bf16[4,512]{1,0:T(4,128)(2,1)S(1)}, bf16[4,512]{1,0:T(4,128)(2,1)}, u32[]{:S(2)}) copy-start(bf16[4,512]{1,0:T(4,128)(2,1)} %new_ref.1) | copy-start | bytes 12292
  16.8 64.6 %copy-start.4 = (bf16[32,320]{1,0:T(8,128)(2,1)S(1)}, bf16[32,320]{1,0:T(8,128)(2,1)}, u32[]{:S(2)}) copy-start(bf16[32,320]{1,0:T(8,128)(2,1)} %residual_ref.1) | copy-start | bytes 61444
  40.1 48.1 %copy-start.6 = (f32[2560]{0:T(1024)S(1)}, f32[2560]{0:T(1024)}, u32[]{:S(2)}) copy-start(f32[2560]{0:T(1024)} %param.20) | copy-start | bytes 30724
  40.1 25.5 %all-to-all-start.1 = ((bf16[32,4,2688]{2,1,0:T(4,128)(2,1)}), bf16[32,4,2688]{2,1,0:T(4,128)(2,1)S(1)}, u32[]{:S(2)}, u32[]{:S(2)}) async-start(bf16[32,4,2688]{2,1,0:T(4,128)(2,1)} %attend_pages.1), calls=%async_computation.1 | async-start | bytes 1376256 | tf_op jit(solution)/shard_map/all_to_all | solution.py:309
  81.3 1.4 %copy-start.2 = (bf16[2560,320]{0,1:T(8,128)(2,1)S(1)}, bf16[2560,320]{0,1:T(8,128)(2,1)}, u32[]{:S(2)}) copy-start(bf16[2560,320]{0,1:T(8,128)(2,1)} %param.19) | copy-start | bytes 4915204
  84.0 10.1 %all-to-all-start.3 = ((bf16[8,32,320]{2,1,0:T(8,128)(2,1)}), bf16[8,32,320]{2,1,0:T(8,128)(2,1)S(1)}, u32[]{:S(2)}, u32[]{:S(2)}) async-start(bf16[8,32,320]{2,1,0:T(8,128)(2,1)} %project_out.1), calls=%async_computation.3 | async-start | bytes 393216 | tf_op jit(solution)/shard_map/all_to_all | solution.py:309
  94.1 16.9 %copy-start.7 = (f32[2560]{0:T(1024)S(1)}, f32[2560]{0:T(1024)}, u32[]{:S(2)}) copy-start(f32[2560]{0:T(1024)} %param.24) | copy-start | bytes 30724
  99.3 2.0 %collective-permute-start = (bf16[32,1280]{1,0:T(8,128)(2,1)S(1)}, bf16[32,1280]{1,0:T(8,128)(2,1)S(1)}, u32[]{:S(2)}, u32[]{:S(2)}) collective-permute-start(bf16[32,1280]{1,0:T(8,128)(2,1)S(1)} %get-tuple-element.19), channel_id=1, source_target_pairs={{0,1},{1,0},{2,3},{3,2},{4,5},{5,4},{6,7},{7,6},{8,9},{9,8},{10,11... | collective-permute-start | bytes 245768 | tf_op jit(solution)/shard_map/ppermute | solution.py:414
  101.2 5.0 %collective-permute-start.1 = (bf16[32,1280]{1,0:T(8,128)(2,1)S(1)}, bf16[32,1280]{1,0:T(8,128)(2,1)S(1)}, u32[]{:S(2)}, u32[]{:S(2)}) collective-permute-start(bf16[32,1280]{1,0:T(8,128)(2,1)S(1)} %add_pair.1), channel_id=1, source_target_pairs={{0,2},{1,3},{2,4},{3,5},{4,6},{5,7},{6,0},{7,1},{8,10},{9,11},{10,... | collective-permute-start | bytes 245768 | tf_op jit(solution)/shard_map/ppermute | solution.py:417
  101.6 4.6 %collective-permute-start.2 = (bf16[32,1280]{1,0:T(8,128)(2,1)S(1)}, bf16[32,1280]{1,0:T(8,128)(2,1)S(1)}, u32[]{:S(2)}, u32[]{:S(2)}) collective-permute-start(bf16[32,1280]{1,0:T(8,128)(2,1)S(1)} %add_pair.1), channel_id=1, source_target_pairs={{0,6},{1,7},{2,0},{3,1},{4,2},{5,3},{6,4},{7,5},{8,14},{9,15},{10,... | collective-permute-start | bytes 245768 | tf_op jit(solution)/shard_map/ppermute | solution.py:417
  104.0 4.8 %collective-permute-start.3 = (bf16[32,1280]{1,0:T(8,128)(2,1)S(1)}, bf16[32,1280]{1,0:T(8,128)(2,1)S(1)}, u32[]{:S(2)}, u32[]{:S(2)}) collective-permute-start(bf16[32,1280]{1,0:T(8,128)(2,1)S(1)} %add_pair.1), channel_id=1, source_target_pairs={{0,4},{1,5},{2,6},{3,7},{4,0},{5,1},{6,2},{7,3},{8,12},{9,13},{10,... | collective-permute-start | bytes 245768 | tf_op jit(solution)/shard_map/ppermute | solution.py:417
  108.9 3.1 %collective-permute-start.4 = (bf16[32,1280]{1,0:T(8,128)(2,1)S(1)}, bf16[32,1280]{1,0:T(8,128)(2,1)S(1)}, u32[]{:S(2)}, u32[]{:S(2)}) collective-permute-start(bf16[32,1280]{1,0:T(8,128)(2,1)S(1)} %add_chips.1.own_ref), channel_id=1, source_target_pairs={{0,1},{1,0},{2,3},{3,2},{4,5},{5,4},{6,7},{7,6},{8,9},{9,8},{10,11... | collective-permute-start | bytes 245768 | tf_op jit(solution)/shard_map/ppermute | solution.py:423
  111.9 1.5 %copy-start.1 = (bf16[2560,384]{1,0:T(8,128)(2,1)S(1)}, bf16[2560,384]{1,0:T(8,128)(2,1)}, u32[]{:S(2)}) copy-start(bf16[2560,384]{1,0:T(8,128)(2,1)} %weight_ref.1) | copy-start | bytes 5898244

commit v3 on v2

v3 whole, which is shorter than its diff:
```python
import functools

import jax
import jax.numpy as jnp
from jax import lax
from jax.experimental import pallas as pl
from jax.experimental.pallas import tpu as pltpu
from jax.sharding import PartitionSpec as P

WINDOW = 2048
NEG_FILL = -1e30
LAST = (((1,), (1,)), ((), ()))
F32 = jnp.float32
BF16 = jnp.bfloat16


def head_major(values, head_dim):
    width = values.shape[1]
    return jnp.concatenate(
        [values[:, start : start + head_dim] for start in range(0, width, head_dim)], axis=0
    )


def put_heads(column, token_count, lanes):
    lane = lax.broadcasted_iota(jnp.int32, (token_count, lanes), 1)
    placed = jnp.zeros((token_count, lanes), F32)
    for head in range(column.shape[0] // token_count):
        part = column[head * token_count : (head + 1) * token_count, :]
        placed = jnp.where(lane == head, part, placed)
    return placed


def send_queries(far_ref, *refs, splits):
    outs, queries_ref, copied = refs[:-2], refs[-2], refs[-1]
    copy = pltpu.make_async_copy(far_ref, queries_ref, copied.at[0])
    copy.start()
    copy.wait()
    for (start, stop), out_ref in zip(splits, outs):
        head_dim = out_ref.shape[2]
        values = queries_ref[:, start * head_dim : stop * head_dim].astype(F32)
        rows = head_major(values, head_dim).astype(BF16)
        for place in range(out_ref.shape[0]):
            out_ref[place] = rows


def attend_new(queries_ref, new_ref, max_ref, sum_ref, acc_ref):
    token_count, width = queries_ref.shape
    head_dim = new_ref.shape[1] // 2
    query = head_major(queries_ref[...].astype(F32), head_dim).astype(BF16)
    scores = lax.dot_general(
        query, new_ref[:, :head_dim], LAST, preferred_element_type=F32
    ) * head_dim ** (-0.5)
    token = lax.broadcasted_iota(jnp.int32, scores.shape, 0) % token_count
    column = lax.broadcasted_iota(jnp.int32, scores.shape, 1)
    valid = column <= token
    peak = jnp.max(jnp.where(valid, scores, NEG_FILL), axis=1, keepdims=True)
    weights = jnp.where(valid, jnp.exp(scores - peak), 0.0)
    rounded = weights.astype(BF16).astype(F32)
    values = new_ref[:, head_dim:].astype(F32)
    acc = jnp.zeros((query.shape[0], head_dim), F32)
    for new in range(token_count):
        acc = acc + rounded[:, new : new + 1] * values[new : new + 1, :]
    max_ref[...] = put_heads(peak, token_count, max_ref.shape[1])
    sum_ref[...] = put_heads(jnp.sum(weights, axis=1, keepdims=True), token_count, sum_ref.shape[1])
    for head in range(width // head_dim):
        acc_ref[:, head * head_dim : (head + 1) * head_dim] = acc[
            head * token_count : (head + 1) * token_count, :
        ]


def attend_pages(
    code_ref, length_ref, rows_ref, front_ref, far_ref, out_ref, score_ref, peak_ref, rest_ref, copied
):
    slot_count, page_len, kv_width = far_ref.shape
    near_count = front_ref.shape[0]
    rest = pltpu.make_async_copy(
        far_ref.at[pl.ds(near_count, slot_count - near_count)], rest_ref, copied.at[0]
    )
    rest.start()

    def cached(slot, span):
        if slot < near_count:
            return front_ref[slot, :, span]
        return rest_ref[slot - near_count, :, span]

    head_dim = kv_width // 2
    token_count = out_ref.shape[1]
    width = out_ref.shape[2] - 128
    query_rows = rows_ref.shape[1]
    head_count = width // head_dim
    page_count = 128
    scale = head_dim ** (-0.5)
    token = lax.broadcasted_iota(jnp.int32, (query_rows, page_len), 0) % token_count
    lane = lax.broadcasted_iota(jnp.int32, (query_rows, page_len), 1)
    low_edge = lane - token + (WINDOW - 1)
    codes = [code_ref[slot] for slot in range(slot_count)]
    sources = [jnp.maximum(code - 1, 0) // page_count for code in codes]
    first = [True] + [
        (codes[slot] == 0) | (codes[slot - 1] == 0) | (sources[slot] != sources[slot - 1])
        for slot in range(1, slot_count)
    ]
    last = first[1:] + [True]
    fill = jnp.full((query_rows, page_len), NEG_FILL, F32)
    peak = fill
    for slot in range(slot_count):
        if slot == near_count:
            rest.wait()
        page = jnp.maximum(codes[slot] - 1, 0) % page_count
        reach = jnp.where(codes[slot] > 0, length_ref[sources[slot]], 0) - page * page_len
        scores = (
            lax.dot_general(
                rows_ref[sources[slot]], cached(slot, slice(0, head_dim)), LAST, preferred_element_type=F32
            )
            * scale
        )
        scores = jnp.where((lane < reach) & (low_edge >= reach), scores, NEG_FILL)
        score_ref[slot] = scores
        peak = jnp.maximum(scores, jnp.where(first[slot], NEG_FILL, peak) if slot else fill)
        peak_ref[slot] = jnp.broadcast_to(jnp.max(peak, axis=1, keepdims=True), (query_rows, page_len))
    for slot in range(slot_count - 2, -1, -1):
        peak_ref[slot] = jnp.where(last[slot], peak_ref[slot], peak_ref[slot + 1])
    total = jnp.zeros((query_rows, page_len), F32)
    acc = jnp.zeros((query_rows, head_dim), F32)
    for slot in range(slot_count):
        weights = jnp.exp(score_ref[slot] - peak_ref[slot])
        value = jnp.dot(weights.astype(BF16), cached(slot, slice(head_dim, kv_width)), preferred_element_type=F32)
        total = weights + (jnp.where(first[slot], 0.0, total) if slot else 0.0)
        acc = value + (jnp.where(first[slot], 0.0, acc) if slot else 0.0)
        finished_total, finished_acc = total, acc

        @pl.when((codes[slot] > 0) & last[slot])
        def _():
            whole_sum = jnp.sum(finished_total, axis=1, keepdims=True)
            result = finished_acc / whole_sum
            for head in range(head_count):
                out_ref[sources[slot], :, head * head_dim : (head + 1) * head_dim] = result[
                    head * token_count : (head + 1) * token_count, :
                ].astype(BF16)
            whole = put_heads(peak_ref[slot][:, :1] + jnp.log(whole_sum), token_count, 128)
            high = whole.astype(BF16).astype(F32)
            middle = (whole - high).astype(BF16).astype(F32)
            low = whole - high - middle
            lanes = lax.broadcasted_iota(jnp.int32, whole.shape, 1)
            packed = jnp.where(
                lanes < 16,
                high,
                jnp.where(lanes < 32, pltpu.roll(middle, 16, 1), pltpu.roll(low, 32, 1)),
            )
            out_ref[sources[slot], :, width:] = packed.astype(BF16)


def merge_new(holder_ref, *refs, splits):
    got_refs = refs[: len(splits)]
    max_ref, sum_ref, acc_ref, attended_ref, spread_ref = refs[len(splits) :]
    holder = holder_ref[0]
    head_dim = 256
    for (first_head, last_head), got_ref in zip(splits, got_refs):
        width = got_ref.shape[2] - 128
        packed = got_ref[holder, :, width:].astype(F32)
        cached = packed + pltpu.roll(packed, 128 - 16, 1) + pltpu.roll(packed, 128 - 32, 1)
        new_max = max_ref[...]
        new_sum = sum_ref[...]
        if first_head:
            new_max = pltpu.roll(new_max, 128 - first_head, 1)
            new_sum = pltpu.roll(new_sum, 128 - first_head, 1)
        peak = jnp.maximum(cached, new_max)
        cached_factor = jnp.exp(cached - peak)
        new_factor = jnp.exp(new_max - peak)
        inverse = 1.0 / (cached_factor + new_factor * new_sum)
        cached_factor = cached_factor * inverse
        new_factor = new_factor * inverse
        for head in range(last_head - first_head):
            whole = slice((first_head + head) * head_dim, (first_head + head + 1) * head_dim)
            rows = (
                got_ref[holder, :, head * head_dim : (head + 1) * head_dim].astype(F32)
                * cached_factor[:, head : head + 1]
                + acc_ref[:, whole] * new_factor[:, head : head + 1]
            ).astype(BF16)
            attended_ref[:, whole] = rows
            for place in range(spread_ref.shape[0]):
                spread_ref[place, :, whole] = rows


def project_out(rows_ref, weight_ref, residual_ref, out_ref):
    places, token_count, width = rows_ref.shape
    rows = jnp.concatenate([rows_ref[place].astype(F32) for place in range(places)], axis=0).astype(BF16)
    attention_out = lax.dot_general(rows, weight_ref[...], LAST, preferred_element_type=F32)
    stream = (residual_ref[...].astype(F32) + attention_out).astype(BF16)
    for place in range(places):
        out_ref[place] = stream


def feed_forward(
    core_ref,
    stream_ref,
    gain_ref,
    gate_ref,
    up_ref,
    down_ref,
    gate_far,
    up_far,
    down_far,
    keep_ref,
    send_ref,
    stream_half_ref,
    whole_ref,
    halves_ref,
    gate_rest,
    up_rest,
    down_rest,
    copied,
):
    parts, rows, width = stream_ref.shape
    total = parts * width
    half = total // 2
    near_rows = gate_ref.shape[0]
    chunks = 2
    step = gate_rest.shape[0] // chunks
    copies = []
    for chunk in range(chunks):
        for far, rest in ((gate_far, gate_rest), (up_far, up_rest), (down_far, down_rest)):
            copies.append(
                pltpu.make_async_copy(
                    far.at[pl.ds(near_rows + chunk * step, step)],
                    rest.at[pl.ds(chunk * step, step)],
                    copied.at[len(copies)],
                )
            )
            copies[-1].start()
    for part in range(parts):
        whole_ref[:, part * width : (part + 1) * width] = stream_ref[part].astype(F32)
    whole = whole_ref[...]
    square = jnp.sum(whole * whole, axis=1, keepdims=True)
    normed = (whole * lax.rsqrt(square / total + 1e-06) * gain_ref[...]).astype(BF16)
    core = core_ref[0]

    @pl.when(core == 0)
    def _():
        stream_half_ref[...] = whole_ref[:, :half]

    @pl.when(core == 1)
    def _():
        stream_half_ref[...] = whole_ref[:, half:]

    def through(gate_rows, up_rows, down_rows):
        gate = lax.dot_general(normed, gate_rows, LAST, preferred_element_type=F32)
        upward = lax.dot_general(normed, up_rows, LAST, preferred_element_type=F32)
        hidden = (jax.nn.gelu(gate, approximate=True) * upward).astype(BF16)
        return jnp.dot(hidden, down_rows, preferred_element_type=F32)

    partial = through(gate_ref[...], up_ref[...], down_ref[...])
    for chunk in range(chunks):
        for copy in copies[3 * chunk : 3 * chunk + 3]:
            copy.wait()
        span = slice(chunk * step, (chunk + 1) * step)
        partial = partial + through(gate_rest[span, :], up_rest[span, :], down_rest[span, :])
    halves_ref[0] = partial[:, :half]
    halves_ref[1] = partial[:, half:]
    keep_ref[...] = halves_ref[core]
    send_ref[...] = halves_ref[1 - core].astype(BF16)


def add_pair(keep_ref, got_ref, send_ref):
    send_ref[...] = (keep_ref[...] + got_ref[...].astype(F32)).astype(BF16)


def add_chips(keep_ref, got_ref, first_ref, second_ref, third_ref, stream_ref, fetched_ref, out_ref):
    total = keep_ref[...] + got_ref[...].astype(F32)
    total = total + first_ref[...].astype(F32) + second_ref[...].astype(F32) + third_ref[...].astype(F32)
    out_ref[...] = (stream_ref[...] + total).astype(BF16)


def project_next(
    place_ref,
    own_ref,
    other_ref,
    gain_ref,
    front_ref,
    weight_far,
    shard_ref,
    out_ref,
    whole_ref,
    rest_ref,
    copied,
):
    rows, half = own_ref.shape
    near_rows = front_ref.shape[0]
    rest = pltpu.make_async_copy(
        weight_far.at[pl.ds(near_rows, rest_ref.shape[0])], rest_ref, copied.at[0]
    )
    rest.start()
    core = place_ref[0] % 2

    @pl.when(core == 0)
    def _():
        whole_ref[:, :half] = own_ref[...].astype(F32)
        whole_ref[:, half:] = other_ref[...].astype(F32)

    @pl.when(core == 1)
    def _():
        whole_ref[:, half:] = own_ref[...].astype(F32)
        whole_ref[:, :half] = other_ref[...].astype(F32)

    part = shard_ref.shape[1]
    for place in range(2 * half // part):

        @pl.when(place_ref[0] == place)
        def _():
            shard_ref[...] = whole_ref[:, place * part : (place + 1) * part].astype(BF16)

    whole = whole_ref[...]
    square = jnp.sum(whole * whole, axis=1, keepdims=True)
    normed = (whole * lax.rsqrt(square / (2 * half) + 1e-06) * gain_ref[...]).astype(BF16)
    front = jnp.dot(normed[:, :near_rows], front_ref[...], preferred_element_type=F32)
    rest.wait()
    back = jnp.dot(normed[:, near_rows:], rest_ref[...], preferred_element_type=F32)
    out_ref[...] = (front + back).astype(BF16)


SMEM = pl.BlockSpec(memory_space=pltpu.SMEM)
VMEM = pl.BlockSpec(memory_space=pltpu.VMEM)
FAR = pl.BlockSpec(memory_space=pl.ANY)


def near(array):
    return pltpu.with_memory_space_constraint(array, pltpu.VMEM)


def call(body, outs, scalars, arrays, far=(), scratch=(), copies=0):
    scratch_shapes = [pltpu.VMEM(shape, dtype) for shape, dtype in scratch]
    if copies:
        scratch_shapes.append(pltpu.SemaphoreType.DMA((copies,)))
    return pl.pallas_call(
        body,
        out_shape=[
            pltpu.VMEM(shape, dtype) if stays else jax.ShapeDtypeStruct(shape, dtype)
            for shape, dtype, stays in outs
        ],
        in_specs=[SMEM] * len(scalars) + [VMEM] * len(arrays) + [FAR] * len(far),
        out_specs=[VMEM] * len(outs),
        scratch_shapes=scratch_shapes,
        name=getattr(body, "func", body).__name__,
    )(*scalars, *[near(array) for array in arrays], *far)


def fetch(parts, after):
    def fetch_rows(*refs):
        fars, outs, copied = refs[1 : 1 + len(parts)], refs[1 + len(parts) : 1 + 2 * len(parts)], refs[-1]
        copies = [
            pltpu.make_async_copy(far.at[pl.ds(0, out.shape[0])], out, copied.at[index])
            for index, (far, out) in enumerate(zip(fars, outs))
        ]
        for copy in copies:
            copy.start()
        for copy in copies:
            copy.wait()

    return pl.pallas_call(
        fetch_rows,
        out_shape=[pltpu.VMEM((rows,) + far.shape[1:], far.dtype) for far, rows in parts]
        + [pltpu.VMEM((8, 128), F32)],
        in_specs=[FAR] * (len(parts) + 1),
        out_specs=[VMEM] * (len(parts) + 1),
        scratch_shapes=[pltpu.SemaphoreType.DMA((len(parts),))],
        name="fetch_rows",
    )(after, *[far for far, _ in parts])


def exchange(copies, axis):
    return lax.all_to_all(copies, axis, split_axis=0, concat_axis=0, tiled=True)


def shards(
    queries,
    new_kv,
    kv_cache,
    lengths,
    page_table,
    residual,
    out_weight,
    norm_gain,
    gate_weight,
    up_weight,
    down_weight,
    next_gain,
    qkv_weight,
):
    seq_count = lax.axis_size("seq")
    mlp_count = lax.axis_size("mlp")
    seq_place = lax.axis_index("seq")
    mlp_place = lax.axis_index("mlp")
    device = seq_place * mlp_count + mlp_place
    slot_count, page_len, kv_width = kv_cache.shape
    head_dim = kv_width // 2
    token_count, width = queries.shape
    page_count = page_table.shape[1]
    row_count, part_width = residual.shape
    half = width // 2

    splits = ((0, width // head_dim),)
    sizes = [token_count * (stop - start) for start, stop in splits]
    sents = call(
        functools.partial(send_queries, splits=splits),
        [((seq_count, size, head_dim), BF16, True) for size in sizes],
        [],
        [],
        [queries],
        [(queries.shape, BF16)],
        1,
    )
    column_rows = [exchange(sent, "seq") for sent in sents]

    column_table = lax.dynamic_index_in_dim(
        page_table.reshape(seq_count, mlp_count, page_count), mlp_place, 1, keepdims=False
    )
    column_lengths = lax.dynamic_index_in_dim(
        lengths.reshape(seq_count, mlp_count), mlp_place, 1, keepdims=False
    )
    entry = (
        jnp.arange(seq_count, dtype=jnp.int32)[:, None] * page_count
        + jnp.arange(page_count, dtype=jnp.int32)[None, :]
        + 1
    )
    slots = device * slot_count + jnp.arange(slot_count, dtype=jnp.int32)
    codes = jnp.max(
        jnp.where(column_table[None] == slots[:, None, None], entry[None], 0), axis=(1, 2)
    )
    own_table = lax.dynamic_index_in_dim(column_table, seq_place, 0, keepdims=False)
    holder = (jnp.max(own_table) // (slot_count * mlp_count)).reshape(1)

    new_max, new_sum, new_acc = call(
        attend_new,
        [((token_count, 128), F32, True)] * 2 + [((token_count, width), F32, True)],
        [],
        [queries, new_kv],
    )
    cache_front, _ = fetch([(kv_cache, 8)], sents[-1])
    returned = []
    for arrived in column_rows:
        (held,) = call(
            attend_pages,
            [((seq_count, token_count, arrived.shape[1] // token_count * head_dim + 128), BF16, True)],
            [codes, column_lengths],
            [arrived, cache_front],
            [kv_cache],
            [((slot_count, arrived.shape[1], page_len), F32)] * 2
            + [((slot_count - 8, page_len, kv_width), BF16)],
            1,
        )
        returned.append(exchange(held, "seq"))
    attended, spread = call(
        functools.partial(merge_new, splits=splits),
        [((token_count, width), BF16, False), ((mlp_count, token_count, width), BF16, True)],
        [holder],
        [*returned, new_max, new_sum, new_acc],
    )
    rows = exchange(spread, "mlp")
    (streams,) = call(
        project_out,
        [((mlp_count, row_count, part_width), BF16, True)],
        [],
        [rows, *fetch([(out_weight.T, part_width)], held)[:-1], residual],
    )
    layers = [(gate_weight.T, 128), (up_weight.T, 128), (down_weight, 128)]
    *front, _ = fetch(layers, streams)
    streams = exchange(streams, "mlp")

    core = (mlp_place % 2).astype(jnp.int32).reshape(1)
    keep, send, stream_half = call(
        feed_forward,
        [((row_count, half), F32, True), ((row_count, half), BF16, True), ((row_count, half), F32, True)],
        [core],
        [streams, norm_gain.reshape(1, width), *front],
        [far for far, _ in layers],
        [((row_count, width), F32), ((2, row_count, half), F32)]
        + [((far.shape[0] - rows, width), BF16) for far, rows in layers],
        6,
    )
    pair = [(i, i ^ 1) for i in range(mlp_count)]
    got = lax.ppermute(send, "mlp", pair)
    (chip_half,) = call(add_pair, [((row_count, half), BF16, True)], [], [keep, got])
    others = [
        lax.ppermute(chip_half, "mlp", [(i, (i + shift) % mlp_count) for i in range(mlp_count)])
        for shift in (2, 6, 4)
    ]
    near_rows = 1664
    qkv_front, fetched = fetch([(qkv_weight, near_rows)], chip_half)
    (after_half,) = call(
        add_chips, [((row_count, half), BF16, True)], [], [keep, got, *others, stream_half], [fetched]
    )
    other_half = lax.ppermute(after_half, "mlp", pair)
    shard_after, next_qkv = call(
        project_next,
        [((row_count, part_width), BF16, False), ((row_count, qkv_weight.shape[1]), BF16, False)],
        [mlp_place.astype(jnp.int32).reshape(1)],
        [after_half, other_half, next_gain.reshape(1, width), qkv_front],
        [qkv_weight],
        [((row_count, width), F32), ((width - near_rows, qkv_weight.shape[1]), BF16)],
        1,
    )
    return (attended, shard_after, next_qkv)


def solution(mesh):
    return jax.shard_map(
        shards,
        mesh=mesh,
        in_specs=(
            P(("seq", "mlp"), None),
            P(("seq", "mlp"), None),
            P(("seq", "mlp"), None, None),
            P(),
            P(),
            P("seq", "mlp"),
            P(None, "mlp"),
            P(),
            P(None, "mlp"),
            P(None, "mlp"),
            P("mlp", None),
            P(),
            P(None, "mlp"),
        ),
        out_specs=(P(("seq", "mlp"), None), P("seq", "mlp"), P("seq", "mlp")),
        check_vma=False,
    )
```

time: 115 us -> 110 us (0.957)
  blocking collectives: 14.9 us -> 0 us
  starting transfers between devices: 30.4 us -> 39.8 us
  Pallas kernels: 19.3 us -> 23.5 us
  waiting for transfers between devices: 40.5 us -> 37.3 us
    all_to_all x1 -> x0, blocking collectives: 14.9 us -> none  [exchange(): return lax.all_to_all(copies, axis, split_axis=0, concat_axis=0, tiled=True)]
    all_to_all x3 -> x4, starting transfers between devices: 24.4 us -> 33.9 us  [exchange(): return lax.all_to_all(copies, axis, split_axis=0, concat_axis=0, tiled=True)]
    pallas_call x0 -> x4, Pallas kernels: none -> 7.29 us  [fetch(): pl.pallas_call(fetch_rows, out_shape=[pltpu.VMEM((rows,) + far.shape[1:],...]
    pallas_call x9, Pallas kernels: 19.3 us -> 16.3 us  [call(): pl.pallas_call(body, out_shape=[pltpu.VMEM(shape, dtype) if stays else ja...]
    ppermute x3, waiting for transfers between devices: 4.79 us -> 1.8 us  [shards(): lax.ppermute(chip_half, 'mlp', [(i, (i + shift) % mlp_count) for i in ran...]
    unnamed x16 -> x20, local copies, waits for them, and re-layouts: 3.76 us -> 3 us
    all_to_all x3 -> x4, waiting for transfers between devices: 33.9 us -> 33.6 us  [exchange(): return lax.all_to_all(copies, axis, split_axis=0, concat_axis=0, tiled=True)]
  transfers between devices with their start and end apart: 8 -> 9, of which waited for: 7 -> 7; matrix products, arithmetic and copies ran while one was open for 3% -> 3% of each run, Pallas kernels for 0% -> 7%
where the time goes in v3:
time: 110 us
  starting transfers between devices  39.8 us (36%)
  waiting for transfers between devices  37.3 us (34%)
  Pallas kernels  23.5 us (21%)
  local copies, waits for them, and re-layouts  4.49 us (4%)
  between operations  2.79 us (3%)
  other arithmetic  1.72 us (2%)
    all_to_all x4, starting transfers between devices, exchange(): return lax.all_to_all(copies, axis, split_axis=0, concat_axis=0, tiled=True)  33.9 us
    all_to_all x4, waiting for transfers between devices, exchange(): return lax.all_to_all(copies, axis, split_axis=0, concat_axis=0, tiled=True)  33.6 us
    pallas_call x9, Pallas kernels, call(): pl.pallas_call(body, out_shape=[pltpu.VMEM(shape, dtype) if stays else ja...  16.3 us
    pallas_call x4, Pallas kernels, fetch(): pl.pallas_call(fetch_rows, out_shape=[pltpu.VMEM((rows,) + far.shape[1:],...  7.29 us
    unnamed x20, local copies, waits for them, and re-layouts  3 us
    ppermute x3, starting transfers between devices, shards(): lax.ppermute(chip_half, 'mlp', [(i, (i + shift) % mlp_count) for i in ran...  2.76 us
  transfers between devices with their start and end apart: 9, of which 7 were waited for; matrix products, arithmetic and copies ran while one was open for 3% of the time, Pallas kernels for 7%

profile of v3, /device:TPU:1, one launch (start us, length us, event | category | flops | bytes accessed | tf_op | source)
XLA Modules:
  0.0 109.6 jit_solution(13377667166714815565)
XLA Ops:
  0.6 0.0 copy-start
  0.6 1.7 %send_queries.1.refs_0_ = bf16[32,40,256]{2,1,0:T(8,128)(2,1)} custom-call(bf16[4,2560]{1,0:T(4,128)(2,1)} %queries_ref.1), custom_call_target="tpu_custom_call" | custom-call | tf_op jit(solution)/shard_map/send_queries/pallas_call | solution.py:333
  2.3 11.9 %all-to-all-start = ((bf16[32,40,256]{2,1,0:T(8,128)(2,1)}), bf16[32,40,256]{2,1,0:T(8,128)(2,1)S(1)}, u32[]{:S(2)}, u32[]{:S(2)}) async-start(bf16[32,40,256]{2,1,0:T(8,128)(2,1)} %send_queries.1.refs_0_), calls=%async_computation | async-start | bytes 1310720 | tf_op jit(solution)/shard_map/all_to_all | solution.py:370
  14.2 0.8 reshape.62
  15.0 1.8 %fetch_rows.4 = (bf16[8,128,512]{2,1,0:T(8,128)(2,1)S(1)}, f32[8,128]{1,0:T(8,128)}) custom-call(bf16[32,40,256]{2,1,0:T(8,128)(2,1)} %send_queries.1.refs_0_, bf16[17,128,512]{2,1,0:T(8,128)(2,1)} %far_ref.3), custom_call_target="tpu_custom_call" | custom-call | tf_op jit(solution)/shard_map/fetch_rows/pallas_call | solution.py:358
  16.8 0.7 dynamic-slice_reduce_fusion.length_ref
  17.5 0.0 copy-done
  17.6 0.1 add_add_fusion
  17.6 1.0 select_reduce_fusion.code_ref
  18.6 12.0 %all-to-all-done.rows_ref = bf16[32,40,256]{2,1,0:T(8,128)(2,1)S(1)} async-done(((bf16[32,40,256]{2,1,0:T(8,128)(2,1)}), bf16[32,40,256]{2,1,0:T(8,128)(2,1)S(1)}, u32[]{:S(2)}, u32[]{:S(2)}) %all-to-all-start) | async-done | bytes 655392 | tf_op jit(solution)/shard_map/all_to_all | solution.py:370
  30.6 6.2 %attend_pages.1.refs_0_ = bf16[32,4,2688]{2,1,0:T(4,128)(2,1)} custom-call(s32[17]{0:T(128)} %select_reduce_fusion.code_ref, s32[32]{0:T(128)} %dynamic-slice_reduce_fusion.length_ref, bf16[32,40,256]{2,1,0:T(8,128)(2,1)S(1)} %all-to-all-done.rows_ref, bf16[8,128,512]{2,1,0:T(8,128)(2,1)S(1)} %get-tuple-element.20.front_ref, bf16[17,128,512]{2,1,0:T(8,128)(2,1)} %far_ref.3), custom_call_target="tpu_custom_call" | custom-call | tf_op jit(solution)/shard_map/attend_pages/pallas_call | solution.py:333
  36.9 0.0 copy-start.5
  36.9 8.4 %all-to-all-start.1 = ((bf16[32,4,2688]{2,1,0:T(4,128)(2,1)}), bf16[32,4,2688]{2,1,0:T(4,128)(2,1)S(1)}, u32[]{:S(2)}, u32[]{:S(2)}) async-start(bf16[32,4,2688]{2,1,0:T(4,128)(2,1)} %attend_pages.1.refs_0_), calls=%async_computation.1 | async-start | bytes 1376256 | tf_op jit(solution)/shard_map/all_to_all | solution.py:370
  45.3 0.6 fusion
  47.9 0.0 copy-done.4
  47.9 0.0 copy-done.7
  47.9 0.3 attend_new.1
  48.3 14.3 %all-to-all-done.1.refs_0_ = bf16[32,4,2688]{2,1,0:T(4,128)(2,1)S(1)} async-done(((bf16[32,4,2688]{2,1,0:T(4,128)(2,1)}), bf16[32,4,2688]{2,1,0:T(4,128)(2,1)S(1)}, u32[]{:S(2)}, u32[]{:S(2)}) %all-to-all-start.1) | async-done | bytes 688160 | tf_op jit(solution)/shard_map/all_to_all | solution.py:370
  62.6 0.9 merge_new.1
  63.5 9.4 %all-to-all-start.2 = ((bf16[8,4,2560]{2,1,0:T(4,128)(2,1)}), bf16[8,4,2560]{2,1,0:T(4,128)(2,1)S(1)}, u32[]{:S(2)}, u32[]{:S(2)}) async-start(bf16[8,4,2560]{2,1,0:T(4,128)(2,1)} %get-tuple-element.25), calls=%async_computation.2 | async-start | bytes 327680 | tf_op jit(solution)/shard_map/all_to_all | solution.py:370
  72.9 2.0 %fetch_rows.5 = (bf16[320,2560]{1,0:T(8,128)(2,1)S(1)}, f32[8,128]{1,0:T(8,128)}) custom-call(bf16[32,4,2688]{2,1,0:T(4,128)(2,1)} %attend_pages.1.refs_0_, bf16[320,2560]{1,0:T(8,128)(2,1)} %bitcast.14), custom_call_target="tpu_custom_call" | custom-call | tf_op jit(solution)/shard_map/fetch_rows/pallas_call | solution.py:358
  74.9 3.5 %all-to-all-done.2.rows_ref = bf16[8,4,2560]{2,1,0:T(4,128)(2,1)S(1)} async-done(((bf16[8,4,2560]{2,1,0:T(4,128)(2,1)}), bf16[8,4,2560]{2,1,0:T(4,128)(2,1)S(1)}, u32[]{:S(2)}, u32[]{:S(2)}) %all-to-all-start.2) | async-done | bytes 163872 | tf_op jit(solution)/shard_map/all_to_all | solution.py:370
  78.4 0.0 copy-done.5
  78.4 1.3 %project_out.1.refs_0_ = bf16[8,32,320]{2,1,0:T(8,128)(2,1)} custom-call(bf16[8,4,2560]{2,1,0:T(4,128)(2,1)S(1)} %all-to-all-done.2.rows_ref, bf16[320,2560]{1,0:T(8,128)(2,1)S(1)} %get-tuple-element.26.weight_ref, bf16[32,320]{1,0:T(8,128)(2,1)S(1)} %copy-done.5), custom_call_target="tpu_custom_call" | custom-call | tf_op jit(solution)/shard_map/project_out/pallas_call | solution.py:333
  79.7 4.2 %all-to-all-start.3 = ((bf16[8,32,320]{2,1,0:T(8,128)(2,1)}), bf16[8,32,320]{2,1,0:T(8,128)(2,1)S(1)}, u32[]{:S(2)}, u32[]{:S(2)}) async-start(bf16[8,32,320]{2,1,0:T(8,128)(2,1)} %project_out.1.refs_0_), calls=%async_computation.3 | async-start | bytes 393216 | tf_op jit(solution)/shard_map/all_to_all | solution.py:370
  83.9 0.0 copy-done.8
  83.9 2.1 %fetch_rows.6 = (bf16[128,2560]{1,0:T(8,128)(2,1)S(1)}, bf16[128,2560]{1,0:T(8,128)(2,1)S(1)}, bf16[128,2560]{1,0:T(8,128)(2,1)S(1)}, f32[8,128]{1,0:T(8,128)}) custom-call(bf16[8,32,320]{2,1,0:T(8,128)(2,1)} %project_out.1.refs_0_, bf16[480,2560]{1,0:T(8,128)(2,1)} %bitcast.10, bf16[480,2560]{1,0:T(8,128)(2,1)} %bitcast.12, bf16[480,2560]{1,0:T(8,128)(2,1)} %down_far.1), custom_call_target="tpu_custom_call" | custom-call | tf_op jit(solution)/shard_map/fetch_rows/pallas_call | solution.py:358
  86.0 3.8 %all-to-all-done.3.stream_ref = bf16[8,32,320]{2,1,0:T(8,128)(2,1)S(1)} async-done(((bf16[8,32,320]{2,1,0:T(8,128)(2,1)}), bf16[8,32,320]{2,1,0:T(8,128)(2,1)S(1)}, u32[]{:S(2)}, u32[]{:S(2)}) %all-to-all-start.3) | async-done | bytes 163872 | tf_op jit(solution)/shard_map/all_to_all | solution.py:370
  89.8 3.7 %feed_forward.1 = (f32[32,1280]{1,0:T(8,128)S(1)}, bf16[32,1280]{1,0:T(8,128)(2,1)S(1)}, f32[32,1280]{1,0:T(8,128)S(1)}) custom-call(s32[1]{0:T(128)} %bitcast.4.core_ref, bf16[8,32,320]{2,1,0:T(8,128)(2,1)S(1)} %all-to-all-done.3.stream_ref, f32[1,2560]{1,0:T(1,128)S(1)} %reshape.65.gain_ref, bf16[128,2560]{1,0:T(8,128)(2,1)S(1)} %get-tuple-element.27.gate_ref, ...), custom_call_target="tpu_custom_call" | custom-call | tf_op jit(solution)/shard_map/feed_forward/pallas_call | solution.py:333
  93.5 0.0 copy-start.9
  93.5 1.0 collective-permute-start
  94.5 0.9 collective-permute-done.got_ref
  95.5 0.0 copy-start.3
  95.5 0.4 collective-permute-start.1
  95.9 2.4 %collective-permute-start.2 = (bf16[32,1280]{1,0:T(8,128)(2,1)S(1)}, bf16[32,1280]{1,0:T(8,128)(2,1)S(1)}, u32[]{:S(2)}, u32[]{:S(2)}) collective-permute-start(bf16[32,1280]{1,0:T(8,128)(2,1)S(1)} %add_pair.1.refs_0_), channel_id=1, source_target_pairs={{0,6},{1,7},{2,0},{3,1},{4,2},{5,3},{6,4},{7,5},{8,14},{9,15},{10,... | collective-permute-start | bytes 245768 | tf_op jit(solution)/shard_map/ppermute | solution.py:483
  98.2 0.0 collective-permute-start.3
  98.2 1.3 %fetch_rows.7 = (bf16[1664,384]{1,0:T(8,128)(2,1)S(1)}, f32[8,128]{1,0:T(8,128)S(1)}) custom-call(bf16[32,1280]{1,0:T(8,128)(2,1)} %copy-done.3, bf16[2560,384]{1,0:T(8,128)(2,1)} %weight_far.1), custom_call_target="tpu_custom_call" | custom-call | tf_op jit(solution)/shard_map/fetch_rows/pallas_call | solution.py:358
  99.6 0.0 copy-start.1
  99.6 1.1 copy-done.1
  100.6 0.6 copy-done.6
  101.2 0.0 collective-permute-done.1.first_ref
  101.2 0.0 collective-permute-done.2.second_ref
  101.2 1.8 %collective-permute-done.3.third_ref = bf16[32,1280]{1,0:T(8,128)(2,1)S(1)} collective-permute-done((bf16[32,1280]{1,0:T(8,128)(2,1)S(1)}, bf16[32,1280]{1,0:T(8,128)(2,1)S(1)}, u32[]{:S(2)}, u32[]{:S(2)}) %collective-permute-start.3) | collective-permute-done | bytes 81952 | tf_op jit(solution)/shard_map/ppermute | solution.py:483
  103.0 0.1 add_chips.1.own_ref
  103.1 2.2 %collective-permute-start.4 = (bf16[32,1280]{1,0:T(8,128)(2,1)S(1)}, bf16[32,1280]{1,0:T(8,128)(2,1)S(1)}, u32[]{:S(2)}, u32[]{:S(2)}) collective-permute-start(bf16[32,1280]{1,0:T(8,128)(2,1)S(1)} %add_chips.1.own_ref), channel_id=1, source_target_pairs={{0,1},{1,0},{2,3},{3,2},{4,5},{5,4},{6,7},{7,6},{8,9},{9,8},{10,11... | collective-permute-start | bytes 245768 | tf_op jit(solution)/shard_map/ppermute | solution.py:491
  105.3 0.9 collective-permute-done.4.other_ref
  106.2 1.3 %copy-done.2 = bf16[1664,384]{1,0:T(8,128)(2,1)S(1)} copy-done((bf16[1664,384]{1,0:T(8,128)(2,1)S(1)}, bf16[1664,384]{1,0:T(8,128)(2,1)}, u32[]{:S(2)}) %copy-start.2) | copy-done | bytes 1277976
  107.5 2.1 %project_next.1 = (bf16[32,320]{1,0:T(8,128)(2,1)}, bf16[32,384]{1,0:T(8,128)(2,1)}) custom-call(s32[1]{0:T(128)} %bitcast.3.place_ref, bf16[32,1280]{1,0:T(8,128)(2,1)S(1)} %add_chips.1.own_ref, bf16[32,1280]{1,0:T(8,128)(2,1)S(1)} %collective-permute-done.4.other_ref, f32[1,2560]{1,0:T(1,128)S(1)} %reshape.66.gain_ref, bf16[1664,384]{1,0:T(8,128)(2,1)S(1)} %copy-done.2, ...), custom_call_target="tpu_custom_call" | custom-call | tf_op jit(solution)/shard_map/project_next/pallas_call | solution.py:333
  (13 shorter events, 0.1 us)
Async XLA Ops:
  0.6 16.9 %copy-start = (s32[256,128]{1,0:T(8,128)S(1)}, s32[256,128]{1,0:T(8,128)}, u32[]{:S(2)}) copy-start(s32[256,128]{1,0:T(8,128)} %param.17) | copy-start | bytes 393220
  2.3 28.3 %all-to-all-start = ((bf16[32,40,256]{2,1,0:T(8,128)(2,1)}), bf16[32,40,256]{2,1,0:T(8,128)(2,1)S(1)}, u32[]{:S(2)}, u32[]{:S(2)}) async-start(bf16[32,40,256]{2,1,0:T(8,128)(2,1)} %send_queries.1.refs_0_), calls=%async_computation | async-start | bytes 1310720 | tf_op jit(solution)/shard_map/all_to_all | solution.py:370
  30.6 17.3 %copy-start.4 = (bf16[4,2560]{1,0:T(4,128)(2,1)S(1)}, bf16[4,2560]{1,0:T(4,128)(2,1)}, u32[]{:S(2)}) copy-start(bf16[4,2560]{1,0:T(4,128)(2,1)} %queries_ref.1) | copy-start | bytes 61444
  30.6 17.3 %copy-start.7 = (bf16[4,512]{1,0:T(4,128)(2,1)S(1)}, bf16[4,512]{1,0:T(4,128)(2,1)}, u32[]{:S(2)}) copy-start(bf16[4,512]{1,0:T(4,128)(2,1)} %new_ref.1) | copy-start | bytes 12292
  36.9 41.6 %copy-start.5 = (bf16[32,320]{1,0:T(8,128)(2,1)S(1)}, bf16[32,320]{1,0:T(8,128)(2,1)}, u32[]{:S(2)}) copy-start(bf16[32,320]{1,0:T(8,128)(2,1)} %residual_ref.1) | copy-start | bytes 61444
  36.9 25.7 %all-to-all-start.1 = ((bf16[32,4,2688]{2,1,0:T(4,128)(2,1)}), bf16[32,4,2688]{2,1,0:T(4,128)(2,1)S(1)}, u32[]{:S(2)}, u32[]{:S(2)}) async-start(bf16[32,4,2688]{2,1,0:T(4,128)(2,1)} %attend_pages.1.refs_0_), calls=%async_computation.1 | async-start | bytes 1376256 | tf_op jit(solution)/shard_map/all_to_all | solution.py:370
  63.5 15.0 %all-to-all-start.2 = ((bf16[8,4,2560]{2,1,0:T(4,128)(2,1)}), bf16[8,4,2560]{2,1,0:T(4,128)(2,1)S(1)}, u32[]{:S(2)}, u32[]{:S(2)}) async-start(bf16[8,4,2560]{2,1,0:T(4,128)(2,1)} %get-tuple-element.25), calls=%async_computation.2 | async-start | bytes 327680 | tf_op jit(solution)/shard_map/all_to_all | solution.py:370
  72.8 11.1 %copy-start.8 = (f32[2560]{0:T(1024)S(1)}, f32[2560]{0:T(1024)}, u32[]{:S(2)}) copy-start(f32[2560]{0:T(1024)} %param.20) | copy-start | bytes 30724
  79.7 10.1 %all-to-all-start.3 = ((bf16[8,32,320]{2,1,0:T(8,128)(2,1)}), bf16[8,32,320]{2,1,0:T(8,128)(2,1)S(1)}, u32[]{:S(2)}, u32[]{:S(2)}) async-start(bf16[8,32,320]{2,1,0:T(8,128)(2,1)} %project_out.1.refs_0_), calls=%async_computation.3 | async-start | bytes 393216 | tf_op jit(solution)/shard_map/all_to_all | solution.py:370
  93.5 11.8 %copy-start.9 = (f32[2560]{0:T(1024)S(1)}, f32[2560]{0:T(1024)}, u32[]{:S(2)}) copy-start(f32[2560]{0:T(1024)} %param.24) | copy-start | bytes 30724
  93.5 2.0 %collective-permute-start = (bf16[32,1280]{1,0:T(8,128)(2,1)S(1)}, bf16[32,1280]{1,0:T(8,128)(2,1)S(1)}, u32[]{:S(2)}, u32[]{:S(2)}) collective-permute-start(bf16[32,1280]{1,0:T(8,128)(2,1)S(1)} %get-tuple-element.31), channel_id=1, source_target_pairs={{0,1},{1,0},{2,3},{3,2},{4,5},{5,4},{6,7},{7,6},{8,9},{9,8},{10,11... | collective-permute-start | bytes 245768 | tf_op jit(solution)/shard_map/ppermute | solution.py:480
  95.5 2.8 %copy-start.3 = (bf16[32,1280]{1,0:T(8,128)(2,1)}, bf16[32,1280]{1,0:T(8,128)(2,1)S(1)}, u32[]{:S(2)}) copy-start(bf16[32,1280]{1,0:T(8,128)(2,1)S(1)} %add_pair.1.refs_0_) | copy-start | bytes 245764
  95.5 5.8 %collective-permute-start.1 = (bf16[32,1280]{1,0:T(8,128)(2,1)S(1)}, bf16[32,1280]{1,0:T(8,128)(2,1)S(1)}, u32[]{:S(2)}, u32[]{:S(2)}) collective-permute-start(bf16[32,1280]{1,0:T(8,128)(2,1)S(1)} %add_pair.1.refs_0_), channel_id=1, source_target_pairs={{0,2},{1,3},{2,4},{3,5},{4,6},{5,7},{6,0},{7,1},{8,10},{9,11},{10,... | collective-permute-start | bytes 245768 | tf_op jit(solution)/shard_map/ppermute | solution.py:483
  95.9 5.4 %collective-permute-start.2 = (bf16[32,1280]{1,0:T(8,128)(2,1)S(1)}, bf16[32,1280]{1,0:T(8,128)(2,1)S(1)}, u32[]{:S(2)}, u32[]{:S(2)}) collective-permute-start(bf16[32,1280]{1,0:T(8,128)(2,1)S(1)} %add_pair.1.refs_0_), channel_id=1, source_target_pairs={{0,6},{1,7},{2,0},{3,1},{4,2},{5,3},{6,4},{7,5},{8,14},{9,15},{10,... | collective-permute-start | bytes 245768 | tf_op jit(solution)/shard_map/ppermute | solution.py:483
  98.2 4.8 %collective-permute-start.3 = (bf16[32,1280]{1,0:T(8,128)(2,1)S(1)}, bf16[32,1280]{1,0:T(8,128)(2,1)S(1)}, u32[]{:S(2)}, u32[]{:S(2)}) collective-permute-start(bf16[32,1280]{1,0:T(8,128)(2,1)S(1)} %add_pair.1.refs_0_), channel_id=1, source_target_pairs={{0,4},{1,5},{2,6},{3,7},{4,0},{5,1},{6,2},{7,3},{8,12},{9,13},{10,... | collective-permute-start | bytes 245768 | tf_op jit(solution)/shard_map/ppermute | solution.py:483
  99.6 1.1 copy-start.1
  100.6 0.6 copy-start.6
  103.1 3.1 %collective-permute-start.4 = (bf16[32,1280]{1,0:T(8,128)(2,1)S(1)}, bf16[32,1280]{1,0:T(8,128)(2,1)S(1)}, u32[]{:S(2)}, u32[]{:S(2)}) collective-permute-start(bf16[32,1280]{1,0:T(8,128)(2,1)S(1)} %add_chips.1.own_ref), channel_id=1, source_target_pairs={{0,1},{1,0},{2,3},{3,2},{4,5},{5,4},{6,7},{7,6},{8,9},{9,8},{10,11... | collective-permute-start | bytes 245768 | tf_op jit(solution)/shard_map/ppermute | solution.py:491
  106.2 1.3 %copy-start.2 = (bf16[1664,384]{1,0:T(8,128)(2,1)S(1)}, bf16[1664,384]{1,0:T(8,128)(2,1)}, u32[]{:S(2)}) copy-start(bf16[1664,384]{1,0:T(8,128)(2,1)} %copy-done.1) | copy-start | bytes 3833860

commit v4 on v3

--- a/solution.py
+++ b/solution.py
@@ -30,17 +30,10 @@
     return placed
 
 
-def send_queries(far_ref, *refs, splits):
-    outs, queries_ref, copied = refs[:-2], refs[-2], refs[-1]
-    copy = pltpu.make_async_copy(far_ref, queries_ref, copied.at[0])
-    copy.start()
-    copy.wait()
-    for (start, stop), out_ref in zip(splits, outs):
-        head_dim = out_ref.shape[2]
-        values = queries_ref[:, start * head_dim : stop * head_dim].astype(F32)
-        rows = head_major(values, head_dim).astype(BF16)
-        for place in range(out_ref.shape[0]):
-            out_ref[place] = rows
+def send_queries(queries_ref, out_ref):
+    rows = head_major(queries_ref[...].astype(F32), out_ref.shape[2]).astype(BF16)
+    for place in range(out_ref.shape[0]):
+        out_ref[place] = rows
 
 
 def attend_new(queries_ref, new_ref, max_ref, sum_ref, acc_ref):
@@ -69,7 +62,7 @@
 
 
 def attend_pages(
-    code_ref, length_ref, rows_ref, front_ref, far_ref, out_ref, score_ref, peak_ref, rest_ref, copied
+    code_ref, length_ref, rows_ref, front_ref, far_ref, out_ref, score_ref, peak_ref, acc_ref, rest_ref, end_ref, copied
 ):
     slot_count, page_len, kv_width = far_ref.shape
     near_count = front_ref.shape[0]
@@ -117,36 +110,42 @@
         score_ref[slot] = scores
         peak = jnp.maximum(scores, jnp.where(first[slot], NEG_FILL, peak) if slot else fill)
         peak_ref[slot] = jnp.broadcast_to(jnp.max(peak, axis=1, keepdims=True), (query_rows, page_len))
+    peak = peak_ref[slot_count - 1]
     for slot in range(slot_count - 2, -1, -1):
-        peak_ref[slot] = jnp.where(last[slot], peak_ref[slot], peak_ref[slot + 1])
+        peak = jnp.where(last[slot], peak_ref[slot], peak)
+        peak_ref[slot] = peak
     total = jnp.zeros((query_rows, page_len), F32)
     acc = jnp.zeros((query_rows, head_dim), F32)
+    held = jnp.int32(0)
     for slot in range(slot_count):
         weights = jnp.exp(score_ref[slot] - peak_ref[slot])
-        value = jnp.dot(weights.astype(BF16), cached(slot, slice(head_dim, kv_width)), preferred_element_type=F32)
+        value = jnp.dot(
+            weights.astype(BF16), cached(slot, slice(head_dim, kv_width)), preferred_element_type=F32
+        )
         total = weights + (jnp.where(first[slot], 0.0, total) if slot else 0.0)
         acc = value + (jnp.where(first[slot], 0.0, acc) if slot else 0.0)
-        finished_total, finished_acc = total, acc
-
-        @pl.when((codes[slot] > 0) & last[slot])
-        def _():
-            whole_sum = jnp.sum(finished_total, axis=1, keepdims=True)
-            result = finished_acc / whole_sum
-            for head in range(head_count):
-                out_ref[sources[slot], :, head * head_dim : (head + 1) * head_dim] = result[
-                    head * token_count : (head + 1) * token_count, :
-                ].astype(BF16)
-            whole = put_heads(peak_ref[slot][:, :1] + jnp.log(whole_sum), token_count, 128)
-            high = whole.astype(BF16).astype(F32)
-            middle = (whole - high).astype(BF16).astype(F32)
-            low = whole - high - middle
-            lanes = lax.broadcasted_iota(jnp.int32, whole.shape, 1)
-            packed = jnp.where(
-                lanes < 16,
-                high,
-                jnp.where(lanes < 32, pltpu.roll(middle, 16, 1), pltpu.roll(low, 32, 1)),
-            )
-            out_ref[sources[slot], :, width:] = packed.astype(BF16)
+        score_ref[slot] = total
+        acc_ref[slot] = acc
+        end_ref[held] = slot
+        held = held + ((codes[slot] > 0) & last[slot]).astype(jnp.int32)
+    lanes = lax.broadcasted_iota(jnp.int32, (token_count, 128), 1)
+    for turn in range(slot_count // 2):
+        slot = end_ref[jnp.where(turn < held, turn, 0)]
+        source = jnp.maximum(code_ref[slot] - 1, 0) // page_count
+        whole_sum = jnp.sum(score_ref[slot], axis=1, keepdims=True)
+        result = acc_ref[slot] / whole_sum
+        for head in range(head_count):
+            out_ref[source, :, head * head_dim : (head + 1) * head_dim] = result[
+                head * token_count : (head + 1) * token_count, :
+            ].astype(BF16)
+        whole = put_heads(peak_ref[slot][:, :1] + jnp.log(whole_sum), token_count, 128)
+        high = whole.astype(BF16).astype(F32)
+        middle = (whole - high).astype(BF16).astype(F32)
+        low = whole - high - middle
+        packed = jnp.where(
+            lanes < 16, high, jnp.where(lanes < 32, pltpu.roll(middle, 16, 1), pltpu.roll(low, 32, 1))
+        )
+        out_ref[source, :, width:] = packed.astype(BF16)
 
 
 def merge_new(holder_ref, *refs, splits):
@@ -181,35 +180,24 @@
                 spread_ref[place, :, whole] = rows
 
 
-def project_out(rows_ref, weight_ref, residual_ref, out_ref):
-    places, token_count, width = rows_ref.shape
+def project_out(rows_ref, residual_ref, front_ref, weight_far, out_ref, rest_ref, copied):
+    places = rows_ref.shape[0]
+    near_rows = front_ref.shape[0]
+    rest = pltpu.make_async_copy(weight_far.at[pl.ds(near_rows, rest_ref.shape[0])], rest_ref, copied.at[0])
+    rest.start()
     rows = jnp.concatenate([rows_ref[place].astype(F32) for place in range(places)], axis=0).astype(BF16)
-    attention_out = lax.dot_general(rows, weight_ref[...], LAST, preferred_element_type=F32)
-    stream = (residual_ref[...].astype(F32) + attention_out).astype(BF16)
-    for place in range(places):
-        out_ref[place] = stream
-
-
-def feed_forward(
-    core_ref,
-    stream_ref,
-    gain_ref,
-    gate_ref,
-    up_ref,
-    down_ref,
-    gate_far,
-    up_far,
-    down_far,
-    keep_ref,
-    send_ref,
-    stream_half_ref,
-    whole_ref,
-    halves_ref,
-    gate_rest,
-    up_rest,
-    down_rest,
-    copied,
-):
+    attention_out = lax.dot_general(rows, front_ref[...], LAST, preferred_element_type=F32)
+    out_ref[:, :near_rows] = (residual_ref[:, :near_rows].astype(F32) + attention_out).astype(BF16)
+    rest.wait()
+    attention_out = lax.dot_general(rows, rest_ref[...], LAST, preferred_element_type=F32)
+    out_ref[:, near_rows:] = (residual_ref[:, near_rows:].astype(F32) + attention_out).astype(BF16)
+
+
+def feed_forward(place_ref, *refs):
+    block_refs = refs[:8]
+    gain_ref, gate_ref, up_ref, down_ref, gate_far, up_far, down_far = refs[8:15]
+    keep_ref, send_ref, base_ref = refs[15:18]
+    stream_ref, whole_ref, halves_ref, gate_rest, up_rest, down_rest, copied = refs[18:]
     parts, rows, width = stream_ref.shape
     total = parts * width
     half = total // 2
@@ -227,20 +215,14 @@
                 )
             )
             copies[-1].start()
+    for distance, block_ref in enumerate(block_refs):
+        stream_ref[place_ref[0] ^ distance] = block_ref[...].astype(F32)
     for part in range(parts):
-        whole_ref[:, part * width : (part + 1) * width] = stream_ref[part].astype(F32)
+        whole_ref[:, part * width : (part + 1) * width] = stream_ref[part]
     whole = whole_ref[...]
     square = jnp.sum(whole * whole, axis=1, keepdims=True)
     normed = (whole * lax.rsqrt(square / total + 1e-06) * gain_ref[...]).astype(BF16)
-    core = core_ref[0]
-
-    @pl.when(core == 0)
-    def _():
-        stream_half_ref[...] = whole_ref[:, :half]
-
-    @pl.when(core == 1)
-    def _():
-        stream_half_ref[...] = whole_ref[:, half:]
+    core = place_ref[0] % 2
 
     def through(gate_rows, up_rows, down_rows):
         gate = lax.dot_general(normed, gate_rows, LAST, preferred_element_type=F32)
@@ -259,15 +241,23 @@
     keep_ref[...] = halves_ref[core]
     send_ref[...] = halves_ref[1 - core].astype(BF16)
 
+    @pl.when(core == 0)
+    def _():
+        base_ref[...] = whole_ref[:, :half] + keep_ref[...]
+
+    @pl.when(core == 1)
+    def _():
+        base_ref[...] = whole_ref[:, half:] + keep_ref[...]
+
 
 def add_pair(keep_ref, got_ref, send_ref):
     send_ref[...] = (keep_ref[...] + got_ref[...].astype(F32)).astype(BF16)
 
 
-def add_chips(keep_ref, got_ref, first_ref, second_ref, third_ref, stream_ref, fetched_ref, out_ref):
-    total = keep_ref[...] + got_ref[...].astype(F32)
+def add_chips(base_ref, got_ref, first_ref, second_ref, third_ref, fetched_ref, out_ref):
+    total = base_ref[...] + got_ref[...].astype(F32)
     total = total + first_ref[...].astype(F32) + second_ref[...].astype(F32) + third_ref[...].astype(F32)
-    out_ref[...] = (stream_ref[...] + total).astype(BF16)
+    out_ref[...] = total.astype(BF16)
 
 
 def project_next(
@@ -326,8 +316,8 @@
     return pltpu.with_memory_space_constraint(array, pltpu.VMEM)
 
 
-def call(body, outs, scalars, arrays, far=(), scratch=(), copies=0):
-    scratch_shapes = [pltpu.VMEM(shape, dtype) for shape, dtype in scratch]
+def call(body, outs, scalars, arrays, far=(), scratch=(), copies=0, more=()):
+    scratch_shapes = [pltpu.VMEM(shape, dtype) for shape, dtype in scratch] + list(more)
     if copies:
         scratch_shapes.append(pltpu.SemaphoreType.DMA((copies,)))
     return pl.pallas_call(
@@ -358,7 +348,7 @@
     return pl.pallas_call(
         fetch_rows,
         out_shape=[pltpu.VMEM((rows,) + far.shape[1:], far.dtype) for far, rows in parts]
-        + [pltpu.VMEM((8, 128), F32)],
+        + [jax.ShapeDtypeStruct((8, 128), F32)],
         in_specs=[FAR] * (len(parts) + 1),
         out_specs=[VMEM] * (len(parts) + 1),
         scratch_shapes=[pltpu.SemaphoreType.DMA((len(parts),))],
@@ -368,6 +358,17 @@
 
 def exchange(copies, axis):
     return lax.all_to_all(copies, axis, split_axis=0, concat_axis=0, tiled=True)
+
+
+def partner(block, distance):
+    count = lax.axis_size("mlp")
+    return lax.ppermute(block, "mlp", [(i, i ^ distance) for i in range(count)])
+
+
+def gather(block):
+    near = {0: block, **{distance: partner(block, distance) for distance in (2, 6, 4)}}
+    far = {distance ^ 1: partner(near[distance], 1) for distance in near}
+    return [{**near, **far}[distance] for distance in range(8)]
 
 
 def shards(
@@ -398,17 +399,16 @@
     half = width // 2
 
     splits = ((0, width // head_dim),)
-    sizes = [token_count * (stop - start) for start, stop in splits]
-    sents = call(
-        functools.partial(send_queries, splits=splits),
-        [((seq_count, size, head_dim), BF16, True) for size in sizes],
-        [],
-        [],
-        [queries],
-        [(queries.shape, BF16)],
-        1,
-    )
-    column_rows = [exchange(sent, "seq") for sent in sents]
+    query_rows = token_count * (width // head_dim)
+    sent = pl.pallas_call(
+        send_queries,
+        out_shape=jax.ShapeDtypeStruct((seq_count, query_rows, head_dim), BF16),
+        in_specs=[VMEM],
+        out_specs=VMEM,
+        name="send_queries",
+    )(queries)
+    sents = [sent]
+    column_rows = [exchange(sent, "seq")]
 
     column_table = lax.dynamic_index_in_dim(
         page_table.reshape(seq_count, mlp_count, page_count), mlp_place, 1, keepdims=False
@@ -434,18 +434,21 @@
         [],
         [queries, new_kv],
     )
-    cache_front, _ = fetch([(kv_cache, 8)], sents[-1])
+    near_slots = 11
+    cache_front, _ = fetch([(kv_cache, near_slots)], sents[-1])
     returned = []
     for arrived in column_rows:
         (held,) = call(
             attend_pages,
-            [((seq_count, token_count, arrived.shape[1] // token_count * head_dim + 128), BF16, True)],
+            [((seq_count, token_count, arrived.shape[1] // token_count * head_dim + 128), BF16, False)],
             [codes, column_lengths],
             [arrived, cache_front],
             [kv_cache],
             [((slot_count, arrived.shape[1], page_len), F32)] * 2
-            + [((slot_count - 8, page_len, kv_width), BF16)],
+            + [((slot_count, arrived.shape[1], head_dim), F32)]
+            + [((slot_count - near_slots, page_len, kv_width), BF16)],
             1,
+            [pltpu.SMEM((slot_count + 1,), jnp.int32)],
         )
         returned.append(exchange(held, "seq"))
     attended, spread = call(
@@ -455,44 +458,45 @@
         [*returned, new_max, new_sum, new_acc],
     )
     rows = exchange(spread, "mlp")
-    (streams,) = call(
+    layers = [(gate_weight.T, 96), (up_weight.T, 96), (down_weight, 96)]
+    out_front, *front, _ = fetch([(out_weight.T, 128), *layers], held)
+    (stream,) = call(
         project_out,
-        [((mlp_count, row_count, part_width), BF16, True)],
+        [((row_count, part_width), BF16, True)],
         [],
-        [rows, *fetch([(out_weight.T, part_width)], held)[:-1], residual],
-    )
-    layers = [(gate_weight.T, 128), (up_weight.T, 128), (down_weight, 128)]
-    *front, _ = fetch(layers, streams)
-    streams = exchange(streams, "mlp")
-
-    core = (mlp_place % 2).astype(jnp.int32).reshape(1)
-    keep, send, stream_half = call(
+        [rows, residual, out_front],
+        [out_weight.T],
+        [((part_width - 128, width), BF16)],
+        1,
+    )
+    place = mlp_place.astype(jnp.int32).reshape(1)
+    keep, send, base = call(
         feed_forward,
         [((row_count, half), F32, True), ((row_count, half), BF16, True), ((row_count, half), F32, True)],
-        [core],
-        [streams, norm_gain.reshape(1, width), *front],
+        [place],
+        [*gather(stream), norm_gain.reshape(1, width), *front],
         [far for far, _ in layers],
-        [((row_count, width), F32), ((2, row_count, half), F32)]
+        [
+            ((mlp_count, row_count, part_width), F32),
+            ((row_count, width), F32),
+            ((2, row_count, half), F32),
+        ]
         + [((far.shape[0] - rows, width), BF16) for far, rows in layers],
         6,
     )
-    pair = [(i, i ^ 1) for i in range(mlp_count)]
-    got = lax.ppermute(send, "mlp", pair)
+    got = partner(send, 1)
     (chip_half,) = call(add_pair, [((row_count, half), BF16, True)], [], [keep, got])
-    others = [
-        lax.ppermute(chip_half, "mlp", [(i, (i + shift) % mlp_count) for i in range(mlp_count)])
-        for shift in (2, 6, 4)
-    ]
-    near_rows = 1664
-    qkv_front, fetched = fetch([(qkv_weight, near_rows)], chip_half)
+    others = [partner(chip_half, distance) for distance in (2, 6, 4)]
+    near_rows = 1536
+    qkv_front, fetched = fetch([(qkv_weight, near_rows)], held)
     (after_half,) = call(
-        add_chips, [((row_count, half), BF16, True)], [], [keep, got, *others, stream_half], [fetched]
-    )
-    other_half = lax.ppermute(after_half, "mlp", pair)
+        add_chips, [((row_count, half), BF16, True)], [], [base, got, *others], [fetched]
+    )
+    other_half = partner(after_half, 1)
     shard_after, next_qkv = call(
         project_next,
         [((row_count, part_width), BF16, False), ((row_count, qkv_weight.shape[1]), BF16, False)],
-        [mlp_place.astype(jnp.int32).reshape(1)],
+        [place],
         [after_half, other_half, next_gain.reshape(1, width), qkv_front],
         [qkv_weight],
         [((row_count, width), F32), ((width - near_rows, qkv_weight.shape[1]), BF16)],

time: 110 us -> 106 us (0.964)
  starting transfers between devices: 39.8 us -> 43.9 us
  waiting for transfers between devices: 37.3 us -> 33.8 us
  local copies, waits for them, and re-layouts: 4.49 us -> 1.52 us
  Pallas kernels: 23.5 us -> 21.1 us
    ppermute x5 -> x12, starting transfers between devices: 5.95 us -> 14.3 us  [partner(): return lax.ppermute(block, 'mlp', [(i, i ^ distance) for i in range(count)])]
    all_to_all x4 -> x3, starting transfers between devices: 33.9 us -> 29.6 us  [exchange(): return lax.all_to_all(copies, axis, split_axis=0, concat_axis=0, tiled=True)]
    all_to_all x4 -> x3, waiting for transfers between devices: 33.6 us -> 29.6 us  [exchange(): return lax.all_to_all(copies, axis, split_axis=0, concat_axis=0, tiled=True)]
    unnamed x20 -> x12, local copies, waits for them, and re-layouts: 3 us -> 0.03 us
    pallas_call x9 -> x8, Pallas kernels: 16.3 us -> 13.4 us  [call(): pl.pallas_call(body, out_shape=[pltpu.VMEM(shape, dtype) if stays else ja...]
    pallas_call x0 -> x1, Pallas kernels: none -> 1.68 us  [shards(): pl.pallas_call(send_queries, out_shape=jax.ShapeDtypeStruct((seq_count, q...]
    pallas_call x4 -> x3, Pallas kernels: 7.29 us -> 6 us  [fetch(): pl.pallas_call(fetch_rows, out_shape=[pltpu.VMEM((rows,) + far.shape[1:],...]
    ppermute x5 -> x12, waiting for transfers between devices: 3.63 us -> 4.2 us  [partner(): return lax.ppermute(block, 'mlp', [(i, i ^ distance) for i in range(count)])]
  transfers between devices with their start and end apart: 9 -> 15, of which waited for: 7 -> 7; matrix products, arithmetic and copies ran while one was open for 3% -> 3% of each run, Pallas kernels for 7% -> 6%
where the time goes in v4:
time: 106 us; the launch traced here: 105 us
  starting transfers between devices  43.9 us (41%)
  waiting for transfers between devices  33.8 us (32%)
  Pallas kernels  21.1 us (20%)
  between operations  2.81 us (3%)
  other arithmetic  1.72 us (2%)
  local copies, waits for them, and re-layouts  1.52 us (1%)
    all_to_all x3, starting transfers between devices, exchange(): return lax.all_to_all(copies, axis, split_axis=0, concat_axis=0, tiled=True)  29.6 us
    all_to_all x3, waiting for transfers between devices, exchange(): return lax.all_to_all(copies, axis, split_axis=0, concat_axis=0, tiled=True)  29.6 us
    ppermute x12, starting transfers between devices, partner(): return lax.ppermute(block, 'mlp', [(i, i ^ distance) for i in range(count)])  14.3 us
    pallas_call x8, Pallas kernels, call(): pl.pallas_call(body, out_shape=[pltpu.VMEM(shape, dtype) if stays else ja...  13.4 us
    pallas_call x3, Pallas kernels, fetch(): pl.pallas_call(fetch_rows, out_shape=[pltpu.VMEM((rows,) + far.shape[1:],...  6 us
    ppermute x12, waiting for transfers between devices, partner(): return lax.ppermute(block, 'mlp', [(i, i ^ distance) for i in range(count)])  4.2 us
  transfers between devices with their start and end apart: 15, of which 7 were waited for; matrix products, arithmetic and copies ran while one was open for 3% of the time, Pallas kernels for 6%

profile of v4, /device:TPU:1, one launch (start us, length us, event | category | flops | bytes accessed | tf_op | source)
XLA Modules:
  0.0 104.9 jit_solution(10596382031767744853)
XLA Ops:
  0.6 0.0 copy-start
  0.6 1.7 %send_queries.1.refs_0_ = bf16[32,40,256]{2,1,0:T(8,128)(2,1)} custom-call(bf16[4,2560]{1,0:T(4,128)(2,1)} %queries_ref.3), custom_call_target="tpu_custom_call" | custom-call | tf_op jit(solution)/shard_map/send_queries/pallas_call | solution.py:403
  2.3 11.9 %all-to-all-start = ((bf16[32,40,256]{2,1,0:T(8,128)(2,1)}), bf16[32,40,256]{2,1,0:T(8,128)(2,1)S(1)}, u32[]{:S(2)}, u32[]{:S(2)}) async-start(bf16[32,40,256]{2,1,0:T(8,128)(2,1)} %send_queries.1.refs_0_), calls=%async_computation | async-start | bytes 1310720 | tf_op jit(solution)/shard_map/all_to_all | solution.py:360
  14.2 0.8 reshape.59
  15.0 2.0 %fetch_rows.3 = (bf16[11,128,512]{2,1,0:T(8,128)(2,1)S(1)}, f32[8,128]{1,0:T(8,128)}) custom-call(bf16[32,40,256]{2,1,0:T(8,128)(2,1)} %send_queries.1.refs_0_, bf16[17,128,512]{2,1,0:T(8,128)(2,1)} %far_ref.1), custom_call_target="tpu_custom_call" | custom-call | tf_op jit(solution)/shard_map/fetch_rows/pallas_call | solution.py:348
  16.9 0.7 dynamic-slice_reduce_fusion.length_ref
  17.7 0.1 add_add_fusion
  17.8 1.0 select_reduce_fusion.code_ref
  18.8 11.8 %all-to-all-done.rows_ref = bf16[32,40,256]{2,1,0:T(8,128)(2,1)S(1)} async-done(((bf16[32,40,256]{2,1,0:T(8,128)(2,1)}), bf16[32,40,256]{2,1,0:T(8,128)(2,1)S(1)}, u32[]{:S(2)}, u32[]{:S(2)}) %all-to-all-start) | async-done | bytes 655392 | tf_op jit(solution)/shard_map/all_to_all | solution.py:360
  30.6 3.9 %attend_pages.1.refs_0_ = bf16[32,4,2688]{2,1,0:T(4,128)(2,1)} custom-call(s32[17]{0:T(128)} %select_reduce_fusion.code_ref, s32[32]{0:T(128)} %dynamic-slice_reduce_fusion.length_ref, bf16[32,40,256]{2,1,0:T(8,128)(2,1)S(1)} %all-to-all-done.rows_ref, bf16[11,128,512]{2,1,0:T(8,128)(2,1)S(1)} %get-tuple-element.20.front_ref, bf16[17,128,512]{2,1,0:T(8,128)(2,1)} %far_ref.1), custom_call_target="tpu_custom_call" | custom-call | tf_op jit(solution)/shard_map/attend_pages/pallas_call | solution.py:323
  34.5 8.4 %all-to-all-start.1 = ((bf16[32,4,2688]{2,1,0:T(4,128)(2,1)}), bf16[32,4,2688]{2,1,0:T(4,128)(2,1)S(1)}, u32[]{:S(2)}, u32[]{:S(2)}) async-start(bf16[32,4,2688]{2,1,0:T(4,128)(2,1)} %attend_pages.1.refs_0_), calls=%async_computation.1 | async-start | bytes 1376256 | tf_op jit(solution)/shard_map/all_to_all | solution.py:360
  42.9 0.6 fusion
  45.5 0.3 attend_new.1
  45.9 14.3 %all-to-all-done.1.refs_0_ = bf16[32,4,2688]{2,1,0:T(4,128)(2,1)S(1)} async-done(((bf16[32,4,2688]{2,1,0:T(4,128)(2,1)}), bf16[32,4,2688]{2,1,0:T(4,128)(2,1)S(1)}, u32[]{:S(2)}, u32[]{:S(2)}) %all-to-all-start.1) | async-done | bytes 688160 | tf_op jit(solution)/shard_map/all_to_all | solution.py:360
  60.2 0.9 merge_new.1
  61.1 9.4 %all-to-all-start.2 = ((bf16[8,4,2560]{2,1,0:T(4,128)(2,1)}), bf16[8,4,2560]{2,1,0:T(4,128)(2,1)S(1)}, u32[]{:S(2)}, u32[]{:S(2)}) async-start(bf16[8,4,2560]{2,1,0:T(4,128)(2,1)} %get-tuple-element.25), calls=%async_computation.2 | async-start | bytes 327680 | tf_op jit(solution)/shard_map/all_to_all | solution.py:360
  70.5 2.2 %fetch_rows.4 = (bf16[128,2560]{1,0:T(8,128)(2,1)S(1)}, bf16[96,2560]{1,0:T(8,128)(2,1)S(1)}, bf16[96,2560]{1,0:T(8,128)(2,1)S(1)}, bf16[96,2560]{1,0:T(8,128)(2,1)S(1)}, f32[8,128]{1,0:T(8,128)}) custom-call(bf16[32,4,2688]{2,1,0:T(4,128)(2,1)} %attend_pages.1.refs_0_, bf16[320,2560]{1,0:T(8,128)(2,1)} %bitcast.13, bf16[480,2560]{1,0:T(8,128)(2,1)} %bitcast.9, ...), custom_call_target="tpu_custom_call" | custom-call | tf_op jit(solution)/shard_map/fetch_rows/pallas_call | solution.py:348
  72.6 0.0 copy-start.4
  72.6 3.4 %all-to-all-done.2.rows_ref = bf16[8,4,2560]{2,1,0:T(4,128)(2,1)S(1)} async-done(((bf16[8,4,2560]{2,1,0:T(4,128)(2,1)}), bf16[8,4,2560]{2,1,0:T(4,128)(2,1)S(1)}, u32[]{:S(2)}, u32[]{:S(2)}) %all-to-all-start.2) | async-done | bytes 163872 | tf_op jit(solution)/shard_map/all_to_all | solution.py:360
  76.0 1.8 %project_out.1.refs_0_ = bf16[32,320]{1,0:T(8,128)(2,1)S(1)} custom-call(bf16[8,4,2560]{2,1,0:T(4,128)(2,1)S(1)} %all-to-all-done.2.rows_ref, bf16[32,320]{1,0:T(8,128)(2,1)S(1)} %copy-done.2, bf16[128,2560]{1,0:T(8,128)(2,1)S(1)} %get-tuple-element.26.front_ref, bf16[320,2560]{1,0:T(8,128)(2,1)} %bitcast.14), custom_call_target="tpu_custom_call" | custom-call | tf_op jit(solution)/shard_map/project_out/pallas_call | solution.py:323
  77.9 0.4 collective-permute-start.1
  78.2 1.8 %collective-permute-start.3 = (bf16[32,320]{1,0:T(8,128)(2,1)S(1)}, bf16[32,320]{1,0:T(8,128)(2,1)S(1)}, u32[]{:S(2)}, u32[]{:S(2)}) collective-permute-start(bf16[32,320]{1,0:T(8,128)(2,1)S(1)} %project_out.1.refs_0_), channel_id=1, source_target_pairs={{0,4},{1,5},{2,6},{3,7},{4,0},{5,1},{6,2},{7,3},{8,12},{9,13},{10,... | collective-permute-start | bytes 61448 | tf_op jit(solution)/shard_map/ppermute | solution.py:365
  80.0 1.8 %collective-permute-start.5 = (bf16[32,320]{1,0:T(8,128)(2,1)S(1)}, bf16[32,320]{1,0:T(8,128)(2,1)S(1)}, u32[]{:S(2)}, u32[]{:S(2)}) collective-permute-start(bf16[32,320]{1,0:T(8,128)(2,1)S(1)} %project_out.1.refs_0_), channel_id=1, source_target_pairs={{0,6},{1,7},{2,4},{3,5},{4,2},{5,3},{6,0},{7,1},{8,14},{9,15},{10,... | collective-permute-start | bytes 61448 | tf_op jit(solution)/shard_map/ppermute | solution.py:365
  81.8 1.7 %collective-permute-start = (bf16[32,320]{1,0:T(8,128)(2,1)S(1)}, bf16[32,320]{1,0:T(8,128)(2,1)S(1)}, u32[]{:S(2)}, u32[]{:S(2)}) collective-permute-start(bf16[32,320]{1,0:T(8,128)(2,1)S(1)} %project_out.1.refs_0_), channel_id=1, source_target_pairs={{0,1},{1,0},{2,3},{3,2},{4,5},{5,4},{6,7},{7,6},{8,9},{9,8},{10,11... | collective-permute-start | bytes 61448 | tf_op jit(solution)/shard_map/ppermute | solution.py:365
  83.6 0.0 collective-permute-done.1.refs_2_
  83.6 0.0 collective-permute-start.2
  83.6 0.0 collective-permute-done.3.refs_4_
  83.6 1.3 %collective-permute-start.4 = (bf16[32,320]{1,0:T(8,128)(2,1)S(1)}, bf16[32,320]{1,0:T(8,128)(2,1)S(1)}, u32[]{:S(2)}, u32[]{:S(2)}) collective-permute-start(bf16[32,320]{1,0:T(8,128)(2,1)S(1)} %collective-permute-done.3.refs_4_), channel_id=1, source_target_pairs={{0,1},{1,0},{2,3},{3,2},{4,5},{5,4},{6,7},{7,6},{8,9},{9,8},{10,11... | collective-permute-start | bytes 61448 | tf_op jit(solution)/shard_map/ppermute | solution.py:365
  84.9 0.0 collective-permute-done.5.refs_6_
  84.9 1.7 %collective-permute-start.6 = (bf16[32,320]{1,0:T(8,128)(2,1)S(1)}, bf16[32,320]{1,0:T(8,128)(2,1)S(1)}, u32[]{:S(2)}, u32[]{:S(2)}) collective-permute-start(bf16[32,320]{1,0:T(8,128)(2,1)S(1)} %collective-permute-done.5.refs_6_), channel_id=1, source_target_pairs={{0,1},{1,0},{2,3},{3,2},{4,5},{5,4},{6,7},{7,6},{8,9},{9,8},{10,11... | collective-permute-start | bytes 61448 | tf_op jit(solution)/shard_map/ppermute | solution.py:365
  86.5 0.0 collective-permute-done.refs_1_
  86.6 0.0 collective-permute-done.2.refs_3_
  86.6 0.0 collective-permute-done.4.refs_5_
  86.6 0.8 collective-permute-done.6.refs_7_
  87.4 4.3 %feed_forward.1 = (f32[32,1280]{1,0:T(8,128)S(1)}, bf16[32,1280]{1,0:T(8,128)(2,1)S(1)}, f32[32,1280]{1,0:T(8,128)S(1)}) custom-call(s32[1]{0:T(128)} %bitcast.3.place_ref, bf16[32,320]{1,0:T(8,128)(2,1)S(1)} %project_out.1.refs_0_, bf16[32,320]{1,0:T(8,128)(2,1)S(1)} %collective-permute-done.refs_1_, bf16[32,320]{1,0:T(8,128)(2,1)S(1)} %collective-permute-done.1.refs_2_, ...), custom_call_target="tpu_custom_call" | custom-call | tf_op jit(solution)/shard_map/feed_forward/pallas_call | solution.py:323
  91.7 0.0 copy-start.5
  91.7 0.4 collective-permute-start.7
  92.1 0.9 collective-permute-done.7.got_ref
  93.1 0.1 collective-permute-start.8
  93.2 1.9 %collective-permute-start.9 = (bf16[32,1280]{1,0:T(8,128)(2,1)S(1)}, bf16[32,1280]{1,0:T(8,128)(2,1)S(1)}, u32[]{:S(2)}, u32[]{:S(2)}) collective-permute-start(bf16[32,1280]{1,0:T(8,128)(2,1)S(1)} %add_pair.1), channel_id=1, source_target_pairs={{0,6},{1,7},{2,4},{3,5},{4,2},{5,3},{6,0},{7,1},{8,14},{9,15},{10,... | collective-permute-start | bytes 245768 | tf_op jit(solution)/shard_map/ppermute | solution.py:365
  95.1 1.4 %collective-permute-start.10 = (bf16[32,1280]{1,0:T(8,128)(2,1)S(1)}, bf16[32,1280]{1,0:T(8,128)(2,1)S(1)}, u32[]{:S(2)}, u32[]{:S(2)}) collective-permute-start(bf16[32,1280]{1,0:T(8,128)(2,1)S(1)} %add_pair.1), channel_id=1, source_target_pairs={{0,4},{1,5},{2,6},{3,7},{4,0},{5,1},{6,2},{7,3},{8,12},{9,13},{10,... | collective-permute-start | bytes 245768 | tf_op jit(solution)/shard_map/ppermute | solution.py:365
  96.4 1.9 %fetch_rows.5 = (bf16[1536,384]{1,0:T(8,128)(2,1)S(1)}, f32[8,128]{1,0:T(8,128)}) custom-call(bf16[32,4,2688]{2,1,0:T(4,128)(2,1)} %attend_pages.1.refs_0_, bf16[2560,384]{1,0:T(8,128)(2,1)} %weight_far.1), custom_call_target="tpu_custom_call" | custom-call | tf_op jit(solution)/shard_map/fetch_rows/pallas_call | solution.py:348
  98.3 0.0 collective-permute-done.8.first_ref
  98.3 1.5 %collective-permute-done.10.third_ref = bf16[32,1280]{1,0:T(8,128)(2,1)S(1)} collective-permute-done((bf16[32,1280]{1,0:T(8,128)(2,1)S(1)}, bf16[32,1280]{1,0:T(8,128)(2,1)S(1)}, u32[]{:S(2)}, u32[]{:S(2)}) %collective-permute-start.10) | collective-permute-done | bytes 81952 | tf_op jit(solution)/shard_map/ppermute | solution.py:365
  99.9 0.1 add_chips.1.own_ref
  99.9 1.9 %collective-permute-start.11 = (bf16[32,1280]{1,0:T(8,128)(2,1)S(1)}, bf16[32,1280]{1,0:T(8,128)(2,1)S(1)}, u32[]{:S(2)}, u32[]{:S(2)}) collective-permute-start(bf16[32,1280]{1,0:T(8,128)(2,1)S(1)} %add_chips.1.own_ref), channel_id=1, source_target_pairs={{0,1},{1,0},{2,3},{3,2},{4,5},{5,4},{6,7},{7,6},{8,9},{9,8},{10,11... | collective-permute-start | bytes 245768 | tf_op jit(solution)/shard_map/ppermute | solution.py:365
  101.8 0.9 collective-permute-done.11.other_ref
  102.7 2.2 %project_next.1 = (bf16[32,320]{1,0:T(8,128)(2,1)}, bf16[32,384]{1,0:T(8,128)(2,1)}) custom-call(s32[1]{0:T(128)} %bitcast.3.place_ref, bf16[32,1280]{1,0:T(8,128)(2,1)S(1)} %add_chips.1.own_ref, bf16[32,1280]{1,0:T(8,128)(2,1)S(1)} %collective-permute-done.11.other_ref, f32[1,2560]{1,0:T(1,128)S(1)} %reshape.62.gain_ref, ...), custom_call_target="tpu_custom_call" | custom-call | tf_op jit(solution)/shard_map/project_next/pallas_call | solution.py:323
  (16 shorter events, 0.1 us)
Async XLA Ops:
  0.6 17.0 %copy-start = (s32[256,128]{1,0:T(8,128)S(1)}, s32[256,128]{1,0:T(8,128)}, u32[]{:S(2)}) copy-start(s32[256,128]{1,0:T(8,128)} %param.17) | copy-start | bytes 393220
  2.3 28.3 %all-to-all-start = ((bf16[32,40,256]{2,1,0:T(8,128)(2,1)}), bf16[32,40,256]{2,1,0:T(8,128)(2,1)S(1)}, u32[]{:S(2)}, u32[]{:S(2)}) async-start(bf16[32,40,256]{2,1,0:T(8,128)(2,1)} %send_queries.1.refs_0_), calls=%async_computation | async-start | bytes 1310720 | tf_op jit(solution)/shard_map/all_to_all | solution.py:360
  30.6 14.9 %copy-start.1 = (bf16[4,2560]{1,0:T(4,128)(2,1)S(1)}, bf16[4,2560]{1,0:T(4,128)(2,1)}, u32[]{:S(2)}) copy-start(bf16[4,2560]{1,0:T(4,128)(2,1)} %queries_ref.3) | copy-start | bytes 61444
  30.6 14.9 %copy-start.3 = (bf16[4,512]{1,0:T(4,128)(2,1)S(1)}, bf16[4,512]{1,0:T(4,128)(2,1)}, u32[]{:S(2)}) copy-start(bf16[4,512]{1,0:T(4,128)(2,1)} %new_ref.1) | copy-start | bytes 12292
  34.5 25.7 %all-to-all-start.1 = ((bf16[32,4,2688]{2,1,0:T(4,128)(2,1)}), bf16[32,4,2688]{2,1,0:T(4,128)(2,1)S(1)}, u32[]{:S(2)}, u32[]{:S(2)}) async-start(bf16[32,4,2688]{2,1,0:T(4,128)(2,1)} %attend_pages.1.refs_0_), calls=%async_computation.1 | async-start | bytes 1376256 | tf_op jit(solution)/shard_map/all_to_all | solution.py:360
  61.1 15.0 %all-to-all-start.2 = ((bf16[8,4,2560]{2,1,0:T(4,128)(2,1)}), bf16[8,4,2560]{2,1,0:T(4,128)(2,1)S(1)}, u32[]{:S(2)}, u32[]{:S(2)}) async-start(bf16[8,4,2560]{2,1,0:T(4,128)(2,1)} %get-tuple-element.25), calls=%async_computation.2 | async-start | bytes 327680 | tf_op jit(solution)/shard_map/all_to_all | solution.py:360
  70.5 5.6 %copy-start.2 = (bf16[32,320]{1,0:T(8,128)(2,1)S(1)}, bf16[32,320]{1,0:T(8,128)(2,1)}, u32[]{:S(2)}) copy-start(bf16[32,320]{1,0:T(8,128)(2,1)} %residual_ref.1) | copy-start | bytes 61444
  72.6 13.9 %copy-start.4 = (f32[2560]{0:T(1024)S(1)}, f32[2560]{0:T(1024)}, u32[]{:S(2)}) copy-start(f32[2560]{0:T(1024)} %param.20) | copy-start | bytes 30724
  77.9 5.7 %collective-permute-start.1 = (bf16[32,320]{1,0:T(8,128)(2,1)S(1)}, bf16[32,320]{1,0:T(8,128)(2,1)S(1)}, u32[]{:S(2)}, u32[]{:S(2)}) collective-permute-start(bf16[32,320]{1,0:T(8,128)(2,1)S(1)} %project_out.1.refs_0_), channel_id=1, source_target_pairs={{0,2},{1,3},{2,0},{3,1},{4,6},{5,7},{6,4},{7,5},{8,10},{9,11},{10,... | collective-permute-start | bytes 61448 | tf_op jit(solution)/shard_map/ppermute | solution.py:365
  78.2 5.3 %collective-permute-start.3 = (bf16[32,320]{1,0:T(8,128)(2,1)S(1)}, bf16[32,320]{1,0:T(8,128)(2,1)S(1)}, u32[]{:S(2)}, u32[]{:S(2)}) collective-permute-start(bf16[32,320]{1,0:T(8,128)(2,1)S(1)} %project_out.1.refs_0_), channel_id=1, source_target_pairs={{0,4},{1,5},{2,6},{3,7},{4,0},{5,1},{6,2},{7,3},{8,12},{9,13},{10,... | collective-permute-start | bytes 61448 | tf_op jit(solution)/shard_map/ppermute | solution.py:365
  80.0 4.8 %collective-permute-start.5 = (bf16[32,320]{1,0:T(8,128)(2,1)S(1)}, bf16[32,320]{1,0:T(8,128)(2,1)S(1)}, u32[]{:S(2)}, u32[]{:S(2)}) collective-permute-start(bf16[32,320]{1,0:T(8,128)(2,1)S(1)} %project_out.1.refs_0_), channel_id=1, source_target_pairs={{0,6},{1,7},{2,4},{3,5},{4,2},{5,3},{6,0},{7,1},{8,14},{9,15},{10,... | collective-permute-start | bytes 61448 | tf_op jit(solution)/shard_map/ppermute | solution.py:365
  81.8 4.7 %collective-permute-start = (bf16[32,320]{1,0:T(8,128)(2,1)S(1)}, bf16[32,320]{1,0:T(8,128)(2,1)S(1)}, u32[]{:S(2)}, u32[]{:S(2)}) collective-permute-start(bf16[32,320]{1,0:T(8,128)(2,1)S(1)} %project_out.1.refs_0_), channel_id=1, source_target_pairs={{0,1},{1,0},{2,3},{3,2},{4,5},{5,4},{6,7},{7,6},{8,9},{9,8},{10,11... | collective-permute-start | bytes 61448 | tf_op jit(solution)/shard_map/ppermute | solution.py:365
  83.6 3.0 %collective-permute-start.2 = (bf16[32,320]{1,0:T(8,128)(2,1)S(1)}, bf16[32,320]{1,0:T(8,128)(2,1)S(1)}, u32[]{:S(2)}, u32[]{:S(2)}) collective-permute-start(bf16[32,320]{1,0:T(8,128)(2,1)S(1)} %collective-permute-done.1.refs_2_), channel_id=1, source_target_pairs={{0,1},{1,0},{2,3},{3,2},{4,5},{5,4},{6,7},{7,6},{8,9},{9,8},{10,11... | collective-permute-start | bytes 61448 | tf_op jit(solution)/shard_map/ppermute | solution.py:365
  83.6 3.0 %collective-permute-start.4 = (bf16[32,320]{1,0:T(8,128)(2,1)S(1)}, bf16[32,320]{1,0:T(8,128)(2,1)S(1)}, u32[]{:S(2)}, u32[]{:S(2)}) collective-permute-start(bf16[32,320]{1,0:T(8,128)(2,1)S(1)} %collective-permute-done.3.refs_4_), channel_id=1, source_target_pairs={{0,1},{1,0},{2,3},{3,2},{4,5},{5,4},{6,7},{7,6},{8,9},{9,8},{10,11... | collective-permute-start | bytes 61448 | tf_op jit(solution)/shard_map/ppermute | solution.py:365
  84.9 2.5 %collective-permute-start.6 = (bf16[32,320]{1,0:T(8,128)(2,1)S(1)}, bf16[32,320]{1,0:T(8,128)(2,1)S(1)}, u32[]{:S(2)}, u32[]{:S(2)}) collective-permute-start(bf16[32,320]{1,0:T(8,128)(2,1)S(1)} %collective-permute-done.5.refs_6_), channel_id=1, source_target_pairs={{0,1},{1,0},{2,3},{3,2},{4,5},{5,4},{6,7},{7,6},{8,9},{9,8},{10,11... | collective-permute-start | bytes 61448 | tf_op jit(solution)/shard_map/ppermute | solution.py:365
  91.7 10.1 %copy-start.5 = (f32[2560]{0:T(1024)S(1)}, f32[2560]{0:T(1024)}, u32[]{:S(2)}) copy-start(f32[2560]{0:T(1024)} %param.24) | copy-start | bytes 30724
  91.7 1.4 %collective-permute-start.7 = (bf16[32,1280]{1,0:T(8,128)(2,1)S(1)}, bf16[32,1280]{1,0:T(8,128)(2,1)S(1)}, u32[]{:S(2)}, u32[]{:S(2)}) collective-permute-start(bf16[32,1280]{1,0:T(8,128)(2,1)S(1)} %get-tuple-element.31), channel_id=1, source_target_pairs={{0,1},{1,0},{2,3},{3,2},{4,5},{5,4},{6,7},{7,6},{8,9},{9,8},{10,11... | collective-permute-start | bytes 245768 | tf_op jit(solution)/shard_map/ppermute | solution.py:365
  93.1 5.2 %collective-permute-start.8 = (bf16[32,1280]{1,0:T(8,128)(2,1)S(1)}, bf16[32,1280]{1,0:T(8,128)(2,1)S(1)}, u32[]{:S(2)}, u32[]{:S(2)}) collective-permute-start(bf16[32,1280]{1,0:T(8,128)(2,1)S(1)} %add_pair.1), channel_id=1, source_target_pairs={{0,2},{1,3},{2,0},{3,1},{4,6},{5,7},{6,4},{7,5},{8,10},{9,11},{10,... | collective-permute-start | bytes 245768 | tf_op jit(solution)/shard_map/ppermute | solution.py:365
  93.2 5.1 %collective-permute-start.9 = (bf16[32,1280]{1,0:T(8,128)(2,1)S(1)}, bf16[32,1280]{1,0:T(8,128)(2,1)S(1)}, u32[]{:S(2)}, u32[]{:S(2)}) collective-permute-start(bf16[32,1280]{1,0:T(8,128)(2,1)S(1)} %add_pair.1), channel_id=1, source_target_pairs={{0,6},{1,7},{2,4},{3,5},{4,2},{5,3},{6,0},{7,1},{8,14},{9,15},{10,... | collective-permute-start | bytes 245768 | tf_op jit(solution)/shard_map/ppermute | solution.py:365
  95.1 4.8 %collective-permute-start.10 = (bf16[32,1280]{1,0:T(8,128)(2,1)S(1)}, bf16[32,1280]{1,0:T(8,128)(2,1)S(1)}, u32[]{:S(2)}, u32[]{:S(2)}) collective-permute-start(bf16[32,1280]{1,0:T(8,128)(2,1)S(1)} %add_pair.1), channel_id=1, source_target_pairs={{0,4},{1,5},{2,6},{3,7},{4,0},{5,1},{6,2},{7,3},{8,12},{9,13},{10,... | collective-permute-start | bytes 245768 | tf_op jit(solution)/shard_map/ppermute | solution.py:365
  99.9 2.8 %collective-permute-start.11 = (bf16[32,1280]{1,0:T(8,128)(2,1)S(1)}, bf16[32,1280]{1,0:T(8,128)(2,1)S(1)}, u32[]{:S(2)}, u32[]{:S(2)}) collective-permute-start(bf16[32,1280]{1,0:T(8,128)(2,1)S(1)} %add_chips.1.own_ref), channel_id=1, source_target_pairs={{0,1},{1,0},{2,3},{3,2},{4,5},{5,4},{6,7},{7,6},{8,9},{9,8},{10,11... | collective-permute-start | bytes 245768 | tf_op jit(solution)/shard_map/ppermute | solution.py:365

commit v5 on v4

--- a/solution.py
+++ b/solution.py
@@ -1,5 +1,3 @@
-import functools
-
 import jax
 import jax.numpy as jnp
 from jax import lax
@@ -30,10 +28,10 @@
     return placed
 
 
-def send_queries(queries_ref, out_ref):
-    rows = head_major(queries_ref[...].astype(F32), out_ref.shape[2]).astype(BF16)
+def copy_queries(queries_ref, out_ref):
+    queries = queries_ref[...]
     for place in range(out_ref.shape[0]):
-        out_ref[place] = rows
+        out_ref[place] = queries
 
 
 def attend_new(queries_ref, new_ref, max_ref, sum_ref, acc_ref):
@@ -79,7 +77,7 @@
     head_dim = kv_width // 2
     token_count = out_ref.shape[1]
     width = out_ref.shape[2] - 128
-    query_rows = rows_ref.shape[1]
+    query_rows = token_count * (width // head_dim)
     head_count = width // head_dim
     page_count = 128
     scale = head_dim ** (-0.5)
@@ -102,7 +100,9 @@
         reach = jnp.where(codes[slot] > 0, length_ref[sources[slot]], 0) - page * page_len
         scores = (
             lax.dot_general(
-                rows_ref[sources[slot]], cached(slot, slice(0, head_dim)), LAST, preferred_element_type=F32
+                head_major(rows_ref[sources[slot]].astype(F32), head_dim).astype(BF16),
+                cached(slot, slice(0, head_dim)),
+                LAST, preferred_element_type=F32
             )
             * scale
         )
@@ -148,36 +148,28 @@
         out_ref[source, :, width:] = packed.astype(BF16)
 
 
-def merge_new(holder_ref, *refs, splits):
-    got_refs = refs[: len(splits)]
-    max_ref, sum_ref, acc_ref, attended_ref, spread_ref = refs[len(splits) :]
+def merge_new(holder_ref, got_ref, max_ref, sum_ref, acc_ref, attended_ref, spread_ref):
     holder = holder_ref[0]
     head_dim = 256
-    for (first_head, last_head), got_ref in zip(splits, got_refs):
-        width = got_ref.shape[2] - 128
-        packed = got_ref[holder, :, width:].astype(F32)
-        cached = packed + pltpu.roll(packed, 128 - 16, 1) + pltpu.roll(packed, 128 - 32, 1)
-        new_max = max_ref[...]
-        new_sum = sum_ref[...]
-        if first_head:
-            new_max = pltpu.roll(new_max, 128 - first_head, 1)
-            new_sum = pltpu.roll(new_sum, 128 - first_head, 1)
-        peak = jnp.maximum(cached, new_max)
-        cached_factor = jnp.exp(cached - peak)
-        new_factor = jnp.exp(new_max - peak)
-        inverse = 1.0 / (cached_factor + new_factor * new_sum)
-        cached_factor = cached_factor * inverse
-        new_factor = new_factor * inverse
-        for head in range(last_head - first_head):
-            whole = slice((first_head + head) * head_dim, (first_head + head + 1) * head_dim)
-            rows = (
-                got_ref[holder, :, head * head_dim : (head + 1) * head_dim].astype(F32)
-                * cached_factor[:, head : head + 1]
-                + acc_ref[:, whole] * new_factor[:, head : head + 1]
-            ).astype(BF16)
-            attended_ref[:, whole] = rows
-            for place in range(spread_ref.shape[0]):
-                spread_ref[place, :, whole] = rows
+    width = attended_ref.shape[1]
+    packed = got_ref[holder, :, width:].astype(F32)
+    cached = packed + pltpu.roll(packed, 128 - 16, 1) + pltpu.roll(packed, 128 - 32, 1)
+    new_max = max_ref[...]
+    peak = jnp.maximum(cached, new_max)
+    cached_factor = jnp.exp(cached - peak)
+    new_factor = jnp.exp(new_max - peak)
+    inverse = 1.0 / (cached_factor + new_factor * sum_ref[...])
+    cached_factor = cached_factor * inverse
+    new_factor = new_factor * inverse
+    for head in range(width // head_dim):
+        span = slice(head * head_dim, (head + 1) * head_dim)
+        rows = (
+            got_ref[holder, :, span].astype(F32) * cached_factor[:, head : head + 1]
+            + acc_ref[:, span] * new_factor[:, head : head + 1]
+        ).astype(BF16)
+        attended_ref[:, span] = rows
+        for place in range(spread_ref.shape[0]):
+            spread_ref[place, :, span] = rows
 
 
 def project_out(rows_ref, residual_ref, front_ref, weight_far, out_ref, rest_ref, copied):
@@ -202,7 +194,7 @@
     total = parts * width
     half = total // 2
     near_rows = gate_ref.shape[0]
-    chunks = 2
+    chunks = copied.shape[0] // 3
     step = gate_rest.shape[0] // chunks
     copies = []
     for chunk in range(chunks):
@@ -260,51 +252,73 @@
     out_ref[...] = total.astype(BF16)
 
 
-def project_next(
+def fetch_half(place_ref, far_ref, out_ref, token_ref, copied):
+    half = out_ref.shape[0]
+    copy = pltpu.make_async_copy(
+        far_ref.at[pl.ds(pl.multiple_of(place_ref[0] % 2 * half, 128), half)], out_ref, copied.at[0]
+    )
+    copy.start()
+    token_ref[...] = jnp.zeros(token_ref.shape, F32)
+    copy.wait()
+
+
+def project_own(place_ref, own_ref, gain_ref, weight_ref, far_ref, acc_ref, square_ref, other_weight_ref, copied):
+    half = own_ref.shape[1]
+    core = place_ref[0] % 2
+    near_rows = other_weight_ref.shape[0]
+    copy = pltpu.make_async_copy(
+        far_ref.at[pl.ds(pl.multiple_of((1 - core) * half, 128), near_rows)],
+        other_weight_ref,
+        copied.at[0],
+    )
+    copy.start()
+    own = own_ref[...].astype(F32)
+    square_ref[...] = jnp.broadcast_to(jnp.sum(own * own, axis=1, keepdims=True), square_ref.shape)
+    scaled = (own * gain_ref[core]).astype(BF16)
+    acc_ref[...] = jnp.dot(scaled, weight_ref[...], preferred_element_type=F32)
+    copy.wait()
+
+
+def project_other(
     place_ref,
     own_ref,
     other_ref,
     gain_ref,
+    acc_ref,
+    square_ref,
     front_ref,
-    weight_far,
+    far_ref,
     shard_ref,
     out_ref,
-    whole_ref,
     rest_ref,
     copied,
 ):
-    rows, half = own_ref.shape
+    half = own_ref.shape[1]
+    core = place_ref[0] % 2
     near_rows = front_ref.shape[0]
-    rest = pltpu.make_async_copy(
-        weight_far.at[pl.ds(near_rows, rest_ref.shape[0])], rest_ref, copied.at[0]
-    )
-    rest.start()
-    core = place_ref[0] % 2
-
-    @pl.when(core == 0)
-    def _():
-        whole_ref[:, :half] = own_ref[...].astype(F32)
-        whole_ref[:, half:] = other_ref[...].astype(F32)
-
-    @pl.when(core == 1)
-    def _():
-        whole_ref[:, half:] = own_ref[...].astype(F32)
-        whole_ref[:, :half] = other_ref[...].astype(F32)
-
+    copy = pltpu.make_async_copy(
+        far_ref.at[pl.ds(pl.multiple_of((1 - core) * half + near_rows, 128), half - near_rows)],
+        rest_ref,
+        copied.at[0],
+    )
+    copy.start()
     part = shard_ref.shape[1]
-    for place in range(2 * half // part):
+    parts = half // part
+    for place in range(2 * parts):
+        from_ref = own_ref if place // parts == place % 2 else other_ref
+        column = place % parts * part
 
         @pl.when(place_ref[0] == place)
         def _():
-            shard_ref[...] = whole_ref[:, place * part : (place + 1) * part].astype(BF16)
-
-    whole = whole_ref[...]
-    square = jnp.sum(whole * whole, axis=1, keepdims=True)
-    normed = (whole * lax.rsqrt(square / (2 * half) + 1e-06) * gain_ref[...]).astype(BF16)
-    front = jnp.dot(normed[:, :near_rows], front_ref[...], preferred_element_type=F32)
-    rest.wait()
-    back = jnp.dot(normed[:, near_rows:], rest_ref[...], preferred_element_type=F32)
-    out_ref[...] = (front + back).astype(BF16)
+            shard_ref[...] = from_ref[:, column : column + part]
+
+    other = other_ref[...].astype(F32)
+    square = square_ref[:, :1] + jnp.sum(other * other, axis=1, keepdims=True)
+    scaled = (other * gain_ref[1 - core]).astype(BF16)
+    acc = acc_ref[...] + jnp.dot(scaled[:, :near_rows], front_ref[...], preferred_element_type=F32)
+    copy.wait()
+    acc = acc + jnp.dot(scaled[:, near_rows:], rest_ref[...], preferred_element_type=F32)
+    out_ref[...] = (acc * lax.rsqrt(square / (2 * half) + 1e-06)).astype(BF16)
 
 
 SMEM = pl.BlockSpec(memory_space=pltpu.SMEM)
@@ -329,7 +343,7 @@
         in_specs=[SMEM] * len(scalars) + [VMEM] * len(arrays) + [FAR] * len(far),
         out_specs=[VMEM] * len(outs),
         scratch_shapes=scratch_shapes,
-        name=getattr(body, "func", body).__name__,
+        name=body.__name__,
     )(*scalars, *[near(array) for array in arrays], *far)
 
 
@@ -398,17 +412,15 @@
     row_count, part_width = residual.shape
     half = width // 2
 
-    splits = ((0, width // head_dim),)
     query_rows = token_count * (width // head_dim)
     sent = pl.pallas_call(
-        send_queries,
-        out_shape=jax.ShapeDtypeStruct((seq_count, query_rows, head_dim), BF16),
+        copy_queries,
+        out_shape=jax.ShapeDtypeStruct((seq_count, token_count, width), BF16),
         in_specs=[VMEM],
         out_specs=VMEM,
-        name="send_queries",
+        name="copy_queries",
     )(queries)
-    sents = [sent]
-    column_rows = [exchange(sent, "seq")]
+    arrived = exchange(sent, "seq")
 
     column_table = lax.dynamic_index_in_dim(
         page_table.reshape(seq_count, mlp_count, page_count), mlp_place, 1, keepdims=False
@@ -435,27 +447,25 @@
         [queries, new_kv],
     )
     near_slots = 11
-    cache_front, _ = fetch([(kv_cache, near_slots)], sents[-1])
-    returned = []
-    for arrived in column_rows:
-        (held,) = call(
-            attend_pages,
-            [((seq_count, token_count, arrived.shape[1] // token_count * head_dim + 128), BF16, False)],
-            [codes, column_lengths],
-            [arrived, cache_front],
-            [kv_cache],
-            [((slot_count, arrived.shape[1], page_len), F32)] * 2
-            + [((slot_count, arrived.shape[1], head_dim), F32)]
-            + [((slot_count - near_slots, page_len, kv_width), BF16)],
-            1,
-            [pltpu.SMEM((slot_count + 1,), jnp.int32)],
-        )
-        returned.append(exchange(held, "seq"))
+    cache_front, _ = fetch([(kv_cache, near_slots)], sent)
+    (held,) = call(
+        attend_pages,
+        [((seq_count, token_count, width + 128), BF16, False)],
+        [codes, column_lengths],
+        [arrived, cache_front],
+        [kv_cache],
+        [((slot_count, query_rows, page_len), F32)] * 2
+        + [((slot_count, query_rows, head_dim), F32)]
+        + [((slot_count - near_slots, page_len, kv_width), BF16)],
+        1,
+        [pltpu.SMEM((slot_count + 1,), jnp.int32)],
+    )
+    returned = exchange(held, "seq")
     attended, spread = call(
-        functools.partial(merge_new, splits=splits),
+        merge_new,
         [((token_count, width), BF16, False), ((mlp_count, token_count, width), BF16, True)],
         [holder],
-        [*returned, new_max, new_sum, new_acc],
+        [returned, new_max, new_sum, new_acc],
     )
     rows = exchange(spread, "mlp")
     layers = [(gate_weight.T, 96), (up_weight.T, 96), (down_weight, 96)]
@@ -482,24 +492,41 @@
             ((2, row_count, half), F32),
         ]
         + [((far.shape[0] - rows, width), BF16) for far, rows in layers],
-        6,
+        9,
     )
     got = partner(send, 1)
     (chip_half,) = call(add_pair, [((row_count, half), BF16, True)], [], [keep, got])
     others = [partner(chip_half, distance) for distance in (2, 6, 4)]
-    near_rows = 1536
-    qkv_front, fetched = fetch([(qkv_weight, near_rows)], held)
+    columns = qkv_weight.shape[1]
+    near_rows = 1152
+    own_weight, fetched = pl.pallas_call(
+        fetch_half,
+        out_shape=[pltpu.VMEM((half, columns), BF16), jax.ShapeDtypeStruct((8, 128), F32)],
+        in_specs=[SMEM, FAR],
+        out_specs=[VMEM, VMEM],
+        scratch_shapes=[pltpu.SemaphoreType.DMA((1,))],
+        name="fetch_half",
+    )(place, qkv_weight)
     (after_half,) = call(
         add_chips, [((row_count, half), BF16, True)], [], [base, got, *others], [fetched]
     )
     other_half = partner(after_half, 1)
+    gains = next_gain.reshape(2, 1, half)
+    acc, square, other_weight = call(
+        project_own,
+        [((row_count, columns), F32, True), ((row_count, 128), F32, True), ((near_rows, columns), BF16, True)],
+        [place],
+        [after_half, gains, own_weight],
+        [qkv_weight],
+        copies=1,
+    )
     shard_after, next_qkv = call(
-        project_next,
-        [((row_count, part_width), BF16, False), ((row_count, qkv_weight.shape[1]), BF16, False)],
+        project_other,
+        [((row_count, part_width), BF16, False), ((row_count, columns), BF16, False)],
         [place],
-        [after_half, other_half, next_gain.reshape(1, width), qkv_front],
+        [after_half, other_half, gains, acc, square, other_weight],
         [qkv_weight],
-        [((row_count, width), F32), ((width - near_rows, qkv_weight.shape[1]), BF16)],
+        [((half - near_rows, columns), BF16)],
         1,
     )
     return (attended, shard_after, next_qkv)

time: 106 us -> 105 us (level)
    pallas_call x3 -> x2, Pallas kernels: 6 us -> 4.13 us  [fetch(): pl.pallas_call(fetch_rows, out_shape=[pltpu.VMEM((rows,) + far.shape[1:],...]
    pallas_call x1 -> x2, Pallas kernels: 1.68 us -> 3.47 us  [the longest x1 1.8 us: shards(): pl.pallas_call(fetch_half, out_shape=[pltpu.VMEM((half, columns), BF16),...]
    pallas_call x8 -> x9, Pallas kernels: 13.4 us -> 14.1 us  [call(): pl.pallas_call(body, out_shape=[pltpu.VMEM(shape, dtype) if stays else ja...]
  transfers between devices with their start and end apart: 15 -> 15, of which waited for: 7 -> 6; matrix products, arithmetic and copies ran while one was open for 3% -> 3% of each run, Pallas kernels for 6% -> 7%
where the time goes in v5:
time: 105 us
  starting transfers between devices  43.9 us (42%)
  waiting for transfers between devices  32.9 us (31%)
  Pallas kernels  21.7 us (21%)
  between operations  2.82 us (3%)
  other arithmetic  1.72 us (2%)
  local copies, waits for them, and re-layouts  1.53 us (1%)
    all_to_all x3, starting transfers between devices, exchange(): return lax.all_to_all(copies, axis, split_axis=0, concat_axis=0, tiled=True)  29.7 us
    all_to_all x3, waiting for transfers between devices, exchange(): return lax.all_to_all(copies, axis, split_axis=0, concat_axis=0, tiled=True)  29.6 us
    ppermute x12, starting transfers between devices, partner(): return lax.ppermute(block, 'mlp', [(i, i ^ distance) for i in range(count)])  14.3 us
    pallas_call x9, Pallas kernels, call(): pl.pallas_call(body, out_shape=[pltpu.VMEM(shape, dtype) if stays else ja...  14.1 us
    pallas_call x2, Pallas kernels, fetch(): pl.pallas_call(fetch_rows, out_shape=[pltpu.VMEM((rows,) + far.shape[1:],...  4.13 us
    ppermute x12, waiting for transfers between devices, partner(): return lax.ppermute(block, 'mlp', [(i, i ^ distance) for i in range(count)])  3.36 us
  transfers between devices with their start and end apart: 15, of which 6 were waited for; matrix products, arithmetic and copies ran while one was open for 3% of the time, Pallas kernels for 7%

profile of v5, /device:TPU:1, one launch (start us, length us, event | category | flops | bytes accessed | tf_op | source)
XLA Modules:
  0.0 104.6 jit_solution(8644399920695552504)
XLA Ops:
  0.6 0.0 copy-start
  0.6 1.7 %copy_queries.1.refs_0_ = bf16[32,4,2560]{2,1,0:T(4,128)(2,1)} custom-call(bf16[4,2560]{1,0:T(4,128)(2,1)} %queries_ref.3), custom_call_target="tpu_custom_call" | custom-call | tf_op jit(solution)/shard_map/copy_queries/pallas_call | solution.py:416
  2.3 11.9 %all-to-all-start = ((bf16[32,4,2560]{2,1,0:T(4,128)(2,1)}), bf16[32,4,2560]{2,1,0:T(4,128)(2,1)S(1)}, u32[]{:S(2)}, u32[]{:S(2)}) async-start(bf16[32,4,2560]{2,1,0:T(4,128)(2,1)} %copy_queries.1.refs_0_), calls=%async_computation | async-start | bytes 1310720 | tf_op jit(solution)/shard_map/all_to_all | solution.py:374
  14.2 0.8 reshape.59
  15.0 2.0 %fetch_rows.2 = (bf16[11,128,512]{2,1,0:T(8,128)(2,1)S(1)}, f32[8,128]{1,0:T(8,128)}) custom-call(bf16[32,4,2560]{2,1,0:T(4,128)(2,1)} %copy_queries.1.refs_0_, bf16[17,128,512]{2,1,0:T(8,128)(2,1)} %far_ref.4), custom_call_target="tpu_custom_call" | custom-call | tf_op jit(solution)/shard_map/fetch_rows/pallas_call | solution.py:362
  16.9 0.7 dynamic-slice_reduce_fusion.length_ref
  17.7 0.1 add_add_fusion
  17.7 1.0 select_reduce_fusion.code_ref
  18.7 11.8 %all-to-all-done.rows_ref = bf16[32,4,2560]{2,1,0:T(4,128)(2,1)S(1)} async-done(((bf16[32,4,2560]{2,1,0:T(4,128)(2,1)}), bf16[32,4,2560]{2,1,0:T(4,128)(2,1)S(1)}, u32[]{:S(2)}, u32[]{:S(2)}) %all-to-all-start) | async-done | bytes 655392 | tf_op jit(solution)/shard_map/all_to_all | solution.py:374
  30.6 3.9 %attend_pages.1.refs_0_ = bf16[32,4,2688]{2,1,0:T(4,128)(2,1)} custom-call(s32[17]{0:T(128)} %select_reduce_fusion.code_ref, s32[32]{0:T(128)} %dynamic-slice_reduce_fusion.length_ref, bf16[32,4,2560]{2,1,0:T(4,128)(2,1)S(1)} %all-to-all-done.rows_ref, bf16[11,128,512]{2,1,0:T(8,128)(2,1)S(1)} %get-tuple-element.23.front_ref, bf16[17,128,512]{2,1,0:T(8,128)(2,1)} %far_ref.4), custom_call_target="tpu_custom_call" | custom-call | tf_op jit(solution)/shard_map/attend_pages/pallas_call | solution.py:337
  34.5 8.4 %all-to-all-start.1 = ((bf16[32,4,2688]{2,1,0:T(4,128)(2,1)}), bf16[32,4,2688]{2,1,0:T(4,128)(2,1)S(1)}, u32[]{:S(2)}, u32[]{:S(2)}) async-start(bf16[32,4,2688]{2,1,0:T(4,128)(2,1)} %attend_pages.1.refs_0_), calls=%async_computation.1 | async-start | bytes 1376256 | tf_op jit(solution)/shard_map/all_to_all | solution.py:374
  42.9 0.6 fusion
  45.5 0.3 attend_new.1
  45.9 14.3 %all-to-all-done.1.got_ref = bf16[32,4,2688]{2,1,0:T(4,128)(2,1)S(1)} async-done(((bf16[32,4,2688]{2,1,0:T(4,128)(2,1)}), bf16[32,4,2688]{2,1,0:T(4,128)(2,1)S(1)}, u32[]{:S(2)}, u32[]{:S(2)}) %all-to-all-start.1) | async-done | bytes 688160 | tf_op jit(solution)/shard_map/all_to_all | solution.py:374
  60.2 0.9 merge_new.1
  61.1 9.4 %all-to-all-start.2 = ((bf16[8,4,2560]{2,1,0:T(4,128)(2,1)}), bf16[8,4,2560]{2,1,0:T(4,128)(2,1)S(1)}, u32[]{:S(2)}, u32[]{:S(2)}) async-start(bf16[8,4,2560]{2,1,0:T(4,128)(2,1)} %get-tuple-element.28), calls=%async_computation.2 | async-start | bytes 327680 | tf_op jit(solution)/shard_map/all_to_all | solution.py:374
  70.5 2.2 %fetch_rows.3 = (bf16[128,2560]{1,0:T(8,128)(2,1)S(1)}, bf16[96,2560]{1,0:T(8,128)(2,1)S(1)}, bf16[96,2560]{1,0:T(8,128)(2,1)S(1)}, bf16[96,2560]{1,0:T(8,128)(2,1)S(1)}, f32[8,128]{1,0:T(8,128)}) custom-call(bf16[32,4,2688]{2,1,0:T(4,128)(2,1)} %attend_pages.1.refs_0_, bf16[320,2560]{1,0:T(8,128)(2,1)} %bitcast.13, bf16[480,2560]{1,0:T(8,128)(2,1)} %bitcast.9, ...), custom_call_target="tpu_custom_call" | custom-call | tf_op jit(solution)/shard_map/fetch_rows/pallas_call | solution.py:362
  72.6 0.0 copy-start.4
  72.6 3.4 %all-to-all-done.2.rows_ref = bf16[8,4,2560]{2,1,0:T(4,128)(2,1)S(1)} async-done(((bf16[8,4,2560]{2,1,0:T(4,128)(2,1)}), bf16[8,4,2560]{2,1,0:T(4,128)(2,1)S(1)}, u32[]{:S(2)}, u32[]{:S(2)}) %all-to-all-start.2) | async-done | bytes 163872 | tf_op jit(solution)/shard_map/all_to_all | solution.py:374
  76.0 1.8 %project_out.1.refs_0_ = bf16[32,320]{1,0:T(8,128)(2,1)S(1)} custom-call(bf16[8,4,2560]{2,1,0:T(4,128)(2,1)S(1)} %all-to-all-done.2.rows_ref, bf16[32,320]{1,0:T(8,128)(2,1)S(1)} %copy-done.2, bf16[128,2560]{1,0:T(8,128)(2,1)S(1)} %get-tuple-element.29.front_ref, bf16[320,2560]{1,0:T(8,128)(2,1)} %bitcast.14), custom_call_target="tpu_custom_call" | custom-call | tf_op jit(solution)/shard_map/project_out/pallas_call | solution.py:337
  77.9 0.4 collective-permute-start.1
  78.2 1.8 %collective-permute-start.3 = (bf16[32,320]{1,0:T(8,128)(2,1)S(1)}, bf16[32,320]{1,0:T(8,128)(2,1)S(1)}, u32[]{:S(2)}, u32[]{:S(2)}) collective-permute-start(bf16[32,320]{1,0:T(8,128)(2,1)S(1)} %project_out.1.refs_0_), channel_id=1, source_target_pairs={{0,4},{1,5},{2,6},{3,7},{4,0},{5,1},{6,2},{7,3},{8,12},{9,13},{10,... | collective-permute-start | bytes 61448 | tf_op jit(solution)/shard_map/ppermute | solution.py:379
  80.0 1.8 %collective-permute-start.5 = (bf16[32,320]{1,0:T(8,128)(2,1)S(1)}, bf16[32,320]{1,0:T(8,128)(2,1)S(1)}, u32[]{:S(2)}, u32[]{:S(2)}) collective-permute-start(bf16[32,320]{1,0:T(8,128)(2,1)S(1)} %project_out.1.refs_0_), channel_id=1, source_target_pairs={{0,6},{1,7},{2,4},{3,5},{4,2},{5,3},{6,0},{7,1},{8,14},{9,15},{10,... | collective-permute-start | bytes 61448 | tf_op jit(solution)/shard_map/ppermute | solution.py:379
  81.8 1.7 %collective-permute-start = (bf16[32,320]{1,0:T(8,128)(2,1)S(1)}, bf16[32,320]{1,0:T(8,128)(2,1)S(1)}, u32[]{:S(2)}, u32[]{:S(2)}) collective-permute-start(bf16[32,320]{1,0:T(8,128)(2,1)S(1)} %project_out.1.refs_0_), channel_id=1, source_target_pairs={{0,1},{1,0},{2,3},{3,2},{4,5},{5,4},{6,7},{7,6},{8,9},{9,8},{10,11... | collective-permute-start | bytes 61448 | tf_op jit(solution)/shard_map/ppermute | solution.py:379
  83.6 0.0 collective-permute-start.2
  83.6 0.0 collective-permute-done.3.refs_4_
  83.6 1.3 %collective-permute-start.4 = (bf16[32,320]{1,0:T(8,128)(2,1)S(1)}, bf16[32,320]{1,0:T(8,128)(2,1)S(1)}, u32[]{:S(2)}, u32[]{:S(2)}) collective-permute-start(bf16[32,320]{1,0:T(8,128)(2,1)S(1)} %collective-permute-done.3.refs_4_), channel_id=1, source_target_pairs={{0,1},{1,0},{2,3},{3,2},{4,5},{5,4},{6,7},{7,6},{8,9},{9,8},{10,11... | collective-permute-start | bytes 61448 | tf_op jit(solution)/shard_map/ppermute | solution.py:379
  84.9 0.0 collective-permute-done.5.refs_6_
  84.9 1.7 %collective-permute-start.6 = (bf16[32,320]{1,0:T(8,128)(2,1)S(1)}, bf16[32,320]{1,0:T(8,128)(2,1)S(1)}, u32[]{:S(2)}, u32[]{:S(2)}) collective-permute-start(bf16[32,320]{1,0:T(8,128)(2,1)S(1)} %collective-permute-done.5.refs_6_), channel_id=1, source_target_pairs={{0,1},{1,0},{2,3},{3,2},{4,5},{5,4},{6,7},{7,6},{8,9},{9,8},{10,11... | collective-permute-start | bytes 61448 | tf_op jit(solution)/shard_map/ppermute | solution.py:379
  86.6 0.0 collective-permute-done.2.refs_3_
  86.6 0.0 collective-permute-done.4.refs_5_
  86.6 0.8 collective-permute-done.6.refs_7_
  87.4 4.2 %feed_forward.1 = (f32[32,1280]{1,0:T(8,128)S(1)}, bf16[32,1280]{1,0:T(8,128)(2,1)S(1)}, f32[32,1280]{1,0:T(8,128)S(1)}) custom-call(s32[1]{0:T(128)} %bitcast.3.place_ref, bf16[32,320]{1,0:T(8,128)(2,1)S(1)} %project_out.1.refs_0_, bf16[32,320]{1,0:T(8,128)(2,1)S(1)} %collective-permute-done.refs_1_, bf16[32,320]{1,0:T(8,128)(2,1)S(1)} %collective-permute-done.1.refs_2_, ...), custom_call_target="tpu_custom_call" | custom-call | tf_op jit(solution)/shard_map/feed_forward/pallas_call | solution.py:337
  91.5 0.0 copy-start.5
  91.6 0.4 collective-permute-start.7
  92.0 0.9 collective-permute-done.7.got_ref
  92.9 0.1 collective-permute-start.8
  93.0 1.9 %collective-permute-start.9 = (bf16[32,1280]{1,0:T(8,128)(2,1)S(1)}, bf16[32,1280]{1,0:T(8,128)(2,1)S(1)}, u32[]{:S(2)}, u32[]{:S(2)}) collective-permute-start(bf16[32,1280]{1,0:T(8,128)(2,1)S(1)} %add_pair.1), channel_id=1, source_target_pairs={{0,6},{1,7},{2,4},{3,5},{4,2},{5,3},{6,0},{7,1},{8,14},{9,15},{10,... | collective-permute-start | bytes 245768 | tf_op jit(solution)/shard_map/ppermute | solution.py:379
  94.9 1.4 %collective-permute-start.10 = (bf16[32,1280]{1,0:T(8,128)(2,1)S(1)}, bf16[32,1280]{1,0:T(8,128)(2,1)S(1)}, u32[]{:S(2)}, u32[]{:S(2)}) collective-permute-start(bf16[32,1280]{1,0:T(8,128)(2,1)S(1)} %add_pair.1), channel_id=1, source_target_pairs={{0,4},{1,5},{2,6},{3,7},{4,0},{5,1},{6,2},{7,3},{8,12},{9,13},{10,... | collective-permute-start | bytes 245768 | tf_op jit(solution)/shard_map/ppermute | solution.py:379
  96.3 1.8 %fetch_half.1 = (bf16[1280,384]{1,0:T(8,128)(2,1)S(1)}, f32[8,128]{1,0:T(8,128)}) custom-call(s32[1]{0:T(128)} %bitcast.3.place_ref, bf16[2560,384]{1,0:T(8,128)(2,1)} %far_ref.7), custom_call_target="tpu_custom_call" | custom-call | tf_op jit(solution)/shard_map/fetch_half/pallas_call | solution.py:502
  98.1 0.0 collective-permute-done.8.first_ref
  98.1 0.0 collective-permute-done.9.second_ref
  98.1 1.6 %collective-permute-done.10.third_ref = bf16[32,1280]{1,0:T(8,128)(2,1)S(1)} collective-permute-done((bf16[32,1280]{1,0:T(8,128)(2,1)S(1)}, bf16[32,1280]{1,0:T(8,128)(2,1)S(1)}, u32[]{:S(2)}, u32[]{:S(2)}) %collective-permute-start.10) | collective-permute-done | bytes 81952 | tf_op jit(solution)/shard_map/ppermute | solution.py:379
  99.7 0.1 add_chips.1.own_ref
  99.8 1.9 %collective-permute-start.11 = (bf16[32,1280]{1,0:T(8,128)(2,1)S(1)}, bf16[32,1280]{1,0:T(8,128)(2,1)S(1)}, u32[]{:S(2)}, u32[]{:S(2)}) collective-permute-start(bf16[32,1280]{1,0:T(8,128)(2,1)S(1)} %add_chips.1.own_ref), channel_id=1, source_target_pairs={{0,1},{1,0},{2,3},{3,2},{4,5},{5,4},{6,7},{7,6},{8,9},{9,8},{10,11... | collective-permute-start | bytes 245768 | tf_op jit(solution)/shard_map/ppermute | solution.py:379
  101.7 1.3 %project_own.1 = (f32[32,384]{1,0:T(8,128)S(1)}, f32[32,128]{1,0:T(8,128)S(1)}, bf16[1152,384]{1,0:T(8,128)(2,1)S(1)}) custom-call(s32[1]{0:T(128)} %bitcast.3.place_ref, bf16[32,1280]{1,0:T(8,128)(2,1)S(1)} %add_chips.1.own_ref, f32[2,1,1280]{2,1,0:T(1,128)S(1)} %reshape.62.gain_ref, bf16[1280,384]{1,0:T(8,128)(2,1)S(1)} %get-tuple-element.37.weight_ref, ...), custom_call_target="tpu_custom_call" | custom-call | tf_op jit(solution)/shard_map/project_own/pallas_call | solution.py:337
  103.0 0.0 collective-permute-done.11.other_ref
  103.0 1.7 %project_other.1 = (bf16[32,320]{1,0:T(8,128)(2,1)}, bf16[32,384]{1,0:T(8,128)(2,1)}) custom-call(s32[1]{0:T(128)} %bitcast.3.place_ref, bf16[32,1280]{1,0:T(8,128)(2,1)S(1)} %add_chips.1.own_ref, bf16[32,1280]{1,0:T(8,128)(2,1)S(1)} %collective-permute-done.11.other_ref, f32[2,1,1280]{2,1,0:T(1,128)S(1)} %reshape.62.gain_ref, ...), custom_call_target="tpu_custom_call" | custom-call | tf_op jit(solution)/shard_map/project_other/pallas_call | solution.py:337
  (17 shorter events, 0.1 us)
Async XLA Ops:
  0.6 17.0 %copy-start = (s32[256,128]{1,0:T(8,128)S(1)}, s32[256,128]{1,0:T(8,128)}, u32[]{:S(2)}) copy-start(s32[256,128]{1,0:T(8,128)} %param.17) | copy-start | bytes 393220
  2.3 28.3 %all-to-all-start = ((bf16[32,4,2560]{2,1,0:T(4,128)(2,1)}), bf16[32,4,2560]{2,1,0:T(4,128)(2,1)S(1)}, u32[]{:S(2)}, u32[]{:S(2)}) async-start(bf16[32,4,2560]{2,1,0:T(4,128)(2,1)} %copy_queries.1.refs_0_), calls=%async_computation | async-start | bytes 1310720 | tf_op jit(solution)/shard_map/all_to_all | solution.py:374
  30.6 14.9 %copy-start.1 = (bf16[4,2560]{1,0:T(4,128)(2,1)S(1)}, bf16[4,2560]{1,0:T(4,128)(2,1)}, u32[]{:S(2)}) copy-start(bf16[4,2560]{1,0:T(4,128)(2,1)} %queries_ref.3) | copy-start | bytes 61444
  30.6 14.9 %copy-start.3 = (bf16[4,512]{1,0:T(4,128)(2,1)S(1)}, bf16[4,512]{1,0:T(4,128)(2,1)}, u32[]{:S(2)}) copy-start(bf16[4,512]{1,0:T(4,128)(2,1)} %new_ref.1) | copy-start | bytes 12292
  34.5 25.7 %all-to-all-start.1 = ((bf16[32,4,2688]{2,1,0:T(4,128)(2,1)}), bf16[32,4,2688]{2,1,0:T(4,128)(2,1)S(1)}, u32[]{:S(2)}, u32[]{:S(2)}) async-start(bf16[32,4,2688]{2,1,0:T(4,128)(2,1)} %attend_pages.1.refs_0_), calls=%async_computation.1 | async-start | bytes 1376256 | tf_op jit(solution)/shard_map/all_to_all | solution.py:374
  61.1 15.0 %all-to-all-start.2 = ((bf16[8,4,2560]{2,1,0:T(4,128)(2,1)}), bf16[8,4,2560]{2,1,0:T(4,128)(2,1)S(1)}, u32[]{:S(2)}, u32[]{:S(2)}) async-start(bf16[8,4,2560]{2,1,0:T(4,128)(2,1)} %get-tuple-element.28), calls=%async_computation.2 | async-start | bytes 327680 | tf_op jit(solution)/shard_map/all_to_all | solution.py:374
  70.5 5.6 %copy-start.2 = (bf16[32,320]{1,0:T(8,128)(2,1)S(1)}, bf16[32,320]{1,0:T(8,128)(2,1)}, u32[]{:S(2)}) copy-start(bf16[32,320]{1,0:T(8,128)(2,1)} %residual_ref.1) | copy-start | bytes 61444
  72.6 13.9 %copy-start.4 = (f32[2560]{0:T(1024)S(1)}, f32[2560]{0:T(1024)}, u32[]{:S(2)}) copy-start(f32[2560]{0:T(1024)} %param.20) | copy-start | bytes 30724
  77.9 5.7 %collective-permute-start.1 = (bf16[32,320]{1,0:T(8,128)(2,1)S(1)}, bf16[32,320]{1,0:T(8,128)(2,1)S(1)}, u32[]{:S(2)}, u32[]{:S(2)}) collective-permute-start(bf16[32,320]{1,0:T(8,128)(2,1)S(1)} %project_out.1.refs_0_), channel_id=1, source_target_pairs={{0,2},{1,3},{2,0},{3,1},{4,6},{5,7},{6,4},{7,5},{8,10},{9,11},{10,... | collective-permute-start | bytes 61448 | tf_op jit(solution)/shard_map/ppermute | solution.py:379
  78.2 5.3 %collective-permute-start.3 = (bf16[32,320]{1,0:T(8,128)(2,1)S(1)}, bf16[32,320]{1,0:T(8,128)(2,1)S(1)}, u32[]{:S(2)}, u32[]{:S(2)}) collective-permute-start(bf16[32,320]{1,0:T(8,128)(2,1)S(1)} %project_out.1.refs_0_), channel_id=1, source_target_pairs={{0,4},{1,5},{2,6},{3,7},{4,0},{5,1},{6,2},{7,3},{8,12},{9,13},{10,... | collective-permute-start | bytes 61448 | tf_op jit(solution)/shard_map/ppermute | solution.py:379
  80.0 4.8 %collective-permute-start.5 = (bf16[32,320]{1,0:T(8,128)(2,1)S(1)}, bf16[32,320]{1,0:T(8,128)(2,1)S(1)}, u32[]{:S(2)}, u32[]{:S(2)}) collective-permute-start(bf16[32,320]{1,0:T(8,128)(2,1)S(1)} %project_out.1.refs_0_), channel_id=1, source_target_pairs={{0,6},{1,7},{2,4},{3,5},{4,2},{5,3},{6,0},{7,1},{8,14},{9,15},{10,... | collective-permute-start | bytes 61448 | tf_op jit(solution)/shard_map/ppermute | solution.py:379
  81.8 4.7 %collective-permute-start = (bf16[32,320]{1,0:T(8,128)(2,1)S(1)}, bf16[32,320]{1,0:T(8,128)(2,1)S(1)}, u32[]{:S(2)}, u32[]{:S(2)}) collective-permute-start(bf16[32,320]{1,0:T(8,128)(2,1)S(1)} %project_out.1.refs_0_), channel_id=1, source_target_pairs={{0,1},{1,0},{2,3},{3,2},{4,5},{5,4},{6,7},{7,6},{8,9},{9,8},{10,11... | collective-permute-start | bytes 61448 | tf_op jit(solution)/shard_map/ppermute | solution.py:379
  83.6 3.0 %collective-permute-start.2 = (bf16[32,320]{1,0:T(8,128)(2,1)S(1)}, bf16[32,320]{1,0:T(8,128)(2,1)S(1)}, u32[]{:S(2)}, u32[]{:S(2)}) collective-permute-start(bf16[32,320]{1,0:T(8,128)(2,1)S(1)} %collective-permute-done.1.refs_2_), channel_id=1, source_target_pairs={{0,1},{1,0},{2,3},{3,2},{4,5},{5,4},{6,7},{7,6},{8,9},{9,8},{10,11... | collective-permute-start | bytes 61448 | tf_op jit(solution)/shard_map/ppermute | solution.py:379
  83.6 3.0 %collective-permute-start.4 = (bf16[32,320]{1,0:T(8,128)(2,1)S(1)}, bf16[32,320]{1,0:T(8,128)(2,1)S(1)}, u32[]{:S(2)}, u32[]{:S(2)}) collective-permute-start(bf16[32,320]{1,0:T(8,128)(2,1)S(1)} %collective-permute-done.3.refs_4_), channel_id=1, source_target_pairs={{0,1},{1,0},{2,3},{3,2},{4,5},{5,4},{6,7},{7,6},{8,9},{9,8},{10,11... | collective-permute-start | bytes 61448 | tf_op jit(solution)/shard_map/ppermute | solution.py:379
  84.9 2.5 %collective-permute-start.6 = (bf16[32,320]{1,0:T(8,128)(2,1)S(1)}, bf16[32,320]{1,0:T(8,128)(2,1)S(1)}, u32[]{:S(2)}, u32[]{:S(2)}) collective-permute-start(bf16[32,320]{1,0:T(8,128)(2,1)S(1)} %collective-permute-done.5.refs_6_), channel_id=1, source_target_pairs={{0,1},{1,0},{2,3},{3,2},{4,5},{5,4},{6,7},{7,6},{8,9},{9,8},{10,11... | collective-permute-start | bytes 61448 | tf_op jit(solution)/shard_map/ppermute | solution.py:379
  91.5 10.1 %copy-start.5 = (f32[2560]{0:T(1024)S(1)}, f32[2560]{0:T(1024)}, u32[]{:S(2)}) copy-start(f32[2560]{0:T(1024)} %param.24) | copy-start | bytes 30724
  91.6 1.4 %collective-permute-start.7 = (bf16[32,1280]{1,0:T(8,128)(2,1)S(1)}, bf16[32,1280]{1,0:T(8,128)(2,1)S(1)}, u32[]{:S(2)}, u32[]{:S(2)}) collective-permute-start(bf16[32,1280]{1,0:T(8,128)(2,1)S(1)} %get-tuple-element.34), channel_id=1, source_target_pairs={{0,1},{1,0},{2,3},{3,2},{4,5},{5,4},{6,7},{7,6},{8,9},{9,8},{10,11... | collective-permute-start | bytes 245768 | tf_op jit(solution)/shard_map/ppermute | solution.py:379
  92.9 5.2 %collective-permute-start.8 = (bf16[32,1280]{1,0:T(8,128)(2,1)S(1)}, bf16[32,1280]{1,0:T(8,128)(2,1)S(1)}, u32[]{:S(2)}, u32[]{:S(2)}) collective-permute-start(bf16[32,1280]{1,0:T(8,128)(2,1)S(1)} %add_pair.1), channel_id=1, source_target_pairs={{0,2},{1,3},{2,0},{3,1},{4,6},{5,7},{6,4},{7,5},{8,10},{9,11},{10,... | collective-permute-start | bytes 245768 | tf_op jit(solution)/shard_map/ppermute | solution.py:379
  93.0 5.1 %collective-permute-start.9 = (bf16[32,1280]{1,0:T(8,128)(2,1)S(1)}, bf16[32,1280]{1,0:T(8,128)(2,1)S(1)}, u32[]{:S(2)}, u32[]{:S(2)}) collective-permute-start(bf16[32,1280]{1,0:T(8,128)(2,1)S(1)} %add_pair.1), channel_id=1, source_target_pairs={{0,6},{1,7},{2,4},{3,5},{4,2},{5,3},{6,0},{7,1},{8,14},{9,15},{10,... | collective-permute-start | bytes 245768 | tf_op jit(solution)/shard_map/ppermute | solution.py:379
  94.9 4.8 %collective-permute-start.10 = (bf16[32,1280]{1,0:T(8,128)(2,1)S(1)}, bf16[32,1280]{1,0:T(8,128)(2,1)S(1)}, u32[]{:S(2)}, u32[]{:S(2)}) collective-permute-start(bf16[32,1280]{1,0:T(8,128)(2,1)S(1)} %add_pair.1), channel_id=1, source_target_pairs={{0,4},{1,5},{2,6},{3,7},{4,0},{5,1},{6,2},{7,3},{8,12},{9,13},{10,... | collective-permute-start | bytes 245768 | tf_op jit(solution)/shard_map/ppermute | solution.py:379
  99.8 3.2 %collective-permute-start.11 = (bf16[32,1280]{1,0:T(8,128)(2,1)S(1)}, bf16[32,1280]{1,0:T(8,128)(2,1)S(1)}, u32[]{:S(2)}, u32[]{:S(2)}) collective-permute-start(bf16[32,1280]{1,0:T(8,128)(2,1)S(1)} %add_chips.1.own_ref), channel_id=1, source_target_pairs={{0,1},{1,0},{2,3},{3,2},{4,5},{5,4},{6,7},{7,6},{8,9},{9,8},{10,11... | collective-permute-start | bytes 245768 | tf_op jit(solution)/shard_map/ppermute | solution.py:379

commit v6 on v5

--- a/solution.py
+++ b/solution.py
@@ -172,24 +172,22 @@
             spread_ref[place, :, span] = rows
 
 
-def project_out(rows_ref, residual_ref, front_ref, weight_far, out_ref, rest_ref, copied):
+def project_out(rows_ref, residual_ref, weight_ref, out_ref):
     places = rows_ref.shape[0]
-    near_rows = front_ref.shape[0]
-    rest = pltpu.make_async_copy(weight_far.at[pl.ds(near_rows, rest_ref.shape[0])], rest_ref, copied.at[0])
-    rest.start()
     rows = jnp.concatenate([rows_ref[place].astype(F32) for place in range(places)], axis=0).astype(BF16)
-    attention_out = lax.dot_general(rows, front_ref[...], LAST, preferred_element_type=F32)
-    out_ref[:, :near_rows] = (residual_ref[:, :near_rows].astype(F32) + attention_out).astype(BF16)
-    rest.wait()
-    attention_out = lax.dot_general(rows, rest_ref[...], LAST, preferred_element_type=F32)
-    out_ref[:, near_rows:] = (residual_ref[:, near_rows:].astype(F32) + attention_out).astype(BF16)
+    attention_out = lax.dot_general(rows, weight_ref[...], LAST, preferred_element_type=F32)
+    out_ref[...] = (residual_ref[...].astype(F32) + attention_out).astype(BF16)
+
+
+def stack_blocks(first_ref, second_ref, third_ref, fourth_ref, fetched_ref, out_ref):
+    for index, block_ref in enumerate((first_ref, second_ref, third_ref, fourth_ref)):
+        out_ref[index] = block_ref[...]
 
 
 def feed_forward(place_ref, *refs):
-    block_refs = refs[:8]
-    gain_ref, gate_ref, up_ref, down_ref, gate_far, up_far, down_far = refs[8:15]
-    keep_ref, send_ref, base_ref = refs[15:18]
-    stream_ref, whole_ref, halves_ref, gate_rest, up_rest, down_rest, copied = refs[18:]
+    mine_ref, theirs_ref, gain_ref, gate_ref, up_ref, down_ref, gate_far, up_far, down_far = refs[:9]
+    keep_ref, send_ref, stream_half_ref = refs[9:12]
+    stream_ref, whole_ref, halves_ref, gate_rest, up_rest, down_rest, copied = refs[12:]
     parts, rows, width = stream_ref.shape
     total = parts * width
     half = total // 2
@@ -207,14 +205,23 @@
                 )
             )
             copies[-1].start()
-    for distance, block_ref in enumerate(block_refs):
-        stream_ref[place_ref[0] ^ distance] = block_ref[...].astype(F32)
+    for index, distance in enumerate(DISTANCES):
+        stream_ref[place_ref[0] ^ distance] = mine_ref[index].astype(F32)
+        stream_ref[place_ref[0] ^ distance ^ 1] = theirs_ref[index].astype(F32)
     for part in range(parts):
         whole_ref[:, part * width : (part + 1) * width] = stream_ref[part]
     whole = whole_ref[...]
     square = jnp.sum(whole * whole, axis=1, keepdims=True)
     normed = (whole * lax.rsqrt(square / total + 1e-06) * gain_ref[...]).astype(BF16)
     core = place_ref[0] % 2
+
+    @pl.when(core == 0)
+    def _():
+        stream_half_ref[...] = whole_ref[:, :half].astype(BF16)
+
+    @pl.when(core == 1)
+    def _():
+        stream_half_ref[...] = whole_ref[:, half:].astype(BF16)
 
     def through(gate_rows, up_rows, down_rows):
         gate = lax.dot_general(normed, gate_rows, LAST, preferred_element_type=F32)
@@ -233,36 +240,41 @@
     keep_ref[...] = halves_ref[core]
     send_ref[...] = halves_ref[1 - core].astype(BF16)
 
-    @pl.when(core == 0)
-    def _():
-        base_ref[...] = whole_ref[:, :half] + keep_ref[...]
-
-    @pl.when(core == 1)
-    def _():
-        base_ref[...] = whole_ref[:, half:] + keep_ref[...]
-
 
 def add_pair(keep_ref, got_ref, send_ref):
     send_ref[...] = (keep_ref[...] + got_ref[...].astype(F32)).astype(BF16)
 
 
-def add_chips(base_ref, got_ref, first_ref, second_ref, third_ref, fetched_ref, out_ref):
-    total = base_ref[...] + got_ref[...].astype(F32)
+def add_chips(keep_ref, got_ref, first_ref, second_ref, third_ref, stream_ref, fetched_ref, out_ref):
+    total = keep_ref[...] + got_ref[...].astype(F32)
     total = total + first_ref[...].astype(F32) + second_ref[...].astype(F32) + third_ref[...].astype(F32)
-    out_ref[...] = total.astype(BF16)
+    out_ref[...] = (stream_ref[...].astype(F32) + total).astype(BF16)
 
 
 def fetch_half(place_ref, far_ref, out_ref, token_ref, copied):
-    half = out_ref.shape[0]
+    half = far_ref.shape[0] // 2
     copy = pltpu.make_async_copy(
-        far_ref.at[pl.ds(pl.multiple_of(place_ref[0] % 2 * half, 128), half)], out_ref, copied.at[0]
+        far_ref.at[pl.ds(pl.multiple_of(place_ref[0] % 2 * half, 128), out_ref.shape[0])],
+        out_ref,
+        copied.at[0],
     )
     copy.start()
     token_ref[...] = jnp.zeros(token_ref.shape, F32)
     copy.wait()
 
 
-def project_own(place_ref, own_ref, gain_ref, weight_ref, far_ref, acc_ref, square_ref, other_weight_ref, copied):
+def project_own(
+    place_ref,
+    own_ref,
+    gain_ref,
+    front_ref,
+    far_ref,
+    acc_ref,
+    square_ref,
+    other_weight_ref,
+    rest_ref,
+    copied,
+):
     half = own_ref.shape[1]
     core = place_ref[0] % 2
     near_rows = other_weight_ref.shape[0]
@@ -271,11 +283,20 @@
         other_weight_ref,
         copied.at[0],
     )
+    own_rows = front_ref.shape[0]
+    rest = pltpu.make_async_copy(
+        far_ref.at[pl.ds(pl.multiple_of(core * half + own_rows, 128), half - own_rows)],
+        rest_ref,
+        copied.at[1],
+    )
+    rest.start()
     copy.start()
     own = own_ref[...].astype(F32)
     square_ref[...] = jnp.broadcast_to(jnp.sum(own * own, axis=1, keepdims=True), square_ref.shape)
     scaled = (own * gain_ref[core]).astype(BF16)
-    acc_ref[...] = jnp.dot(scaled, weight_ref[...], preferred_element_type=F32)
+    acc = jnp.dot(scaled[:, :own_rows], front_ref[...], preferred_element_type=F32)
+    rest.wait()
+    acc_ref[...] = acc + jnp.dot(scaled[:, own_rows:], rest_ref[...], preferred_element_type=F32)
     copy.wait()
 
 
@@ -324,6 +345,8 @@
 SMEM = pl.BlockSpec(memory_space=pltpu.SMEM)
 VMEM = pl.BlockSpec(memory_space=pltpu.VMEM)
 FAR = pl.BlockSpec(memory_space=pl.ANY)
+DISTANCES = (0, 2, 6, 4)
+NEAR = 128
 
 
 def near(array):
@@ -377,12 +400,6 @@
 def partner(block, distance):
     count = lax.axis_size("mlp")
     return lax.ppermute(block, "mlp", [(i, i ^ distance) for i in range(count)])
-
-
-def gather(block):
-    near = {0: block, **{distance: partner(block, distance) for distance in (2, 6, 4)}}
-    far = {distance ^ 1: partner(near[distance], 1) for distance in near}
-    return [{**near, **far}[distance] for distance in range(8)]
 
 
 def shards(
@@ -468,23 +485,29 @@
         [returned, new_max, new_sum, new_acc],
     )
     rows = exchange(spread, "mlp")
-    layers = [(gate_weight.T, 96), (up_weight.T, 96), (down_weight, 96)]
-    out_front, *front, _ = fetch([(out_weight.T, 128), *layers], held)
+    out_near, _ = fetch([(out_weight.T, part_width)], held)
     (stream,) = call(
         project_out,
         [((row_count, part_width), BF16, True)],
         [],
-        [rows, residual, out_front],
-        [out_weight.T],
-        [((part_width - 128, width), BF16)],
-        1,
-    )
+        [rows, residual, out_near],
+    )
+    layers = [(gate_weight.T, NEAR), (up_weight.T, NEAR), (down_weight, NEAR)]
+    *front, fetched = fetch(layers, held)
+    (mine,) = call(
+        stack_blocks,
+        [((4, row_count, part_width), BF16, True)],
+        [],
+        [stream, *[partner(stream, distance) for distance in DISTANCES[1:]]],
+        [fetched],
+    )
+    theirs = partner(mine, 1)
     place = mlp_place.astype(jnp.int32).reshape(1)
-    keep, send, base = call(
+    keep, send, stream_half = call(
         feed_forward,
-        [((row_count, half), F32, True), ((row_count, half), BF16, True), ((row_count, half), F32, True)],
+        [((row_count, half), F32, True), ((row_count, half), BF16, True), ((row_count, half), BF16, True)],
         [place],
-        [*gather(stream), norm_gain.reshape(1, width), *front],
+        [mine, theirs, norm_gain.reshape(1, width), *front],
         [far for far, _ in layers],
         [
             ((mlp_count, row_count, part_width), F32),
@@ -492,23 +515,24 @@
             ((2, row_count, half), F32),
         ]
         + [((far.shape[0] - rows, width), BF16) for far, rows in layers],
-        9,
+        6,
     )
     got = partner(send, 1)
     (chip_half,) = call(add_pair, [((row_count, half), BF16, True)], [], [keep, got])
-    others = [partner(chip_half, distance) for distance in (2, 6, 4)]
+    others = [partner(chip_half, distance) for distance in DISTANCES[1:]]
     columns = qkv_weight.shape[1]
+    own_rows = 1152
     near_rows = 1152
     own_weight, fetched = pl.pallas_call(
         fetch_half,
-        out_shape=[pltpu.VMEM((half, columns), BF16), jax.ShapeDtypeStruct((8, 128), F32)],
+        out_shape=[pltpu.VMEM((own_rows, columns), BF16), jax.ShapeDtypeStruct((8, 128), F32)],
         in_specs=[SMEM, FAR],
         out_specs=[VMEM, VMEM],
         scratch_shapes=[pltpu.SemaphoreType.DMA((1,))],
         name="fetch_half",
     )(place, qkv_weight)
     (after_half,) = call(
-        add_chips, [((row_count, half), BF16, True)], [], [base, got, *others], [fetched]
+        add_chips, [((row_count, half), BF16, True)], [], [keep, got, *others, stream_half], [fetched]
     )
     other_half = partner(after_half, 1)
     gains = next_gain.reshape(2, 1, half)
@@ -518,7 +542,8 @@
         [place],
         [after_half, gains, own_weight],
         [qkv_weight],
-        copies=1,
+        [((half - own_rows, columns), BF16)],
+        2,
     )
     shard_after, next_qkv = call(
         project_other,

time: 105 us -> 104 us (level)
  starting transfers between devices: 43.9 us -> 41.3 us
  waiting for transfers between devices: 32.9 us -> 34 us
    ppermute x12 -> x9, starting transfers between devices: 14.3 us -> 11.6 us  [partner(): return lax.ppermute(block, 'mlp', [(i, i ^ distance) for i in range(count)])]
    pallas_call x2 -> x3, Pallas kernels: 4.13 us -> 6.11 us  [fetch(): pl.pallas_call(fetch_rows, out_shape=[pltpu.VMEM((rows,) + far.shape[1:],...]
    pallas_call x9 -> x10, Pallas kernels: 14.1 us -> 12.4 us  [call(): pl.pallas_call(body, out_shape=[pltpu.VMEM(shape, dtype) if stays else ja...]
    ppermute x12 -> x9, waiting for transfers between devices: 3.36 us -> 4.27 us  [partner(): return lax.ppermute(block, 'mlp', [(i, i ^ distance) for i in range(count)])]
  transfers between devices with their start and end apart: 15 -> 12, of which waited for: 6 -> 7; matrix products, arithmetic and copies ran while one was open for 3% -> 3% of each run, Pallas kernels for 7% -> 9%
where the time goes in v6:
time: 104 us; the launch traced here: 103 us
  starting transfers between devices  41.3 us (40%)
  waiting for transfers between devices  34 us (33%)
  Pallas kernels  21.9 us (21%)
  between operations  2.82 us (3%)
  other arithmetic  1.72 us (2%)
  local copies, waits for them, and re-layouts  1.53 us (1%)
    all_to_all x3, waiting for transfers between devices, exchange(): return lax.all_to_all(copies, axis, split_axis=0, concat_axis=0, tiled=True)  29.7 us
    all_to_all x3, starting transfers between devices, exchange(): return lax.all_to_all(copies, axis, split_axis=0, concat_axis=0, tiled=True)  29.6 us
    pallas_call x10, Pallas kernels, call(): pl.pallas_call(body, out_shape=[pltpu.VMEM(shape, dtype) if stays else ja...  12.4 us
    ppermute x9, starting transfers between devices, partner(): return lax.ppermute(block, 'mlp', [(i, i ^ distance) for i in range(count)])  11.6 us
    pallas_call x3, Pallas kernels, fetch(): pl.pallas_call(fetch_rows, out_shape=[pltpu.VMEM((rows,) + far.shape[1:],...  6.11 us
    ppermute x9, waiting for transfers between devices, partner(): return lax.ppermute(block, 'mlp', [(i, i ^ distance) for i in range(count)])  4.27 us
  transfers between devices with their start and end apart: 12, of which 7 were waited for; matrix products, arithmetic and copies ran while one was open for 3% of the time, Pallas kernels for 9%

profile of v6, /device:TPU:1, one launch (start us, length us, event | category | flops | bytes accessed | tf_op | source)
XLA Modules:
  0.0 103.2 jit_solution(18289723628642311413)
XLA Ops:
  0.6 0.0 copy-start
  0.6 1.7 %copy_queries.1.refs_0_ = bf16[32,4,2560]{2,1,0:T(4,128)(2,1)} custom-call(bf16[4,2560]{1,0:T(4,128)(2,1)} %queries_ref.3), custom_call_target="tpu_custom_call" | custom-call | tf_op jit(solution)/shard_map/copy_queries/pallas_call | solution.py:433
  2.3 11.9 %all-to-all-start = ((bf16[32,4,2560]{2,1,0:T(4,128)(2,1)}), bf16[32,4,2560]{2,1,0:T(4,128)(2,1)S(1)}, u32[]{:S(2)}, u32[]{:S(2)}) async-start(bf16[32,4,2560]{2,1,0:T(4,128)(2,1)} %copy_queries.1.refs_0_), calls=%async_computation | async-start | bytes 1310720 | tf_op jit(solution)/shard_map/all_to_all | solution.py:397
  14.2 0.8 reshape.59
  15.0 2.0 %fetch_rows.3 = (bf16[11,128,512]{2,1,0:T(8,128)(2,1)S(1)}, f32[8,128]{1,0:T(8,128)}) custom-call(bf16[32,4,2560]{2,1,0:T(4,128)(2,1)} %copy_queries.1.refs_0_, bf16[17,128,512]{2,1,0:T(8,128)(2,1)} %far_ref.4), custom_call_target="tpu_custom_call" | custom-call | tf_op jit(solution)/shard_map/fetch_rows/pallas_call | solution.py:385
  16.9 0.7 dynamic-slice_reduce_fusion.length_ref
  17.6 0.0 copy-done
  17.7 0.1 add_add_fusion
  17.7 1.0 select_reduce_fusion.code_ref
  18.7 11.8 %all-to-all-done.rows_ref = bf16[32,4,2560]{2,1,0:T(4,128)(2,1)S(1)} async-done(((bf16[32,4,2560]{2,1,0:T(4,128)(2,1)}), bf16[32,4,2560]{2,1,0:T(4,128)(2,1)S(1)}, u32[]{:S(2)}, u32[]{:S(2)}) %all-to-all-start) | async-done | bytes 655392 | tf_op jit(solution)/shard_map/all_to_all | solution.py:397
  30.6 3.9 %attend_pages.1.refs_0_ = bf16[32,4,2688]{2,1,0:T(4,128)(2,1)} custom-call(s32[17]{0:T(128)} %select_reduce_fusion.code_ref, s32[32]{0:T(128)} %dynamic-slice_reduce_fusion.length_ref, bf16[32,4,2560]{2,1,0:T(4,128)(2,1)S(1)} %all-to-all-done.rows_ref, bf16[11,128,512]{2,1,0:T(8,128)(2,1)S(1)} %get-tuple-element.24.front_ref, bf16[17,128,512]{2,1,0:T(8,128)(2,1)} %far_ref.4), custom_call_target="tpu_custom_call" | custom-call | tf_op jit(solution)/shard_map/attend_pages/pallas_call | solution.py:360
  34.5 0.0 copy-start.2
  34.5 8.4 %all-to-all-start.1 = ((bf16[32,4,2688]{2,1,0:T(4,128)(2,1)}), bf16[32,4,2688]{2,1,0:T(4,128)(2,1)S(1)}, u32[]{:S(2)}, u32[]{:S(2)}) async-start(bf16[32,4,2688]{2,1,0:T(4,128)(2,1)} %attend_pages.1.refs_0_), calls=%async_computation.1 | async-start | bytes 1376256 | tf_op jit(solution)/shard_map/all_to_all | solution.py:397
  42.9 0.6 fusion
  45.5 0.0 copy-done.1
  45.5 0.3 attend_new.1
  45.9 14.4 %all-to-all-done.1.got_ref = bf16[32,4,2688]{2,1,0:T(4,128)(2,1)S(1)} async-done(((bf16[32,4,2688]{2,1,0:T(4,128)(2,1)}), bf16[32,4,2688]{2,1,0:T(4,128)(2,1)S(1)}, u32[]{:S(2)}, u32[]{:S(2)}) %all-to-all-start.1) | async-done | bytes 688160 | tf_op jit(solution)/shard_map/all_to_all | solution.py:397
  60.2 0.9 merge_new.1
  61.1 9.3 %all-to-all-start.2 = ((bf16[8,4,2560]{2,1,0:T(4,128)(2,1)}), bf16[8,4,2560]{2,1,0:T(4,128)(2,1)S(1)}, u32[]{:S(2)}, u32[]{:S(2)}) async-start(bf16[8,4,2560]{2,1,0:T(4,128)(2,1)} %get-tuple-element.29), calls=%async_computation.2 | async-start | bytes 327680 | tf_op jit(solution)/shard_map/all_to_all | solution.py:397
  70.5 2.0 %fetch_rows.4 = (bf16[320,2560]{1,0:T(8,128)(2,1)S(1)}, f32[8,128]{1,0:T(8,128)}) custom-call(bf16[32,4,2688]{2,1,0:T(4,128)(2,1)} %attend_pages.1.refs_0_, bf16[320,2560]{1,0:T(8,128)(2,1)} %bitcast.13), custom_call_target="tpu_custom_call" | custom-call | tf_op jit(solution)/shard_map/fetch_rows/pallas_call | solution.py:385
  72.5 3.5 %all-to-all-done.2.rows_ref = bf16[8,4,2560]{2,1,0:T(4,128)(2,1)S(1)} async-done(((bf16[8,4,2560]{2,1,0:T(4,128)(2,1)}), bf16[8,4,2560]{2,1,0:T(4,128)(2,1)S(1)}, u32[]{:S(2)}, u32[]{:S(2)}) %all-to-all-start.2) | async-done | bytes 163872 | tf_op jit(solution)/shard_map/all_to_all | solution.py:397
  76.1 0.6 project_out.1.first_ref
  76.6 0.4 collective-permute-start
  77.0 0.7 collective-permute-start.1
  77.7 2.3 %collective-permute-start.2 = (bf16[32,320]{1,0:T(8,128)(2,1)S(1)}, bf16[32,320]{1,0:T(8,128)(2,1)S(1)}, u32[]{:S(2)}, u32[]{:S(2)}) collective-permute-start(bf16[32,320]{1,0:T(8,128)(2,1)S(1)} %project_out.1.first_ref), channel_id=1, source_target_pairs={{0,4},{1,5},{2,6},{3,7},{4,0},{5,1},{6,2},{7,3},{8,12},{9,13},{10,... | collective-permute-start | bytes 61448 | tf_op jit(solution)/shard_map/ppermute | solution.py:402
  80.0 2.1 %fetch_rows.5 = (bf16[128,2560]{1,0:T(8,128)(2,1)S(1)}, bf16[128,2560]{1,0:T(8,128)(2,1)S(1)}, bf16[128,2560]{1,0:T(8,128)(2,1)S(1)}, f32[8,128]{1,0:T(8,128)}) custom-call(bf16[32,4,2688]{2,1,0:T(4,128)(2,1)} %attend_pages.1.refs_0_, bf16[480,2560]{1,0:T(8,128)(2,1)} %bitcast.9, bf16[480,2560]{1,0:T(8,128)(2,1)} %bitcast.11, bf16[480,2560]{1,0:T(8,128)(2,1)} %refs_8_.1), custom_call_target="tpu_custom_call" | custom-call | tf_op jit(solution)/shard_map/fetch_rows/pallas_call | solution.py:385
  82.1 0.0 collective-permute-done.second_ref
  82.1 0.0 collective-permute-done.1.third_ref
  82.1 0.0 collective-permute-done.2.fourth_ref
  82.2 2.2 %collective-permute-start.3 = (bf16[4,32,320]{2,1,0:T(8,128)(2,1)S(1)}, bf16[4,32,320]{2,1,0:T(8,128)(2,1)S(1)}, u32[]{:S(2)}, u32[]{:S(2)}) collective-permute-start(bf16[4,32,320]{2,1,0:T(8,128)(2,1)S(1)} %stack_blocks.1.refs_0_), channel_id=1, source_target_pairs={{0,1},{1,0},{2,3},{3,2},{4,5},{5,4},{6,7},{7,6},{8,9},{9,8},{10,11... | collective-permute-start | bytes 245768 | tf_op jit(solution)/shard_map/ppermute | solution.py:402
  84.4 0.0 copy-done.4
  84.4 0.9 collective-permute-done.3.refs_1_
  85.3 3.7 %feed_forward.1 = (f32[32,1280]{1,0:T(8,128)S(1)}, bf16[32,1280]{1,0:T(8,128)(2,1)S(1)}, bf16[32,1280]{1,0:T(8,128)(2,1)S(1)}) custom-call(s32[1]{0:T(128)} %bitcast.3.place_ref, bf16[4,32,320]{2,1,0:T(8,128)(2,1)S(1)} %stack_blocks.1.refs_0_, bf16[4,32,320]{2,1,0:T(8,128)(2,1)S(1)} %collective-permute-done.3.refs_1_, f32[1,2560]{1,0:T(1,128)S(1)} %reshape.61.refs_2_, ...), custom_call_target="tpu_custom_call" | custom-call | tf_op jit(solution)/shard_map/feed_forward/pallas_call | solution.py:360
  89.0 0.0 copy-start.5
  89.0 0.4 collective-permute-start.4
  89.4 0.9 collective-permute-done.4.got_ref
  90.4 1.1 %collective-permute-start.5 = (bf16[32,1280]{1,0:T(8,128)(2,1)S(1)}, bf16[32,1280]{1,0:T(8,128)(2,1)S(1)}, u32[]{:S(2)}, u32[]{:S(2)}) collective-permute-start(bf16[32,1280]{1,0:T(8,128)(2,1)S(1)} %add_pair.1), channel_id=1, source_target_pairs={{0,2},{1,3},{2,0},{3,1},{4,6},{5,7},{6,4},{7,5},{8,10},{9,11},{10,... | collective-permute-start | bytes 245768 | tf_op jit(solution)/shard_map/ppermute | solution.py:402
  91.5 1.8 %collective-permute-start.6 = (bf16[32,1280]{1,0:T(8,128)(2,1)S(1)}, bf16[32,1280]{1,0:T(8,128)(2,1)S(1)}, u32[]{:S(2)}, u32[]{:S(2)}) collective-permute-start(bf16[32,1280]{1,0:T(8,128)(2,1)S(1)} %add_pair.1), channel_id=1, source_target_pairs={{0,6},{1,7},{2,4},{3,5},{4,2},{5,3},{6,0},{7,1},{8,14},{9,15},{10,... | collective-permute-start | bytes 245768 | tf_op jit(solution)/shard_map/ppermute | solution.py:402
  93.3 0.6 collective-permute-start.7
  93.9 1.8 %fetch_half.1 = (bf16[1152,384]{1,0:T(8,128)(2,1)S(1)}, f32[8,128]{1,0:T(8,128)}) custom-call(s32[1]{0:T(128)} %bitcast.3.place_ref, bf16[2560,384]{1,0:T(8,128)(2,1)} %far_ref.7), custom_call_target="tpu_custom_call" | custom-call | tf_op jit(solution)/shard_map/fetch_half/pallas_call | solution.py:526
  95.6 0.0 collective-permute-done.5.first_ref
  95.7 0.3 collective-permute-done.6.second_ref
  96.0 2.1 %collective-permute-done.7.third_ref = bf16[32,1280]{1,0:T(8,128)(2,1)S(1)} collective-permute-done((bf16[32,1280]{1,0:T(8,128)(2,1)S(1)}, bf16[32,1280]{1,0:T(8,128)(2,1)S(1)}, u32[]{:S(2)}, u32[]{:S(2)}) %collective-permute-start.7) | collective-permute-done | bytes 81952 | tf_op jit(solution)/shard_map/ppermute | solution.py:402
  98.1 0.1 add_chips.1.own_ref
  98.1 2.2 %collective-permute-start.8 = (bf16[32,1280]{1,0:T(8,128)(2,1)S(1)}, bf16[32,1280]{1,0:T(8,128)(2,1)S(1)}, u32[]{:S(2)}, u32[]{:S(2)}) collective-permute-start(bf16[32,1280]{1,0:T(8,128)(2,1)S(1)} %add_chips.1.own_ref), channel_id=1, source_target_pairs={{0,1},{1,0},{2,3},{3,2},{4,5},{5,4},{6,7},{7,6},{8,9},{9,8},{10,11... | collective-permute-start | bytes 245768 | tf_op jit(solution)/shard_map/ppermute | solution.py:402
  100.3 1.3 %project_own.1 = (f32[32,384]{1,0:T(8,128)S(1)}, f32[32,128]{1,0:T(8,128)S(1)}, bf16[1152,384]{1,0:T(8,128)(2,1)S(1)}) custom-call(s32[1]{0:T(128)} %bitcast.3.place_ref, bf16[32,1280]{1,0:T(8,128)(2,1)S(1)} %add_chips.1.own_ref, f32[2,1,1280]{2,1,0:T(1,128)S(1)} %reshape.62.gain_ref, bf16[1152,384]{1,0:T(8,128)(2,1)S(1)} %get-tuple-element.39.front_ref, ...), custom_call_target="tpu_custom_call" | custom-call | tf_op jit(solution)/shard_map/project_own/pallas_call | solution.py:360
  101.6 0.0 collective-permute-done.8.other_ref
  101.6 1.7 %project_other.1 = (bf16[32,320]{1,0:T(8,128)(2,1)}, bf16[32,384]{1,0:T(8,128)(2,1)}) custom-call(s32[1]{0:T(128)} %bitcast.3.place_ref, bf16[32,1280]{1,0:T(8,128)(2,1)S(1)} %add_chips.1.own_ref, bf16[32,1280]{1,0:T(8,128)(2,1)S(1)} %collective-permute-done.8.other_ref, f32[2,1,1280]{2,1,0:T(1,128)S(1)} %reshape.62.gain_ref, ...), custom_call_target="tpu_custom_call" | custom-call | tf_op jit(solution)/shard_map/project_other/pallas_call | solution.py:360
  (13 shorter events, 0.1 us)
Async XLA Ops:
  0.6 17.0 %copy-start = (s32[256,128]{1,0:T(8,128)S(1)}, s32[256,128]{1,0:T(8,128)}, u32[]{:S(2)}) copy-start(s32[256,128]{1,0:T(8,128)} %param.17) | copy-start | bytes 393220
  2.3 28.3 %all-to-all-start = ((bf16[32,4,2560]{2,1,0:T(4,128)(2,1)}), bf16[32,4,2560]{2,1,0:T(4,128)(2,1)S(1)}, u32[]{:S(2)}, u32[]{:S(2)}) async-start(bf16[32,4,2560]{2,1,0:T(4,128)(2,1)} %copy_queries.1.refs_0_), calls=%async_computation | async-start | bytes 1310720 | tf_op jit(solution)/shard_map/all_to_all | solution.py:397
  30.6 15.0 %copy-start.1 = (bf16[4,2560]{1,0:T(4,128)(2,1)S(1)}, bf16[4,2560]{1,0:T(4,128)(2,1)}, u32[]{:S(2)}) copy-start(bf16[4,2560]{1,0:T(4,128)(2,1)} %queries_ref.3) | copy-start | bytes 61444
  30.6 15.0 %copy-start.3 = (bf16[4,512]{1,0:T(4,128)(2,1)S(1)}, bf16[4,512]{1,0:T(4,128)(2,1)}, u32[]{:S(2)}) copy-start(bf16[4,512]{1,0:T(4,128)(2,1)} %new_ref.1) | copy-start | bytes 12292
  34.5 41.6 %copy-start.2 = (bf16[32,320]{1,0:T(8,128)(2,1)S(1)}, bf16[32,320]{1,0:T(8,128)(2,1)}, u32[]{:S(2)}) copy-start(bf16[32,320]{1,0:T(8,128)(2,1)} %residual_ref.1) | copy-start | bytes 61444
  34.5 25.7 %all-to-all-start.1 = ((bf16[32,4,2688]{2,1,0:T(4,128)(2,1)}), bf16[32,4,2688]{2,1,0:T(4,128)(2,1)S(1)}, u32[]{:S(2)}, u32[]{:S(2)}) async-start(bf16[32,4,2688]{2,1,0:T(4,128)(2,1)} %attend_pages.1.refs_0_), calls=%async_computation.1 | async-start | bytes 1376256 | tf_op jit(solution)/shard_map/all_to_all | solution.py:397
  61.1 14.9 %all-to-all-start.2 = ((bf16[8,4,2560]{2,1,0:T(4,128)(2,1)}), bf16[8,4,2560]{2,1,0:T(4,128)(2,1)S(1)}, u32[]{:S(2)}, u32[]{:S(2)}) async-start(bf16[8,4,2560]{2,1,0:T(4,128)(2,1)} %get-tuple-element.29), calls=%async_computation.2 | async-start | bytes 327680 | tf_op jit(solution)/shard_map/all_to_all | solution.py:397
  76.6 5.5 %collective-permute-start = (bf16[32,320]{1,0:T(8,128)(2,1)S(1)}, bf16[32,320]{1,0:T(8,128)(2,1)S(1)}, u32[]{:S(2)}, u32[]{:S(2)}) collective-permute-start(bf16[32,320]{1,0:T(8,128)(2,1)S(1)} %project_out.1.first_ref), channel_id=1, source_target_pairs={{0,2},{1,3},{2,0},{3,1},{4,6},{5,7},{6,4},{7,5},{8,10},{9,11},{10,... | collective-permute-start | bytes 61448 | tf_op jit(solution)/shard_map/ppermute | solution.py:402
  77.0 5.1 %collective-permute-start.1 = (bf16[32,320]{1,0:T(8,128)(2,1)S(1)}, bf16[32,320]{1,0:T(8,128)(2,1)S(1)}, u32[]{:S(2)}, u32[]{:S(2)}) collective-permute-start(bf16[32,320]{1,0:T(8,128)(2,1)S(1)} %project_out.1.first_ref), channel_id=1, source_target_pairs={{0,6},{1,7},{2,4},{3,5},{4,2},{5,3},{6,0},{7,1},{8,14},{9,15},{10,... | collective-permute-start | bytes 61448 | tf_op jit(solution)/shard_map/ppermute | solution.py:402
  77.7 4.4 %collective-permute-start.2 = (bf16[32,320]{1,0:T(8,128)(2,1)S(1)}, bf16[32,320]{1,0:T(8,128)(2,1)S(1)}, u32[]{:S(2)}, u32[]{:S(2)}) collective-permute-start(bf16[32,320]{1,0:T(8,128)(2,1)S(1)} %project_out.1.first_ref), channel_id=1, source_target_pairs={{0,4},{1,5},{2,6},{3,7},{4,0},{5,1},{6,2},{7,3},{8,12},{9,13},{10,... | collective-permute-start | bytes 61448 | tf_op jit(solution)/shard_map/ppermute | solution.py:402
  80.0 4.4 %copy-start.4 = (f32[2560]{0:T(1024)S(1)}, f32[2560]{0:T(1024)}, u32[]{:S(2)}) copy-start(f32[2560]{0:T(1024)} %param.20) | copy-start | bytes 30724
  82.2 3.2 %collective-permute-start.3 = (bf16[4,32,320]{2,1,0:T(8,128)(2,1)S(1)}, bf16[4,32,320]{2,1,0:T(8,128)(2,1)S(1)}, u32[]{:S(2)}, u32[]{:S(2)}) collective-permute-start(bf16[4,32,320]{2,1,0:T(8,128)(2,1)S(1)} %stack_blocks.1.refs_0_), channel_id=1, source_target_pairs={{0,1},{1,0},{2,3},{3,2},{4,5},{5,4},{6,7},{7,6},{8,9},{9,8},{10,11... | collective-permute-start | bytes 245768 | tf_op jit(solution)/shard_map/ppermute | solution.py:402
  89.0 11.3 %copy-start.5 = (f32[2560]{0:T(1024)S(1)}, f32[2560]{0:T(1024)}, u32[]{:S(2)}) copy-start(f32[2560]{0:T(1024)} %param.24) | copy-start | bytes 30724
  89.0 1.4 %collective-permute-start.4 = (bf16[32,1280]{1,0:T(8,128)(2,1)S(1)}, bf16[32,1280]{1,0:T(8,128)(2,1)S(1)}, u32[]{:S(2)}, u32[]{:S(2)}) collective-permute-start(bf16[32,1280]{1,0:T(8,128)(2,1)S(1)} %get-tuple-element.36), channel_id=1, source_target_pairs={{0,1},{1,0},{2,3},{3,2},{4,5},{5,4},{6,7},{7,6},{8,9},{9,8},{10,11... | collective-permute-start | bytes 245768 | tf_op jit(solution)/shard_map/ppermute | solution.py:402
  90.4 5.3 %collective-permute-start.5 = (bf16[32,1280]{1,0:T(8,128)(2,1)S(1)}, bf16[32,1280]{1,0:T(8,128)(2,1)S(1)}, u32[]{:S(2)}, u32[]{:S(2)}) collective-permute-start(bf16[32,1280]{1,0:T(8,128)(2,1)S(1)} %add_pair.1), channel_id=1, source_target_pairs={{0,2},{1,3},{2,0},{3,1},{4,6},{5,7},{6,4},{7,5},{8,10},{9,11},{10,... | collective-permute-start | bytes 245768 | tf_op jit(solution)/shard_map/ppermute | solution.py:402
  91.5 4.5 %collective-permute-start.6 = (bf16[32,1280]{1,0:T(8,128)(2,1)S(1)}, bf16[32,1280]{1,0:T(8,128)(2,1)S(1)}, u32[]{:S(2)}, u32[]{:S(2)}) collective-permute-start(bf16[32,1280]{1,0:T(8,128)(2,1)S(1)} %add_pair.1), channel_id=1, source_target_pairs={{0,6},{1,7},{2,4},{3,5},{4,2},{5,3},{6,0},{7,1},{8,14},{9,15},{10,... | collective-permute-start | bytes 245768 | tf_op jit(solution)/shard_map/ppermute | solution.py:402
  93.3 4.8 %collective-permute-start.7 = (bf16[32,1280]{1,0:T(8,128)(2,1)S(1)}, bf16[32,1280]{1,0:T(8,128)(2,1)S(1)}, u32[]{:S(2)}, u32[]{:S(2)}) collective-permute-start(bf16[32,1280]{1,0:T(8,128)(2,1)S(1)} %add_pair.1), channel_id=1, source_target_pairs={{0,4},{1,5},{2,6},{3,7},{4,0},{5,1},{6,2},{7,3},{8,12},{9,13},{10,... | collective-permute-start | bytes 245768 | tf_op jit(solution)/shard_map/ppermute | solution.py:402
  98.1 3.4 %collective-permute-start.8 = (bf16[32,1280]{1,0:T(8,128)(2,1)S(1)}, bf16[32,1280]{1,0:T(8,128)(2,1)S(1)}, u32[]{:S(2)}, u32[]{:S(2)}) collective-permute-start(bf16[32,1280]{1,0:T(8,128)(2,1)S(1)} %add_chips.1.own_ref), channel_id=1, source_target_pairs={{0,1},{1,0},{2,3},{3,2},{4,5},{5,4},{6,7},{7,6},{8,9},{9,8},{10,11... | collective-permute-start | bytes 245768 | tf_op jit(solution)/shard_map/ppermute | solution.py:402

commit v7 on v6

--- a/solution.py
+++ b/solution.py
@@ -148,7 +148,7 @@
         out_ref[source, :, width:] = packed.astype(BF16)
 
 
-def merge_new(holder_ref, got_ref, max_ref, sum_ref, acc_ref, attended_ref, spread_ref):
+def merge_new(holder_ref, got_ref, max_ref, sum_ref, acc_ref, attended_ref):
     holder = holder_ref[0]
     head_dim = 256
     width = attended_ref.shape[1]
@@ -168,15 +168,20 @@
             + acc_ref[:, span] * new_factor[:, head : head + 1]
         ).astype(BF16)
         attended_ref[:, span] = rows
-        for place in range(spread_ref.shape[0]):
-            spread_ref[place, :, span] = rows
-
-
-def project_out(rows_ref, residual_ref, weight_ref, out_ref):
-    places = rows_ref.shape[0]
-    rows = jnp.concatenate([rows_ref[place].astype(F32) for place in range(places)], axis=0).astype(BF16)
-    attention_out = lax.dot_general(rows, weight_ref[...], LAST, preferred_element_type=F32)
-    out_ref[...] = (residual_ref[...].astype(F32) + attention_out).astype(BF16)
+
+
+def project_out(place_ref, mine_ref, theirs_ref, residual_ref, *refs):
+    weight_refs, out_ref, rows_ref = refs[:-2], refs[-2], refs[-1]
+    for index, distance in enumerate(DISTANCES):
+        rows_ref[place_ref[0] ^ distance] = mine_ref[index].astype(F32)
+        rows_ref[place_ref[0] ^ distance ^ 1] = theirs_ref[index].astype(F32)
+    rows = jnp.concatenate([rows_ref[place] for place in range(rows_ref.shape[0])], axis=0).astype(BF16)
+    start = 0
+    for weight_ref in weight_refs:
+        span = slice(start, start + weight_ref.shape[0])
+        attention_out = lax.dot_general(rows, weight_ref[...], LAST, preferred_element_type=F32)
+        out_ref[:, span] = (residual_ref[:, span].astype(F32) + attention_out).astype(BF16)
+        start += weight_ref.shape[0]
 
 
 def stack_blocks(first_ref, second_ref, third_ref, fourth_ref, fetched_ref, out_ref):
@@ -370,12 +375,18 @@
     )(*scalars, *[near(array) for array in arrays], *far)
 
 
-def fetch(parts, after):
+def fetch(parts, after, carried=None):
+    extra = [] if carried is None else [carried]
+    count = len(parts)
+
     def fetch_rows(*refs):
-        fars, outs, copied = refs[1 : 1 + len(parts)], refs[1 + len(parts) : 1 + 2 * len(parts)], refs[-1]
+        fars, refs = refs[1 : 1 + count], refs[1 + count :]
+        if extra:
+            refs[1 + count + 1][...] = refs[0][...]
+            refs = refs[1:]
         copies = [
-            pltpu.make_async_copy(far.at[pl.ds(0, out.shape[0])], out, copied.at[index])
-            for index, (far, out) in enumerate(zip(fars, outs))
+            pltpu.make_async_copy(far.at[pl.ds(start, rows)], out, refs[-1].at[index])
+            for index, (far, out, (_, rows, start)) in enumerate(zip(fars, refs, parts))
         ]
         for copy in copies:
             copy.start()
@@ -384,13 +395,14 @@
 
     return pl.pallas_call(
         fetch_rows,
-        out_shape=[pltpu.VMEM((rows,) + far.shape[1:], far.dtype) for far, rows in parts]
-        + [jax.ShapeDtypeStruct((8, 128), F32)],
-        in_specs=[FAR] * (len(parts) + 1),
-        out_specs=[VMEM] * (len(parts) + 1),
-        scratch_shapes=[pltpu.SemaphoreType.DMA((len(parts),))],
+        out_shape=[pltpu.VMEM((rows,) + far.shape[1:], far.dtype) for far, rows, _ in parts]
+        + [jax.ShapeDtypeStruct((8, 128), F32)]
+        + [jax.ShapeDtypeStruct(array.shape, array.dtype) for array in extra],
+        in_specs=[FAR] * (count + 1) + [VMEM] * len(extra),
+        out_specs=[VMEM] * (count + 1 + len(extra)),
+        scratch_shapes=[pltpu.SemaphoreType.DMA((count,))],
         name="fetch_rows",
-    )(after, *[far for far, _ in parts])
+    )(after, *[far for far, _, _ in parts], *[near(array) for array in extra])
 
 
 def exchange(copies, axis):
@@ -400,6 +412,14 @@
 def partner(block, distance):
     count = lax.axis_size("mlp")
     return lax.ppermute(block, "mlp", [(i, i ^ distance) for i in range(count)])
+
+
+def gather(block, fetched):
+    others = [partner(block, distance) for distance in DISTANCES[1:]]
+    (mine,) = call(
+        stack_blocks, [((4,) + block.shape, BF16, True)], [], [block, *others], [fetched]
+    )
+    return mine, partner(mine, 1)
 
 
 def shards(
@@ -464,7 +484,7 @@
         [queries, new_kv],
     )
     near_slots = 11
-    cache_front, _ = fetch([(kv_cache, near_slots)], sent)
+    cache_front, _ = fetch([(kv_cache, near_slots, 0)], sent)
     (held,) = call(
         attend_pages,
         [((seq_count, token_count, width + 128), BF16, False)],
@@ -478,31 +498,26 @@
         [pltpu.SMEM((slot_count + 1,), jnp.int32)],
     )
     returned = exchange(held, "seq")
-    attended, spread = call(
+    (attended,) = call(
         merge_new,
-        [((token_count, width), BF16, False), ((mlp_count, token_count, width), BF16, True)],
+        [((token_count, width), BF16, True)],
         [holder],
         [returned, new_max, new_sum, new_acc],
     )
-    rows = exchange(spread, "mlp")
-    out_near, _ = fetch([(out_weight.T, part_width)], held)
+    place = mlp_place.astype(jnp.int32).reshape(1)
+    spans = [(128, 0), (128, 128), (64, 256)]
+    *out_near, fetched = fetch([(out_weight.T, rows, start) for rows, start in spans], held)
+    mine, theirs = gather(attended, fetched)
     (stream,) = call(
         project_out,
         [((row_count, part_width), BF16, True)],
-        [],
-        [rows, residual, out_near],
+        [place],
+        [mine, theirs, residual, *out_near],
+        scratch=[((mlp_count, token_count, width), F32)],
     )
     layers = [(gate_weight.T, NEAR), (up_weight.T, NEAR), (down_weight, NEAR)]
-    *front, fetched = fetch(layers, held)
-    (mine,) = call(
-        stack_blocks,
-        [((4, row_count, part_width), BF16, True)],
-        [],
-        [stream, *[partner(stream, distance) for distance in DISTANCES[1:]]],
-        [fetched],
-    )
-    theirs = partner(mine, 1)
-    place = mlp_place.astype(jnp.int32).reshape(1)
+    *front, fetched, attended_out = fetch([(far, rows, 0) for far, rows in layers], held, attended)
+    mine, theirs = gather(stream, fetched)
     keep, send, stream_half = call(
         feed_forward,
         [((row_count, half), F32, True), ((row_count, half), BF16, True), ((row_count, half), BF16, True)],
@@ -554,7 +569,7 @@
         [((half - near_rows, columns), BF16)],
         1,
     )
-    return (attended, shard_after, next_qkv)
+    return (attended_out, shard_after, next_qkv)
 
 
 def solution(mesh):

time: 104 us -> 103 us (level)
  waiting for transfers between devices: 34 us -> 32.5 us
    ppermute x9 -> x13, starting transfers between devices: 11.6 us -> 21.9 us  [partner(): return lax.ppermute(block, 'mlp', [(i, i ^ distance) for i in range(count)])]
    all_to_all x3 -> x2, starting transfers between devices: 29.6 us -> 20.3 us  [exchange(): return lax.all_to_all(copies, axis, split_axis=0, concat_axis=0, tiled=True)]
    all_to_all x3 -> x2, waiting for transfers between devices: 29.7 us -> 26.2 us  [exchange(): return lax.all_to_all(copies, axis, split_axis=0, concat_axis=0, tiled=True)]
    ppermute x9 -> x13, waiting for transfers between devices: 4.27 us -> 6.29 us  [partner(): return lax.ppermute(block, 'mlp', [(i, i ^ distance) for i in range(count)])]
    pallas_call x10 -> x11, Pallas kernels: 12.4 us -> 11.7 us  [call(): pl.pallas_call(body, out_shape=[pltpu.VMEM(shape, dtype) if stays else ja...]
  transfers between devices with their start and end apart: 12 -> 15, of which waited for: 7 -> 7; matrix products, arithmetic and copies ran while one was open for 3% -> 3% of each run, Pallas kernels for 9% -> 9%
where the time goes in v7:
time: 103 us; the launch traced here: 102 us
  starting transfers between devices  42.2 us (41%)
  waiting for transfers between devices  32.5 us (32%)
  Pallas kernels  21.3 us (21%)
  between operations  2.83 us (3%)
  other arithmetic  1.72 us (2%)
  local copies, waits for them, and re-layouts  1.52 us (1%)
    all_to_all x2, waiting for transfers between devices, exchange(): return lax.all_to_all(copies, axis, split_axis=0, concat_axis=0, tiled=True)  26.2 us
    ppermute x13, starting transfers between devices, partner(): return lax.ppermute(block, 'mlp', [(i, i ^ distance) for i in range(count)])  21.9 us
    all_to_all x2, starting transfers between devices, exchange(): return lax.all_to_all(copies, axis, split_axis=0, concat_axis=0, tiled=True)  20.3 us
    pallas_call x11, Pallas kernels, call(): pl.pallas_call(body, out_shape=[pltpu.VMEM(shape, dtype) if stays else ja...  11.7 us
    ppermute x13, waiting for transfers between devices, partner(): return lax.ppermute(block, 'mlp', [(i, i ^ distance) for i in range(count)])  6.29 us
    pallas_call x3, Pallas kernels, fetch(): pl.pallas_call(fetch_rows, out_shape=[pltpu.VMEM((rows,) + far.shape[1:],...  6.09 us
  transfers between devices with their start and end apart: 15, of which 7 were waited for; matrix products, arithmetic and copies ran while one was open for 3% of the time, Pallas kernels for 9%

profile of v7, /device:TPU:1, one launch (start us, length us, event | category | flops | bytes accessed | tf_op | source)
XLA Modules:
  0.0 102.0 jit_solution(14020821842580575909)
XLA Ops:
  0.6 0.0 copy-start
  0.6 1.7 %copy_queries.1.refs_0_ = bf16[32,4,2560]{2,1,0:T(4,128)(2,1)} custom-call(bf16[4,2560]{1,0:T(4,128)(2,1)} %queries_ref.3), custom_call_target="tpu_custom_call" | custom-call | tf_op jit(solution)/shard_map/copy_queries/pallas_call | solution.py:453
  2.3 11.9 %all-to-all-start = ((bf16[32,4,2560]{2,1,0:T(4,128)(2,1)}), bf16[32,4,2560]{2,1,0:T(4,128)(2,1)S(1)}, u32[]{:S(2)}, u32[]{:S(2)}) async-start(bf16[32,4,2560]{2,1,0:T(4,128)(2,1)} %copy_queries.1.refs_0_), calls=%async_computation | async-start | bytes 1310720 | tf_op jit(solution)/shard_map/all_to_all | solution.py:409
  14.2 0.8 reshape.58
  15.0 2.0 %fetch_rows.3 = (bf16[11,128,512]{2,1,0:T(8,128)(2,1)S(1)}, f32[8,128]{1,0:T(8,128)}) custom-call(bf16[32,4,2560]{2,1,0:T(4,128)(2,1)} %copy_queries.1.refs_0_, bf16[17,128,512]{2,1,0:T(8,128)(2,1)} %far_ref.4), custom_call_target="tpu_custom_call" | custom-call | tf_op jit(solution)/shard_map/fetch_rows/pallas_call | solution.py:396
  16.9 0.7 dynamic-slice_reduce_fusion.length_ref
  17.7 0.1 add_add_fusion
  17.7 1.0 select_reduce_fusion.code_ref
  18.7 11.8 %all-to-all-done.rows_ref = bf16[32,4,2560]{2,1,0:T(4,128)(2,1)S(1)} async-done(((bf16[32,4,2560]{2,1,0:T(4,128)(2,1)}), bf16[32,4,2560]{2,1,0:T(4,128)(2,1)S(1)}, u32[]{:S(2)}, u32[]{:S(2)}) %all-to-all-start) | async-done | bytes 655392 | tf_op jit(solution)/shard_map/all_to_all | solution.py:409
  30.6 3.9 %attend_pages.1.refs_0_ = bf16[32,4,2688]{2,1,0:T(4,128)(2,1)} custom-call(s32[17]{0:T(128)} %select_reduce_fusion.code_ref, s32[32]{0:T(128)} %dynamic-slice_reduce_fusion.length_ref, bf16[32,4,2560]{2,1,0:T(4,128)(2,1)S(1)} %all-to-all-done.rows_ref, bf16[11,128,512]{2,1,0:T(8,128)(2,1)S(1)} %get-tuple-element.26.front_ref, bf16[17,128,512]{2,1,0:T(8,128)(2,1)} %far_ref.4), custom_call_target="tpu_custom_call" | custom-call | tf_op jit(solution)/shard_map/attend_pages/pallas_call | solution.py:365
  34.5 8.4 %all-to-all-start.1 = ((bf16[32,4,2688]{2,1,0:T(4,128)(2,1)}), bf16[32,4,2688]{2,1,0:T(4,128)(2,1)S(1)}, u32[]{:S(2)}, u32[]{:S(2)}) async-start(bf16[32,4,2688]{2,1,0:T(4,128)(2,1)} %attend_pages.1.refs_0_), calls=%async_computation.1 | async-start | bytes 1376256 | tf_op jit(solution)/shard_map/all_to_all | solution.py:409
  42.9 0.6 fusion
  45.5 0.3 attend_new.1
  45.9 14.3 %all-to-all-done.1.got_ref = bf16[32,4,2688]{2,1,0:T(4,128)(2,1)S(1)} async-done(((bf16[32,4,2688]{2,1,0:T(4,128)(2,1)}), bf16[32,4,2688]{2,1,0:T(4,128)(2,1)S(1)}, u32[]{:S(2)}, u32[]{:S(2)}) %all-to-all-start.1) | async-done | bytes 688160 | tf_op jit(solution)/shard_map/all_to_all | solution.py:409
  60.2 0.2 merge_new.1.refs_4_.first_ref
  60.4 1.4 %collective-permute-start = (bf16[4,2560]{1,0:T(4,128)(2,1)S(1)}, bf16[4,2560]{1,0:T(4,128)(2,1)S(1)}, u32[]{:S(2)}, u32[]{:S(2)}) collective-permute-start(bf16[4,2560]{1,0:T(4,128)(2,1)S(1)} %merge_new.1.refs_4_.first_ref), channel_id=1, source_target_pairs={{0,2},{1,3},{2,0},{3,1},{4,6},{5,7},{6,4},{7,5},{8,10},{9,11},{10,... | collective-permute-start | bytes 61448 | tf_op jit(solution)/shard_map/ppermute | solution.py:414
  61.8 1.9 %collective-permute-start.1 = (bf16[4,2560]{1,0:T(4,128)(2,1)S(1)}, bf16[4,2560]{1,0:T(4,128)(2,1)S(1)}, u32[]{:S(2)}, u32[]{:S(2)}) collective-permute-start(bf16[4,2560]{1,0:T(4,128)(2,1)S(1)} %merge_new.1.refs_4_.first_ref), channel_id=1, source_target_pairs={{0,6},{1,7},{2,4},{3,5},{4,2},{5,3},{6,0},{7,1},{8,14},{9,15},{10,... | collective-permute-start | bytes 61448 | tf_op jit(solution)/shard_map/ppermute | solution.py:414
  63.7 0.7 collective-permute-start.2
  64.4 2.0 %fetch_rows.5 = (bf16[128,2560]{1,0:T(8,128)(2,1)S(1)}, bf16[128,2560]{1,0:T(8,128)(2,1)S(1)}, bf16[64,2560]{1,0:T(8,128)(2,1)S(1)}, f32[8,128]{1,0:T(8,128)}) custom-call(bf16[32,4,2688]{2,1,0:T(4,128)(2,1)} %attend_pages.1.refs_0_, bf16[320,2560]{1,0:T(8,128)(2,1)} %bitcast.9, bf16[320,2560]{1,0:T(8,128)(2,1)} %bitcast.10, bf16[320,2560]{1,0:T(8,128)(2,1)} %bitcast.11), custom_call_target="tpu_custom_call" | custom-call | tf_op jit(solution)/shard_map/fetch_rows/pallas_call | solution.py:396
  66.4 0.0 collective-permute-done.second_ref
  66.5 0.0 collective-permute-done.1.third_ref
  66.5 1.4 %collective-permute-done.2.fourth_ref = bf16[4,2560]{1,0:T(4,128)(2,1)S(1)} collective-permute-done((bf16[4,2560]{1,0:T(4,128)(2,1)S(1)}, bf16[4,2560]{1,0:T(4,128)(2,1)S(1)}, u32[]{:S(2)}, u32[]{:S(2)}) %collective-permute-start.2) | collective-permute-done | bytes 20512 | tf_op jit(solution)/shard_map/ppermute | solution.py:414
  67.9 6.6 %collective-permute-start.3 = (bf16[4,4,2560]{2,1,0:T(4,128)(2,1)S(1)}, bf16[4,4,2560]{2,1,0:T(4,128)(2,1)S(1)}, u32[]{:S(2)}, u32[]{:S(2)}) collective-permute-start(bf16[4,4,2560]{2,1,0:T(4,128)(2,1)S(1)} %stack_blocks.2.mine_ref), channel_id=1, source_target_pairs={{0,1},{1,0},{2,3},{3,2},{4,5},{5,4},{6,7},{7,6},{8,9},{9,8},{10,11... | collective-permute-start | bytes 245768 | tf_op jit(solution)/shard_map/ppermute | solution.py:414
  74.5 0.9 collective-permute-done.3.theirs_ref
  75.4 0.6 project_out.1.first_ref
  76.0 0.5 collective-permute-start.4
  76.5 0.5 collective-permute-start.5
  77.0 2.4 %collective-permute-start.6 = (bf16[32,320]{1,0:T(8,128)(2,1)S(1)}, bf16[32,320]{1,0:T(8,128)(2,1)S(1)}, u32[]{:S(2)}, u32[]{:S(2)}) collective-permute-start(bf16[32,320]{1,0:T(8,128)(2,1)S(1)} %project_out.1.first_ref), channel_id=1, source_target_pairs={{0,4},{1,5},{2,6},{3,7},{4,0},{5,1},{6,2},{7,3},{8,12},{9,13},{10,... | collective-permute-start | bytes 61448 | tf_op jit(solution)/shard_map/ppermute | solution.py:414
  79.4 2.1 %fetch_rows.4 = (bf16[128,2560]{1,0:T(8,128)(2,1)S(1)}, bf16[128,2560]{1,0:T(8,128)(2,1)S(1)}, bf16[128,2560]{1,0:T(8,128)(2,1)S(1)}, f32[8,128]{1,0:T(8,128)}, bf16[4,2560]{1,0:T(4,128)(2,1)}) custom-call(bf16[32,4,2688]{2,1,0:T(4,128)(2,1)} %attend_pages.1.refs_0_, bf16[480,2560]{1,0:T(8,128)(2,1)} %bitcast.12, bf16[480,2560]{1,0:T(8,128)(2,1)} %bitcast.14, ...), custom_call_target="tpu_custom_call" | custom-call | tf_op jit(solution)/shard_map/fetch_rows/pallas_call | solution.py:396
  81.5 0.0 collective-permute-done.4.second_ref
  81.5 0.0 collective-permute-done.5.third_ref
  81.6 1.6 %collective-permute-start.7 = (bf16[4,32,320]{2,1,0:T(8,128)(2,1)S(1)}, bf16[4,32,320]{2,1,0:T(8,128)(2,1)S(1)}, u32[]{:S(2)}, u32[]{:S(2)}) collective-permute-start(bf16[4,32,320]{2,1,0:T(8,128)(2,1)S(1)} %stack_blocks.3.refs_0_), channel_id=1, source_target_pairs={{0,1},{1,0},{2,3},{3,2},{4,5},{5,4},{6,7},{7,6},{8,9},{9,8},{10,11... | collective-permute-start | bytes 245768 | tf_op jit(solution)/shard_map/ppermute | solution.py:414
  83.2 0.9 collective-permute-done.7.refs_1_
  84.2 3.7 %feed_forward.1 = (f32[32,1280]{1,0:T(8,128)S(1)}, bf16[32,1280]{1,0:T(8,128)(2,1)S(1)}, bf16[32,1280]{1,0:T(8,128)(2,1)S(1)}) custom-call(s32[1]{0:T(128)} %bitcast.5.place_ref, bf16[4,32,320]{2,1,0:T(8,128)(2,1)S(1)} %stack_blocks.3.refs_0_, bf16[4,32,320]{2,1,0:T(8,128)(2,1)S(1)} %collective-permute-done.7.refs_1_, f32[1,2560]{1,0:T(1,128)S(1)} %reshape.61.refs_2_, ...), custom_call_target="tpu_custom_call" | custom-call | tf_op jit(solution)/shard_map/feed_forward/pallas_call | solution.py:365
  87.8 0.0 copy-start.5
  87.8 0.4 collective-permute-start.8
  88.3 0.9 collective-permute-done.8.got_ref
  89.2 2.4 %collective-permute-start.10 = (bf16[32,1280]{1,0:T(8,128)(2,1)S(1)}, bf16[32,1280]{1,0:T(8,128)(2,1)S(1)}, u32[]{:S(2)}, u32[]{:S(2)}) collective-permute-start(bf16[32,1280]{1,0:T(8,128)(2,1)S(1)} %add_pair.1), channel_id=1, source_target_pairs={{0,6},{1,7},{2,4},{3,5},{4,2},{5,3},{6,0},{7,1},{8,14},{9,15},{10,... | collective-permute-start | bytes 245768 | tf_op jit(solution)/shard_map/ppermute | solution.py:414
  91.7 0.3 collective-permute-start.11
  92.0 0.6 collective-permute-start.9
  92.6 1.8 %fetch_half.1 = (bf16[1152,384]{1,0:T(8,128)(2,1)S(1)}, f32[8,128]{1,0:T(8,128)}) custom-call(s32[1]{0:T(128)} %bitcast.5.place_ref, bf16[2560,384]{1,0:T(8,128)(2,1)} %far_ref.7), custom_call_target="tpu_custom_call" | custom-call | tf_op jit(solution)/shard_map/fetch_half/pallas_call | solution.py:541
  94.3 2.1 %collective-permute-done.11.third_ref = bf16[32,1280]{1,0:T(8,128)(2,1)S(1)} collective-permute-done((bf16[32,1280]{1,0:T(8,128)(2,1)S(1)}, bf16[32,1280]{1,0:T(8,128)(2,1)S(1)}, u32[]{:S(2)}, u32[]{:S(2)}) %collective-permute-start.11) | collective-permute-done | bytes 81952 | tf_op jit(solution)/shard_map/ppermute | solution.py:414
  96.4 0.0 collective-permute-done.9.first_ref
  96.5 0.1 add_chips.1.own_ref
  96.5 2.5 %collective-permute-start.12 = (bf16[32,1280]{1,0:T(8,128)(2,1)S(1)}, bf16[32,1280]{1,0:T(8,128)(2,1)S(1)}, u32[]{:S(2)}, u32[]{:S(2)}) collective-permute-start(bf16[32,1280]{1,0:T(8,128)(2,1)S(1)} %add_chips.1.own_ref), channel_id=1, source_target_pairs={{0,1},{1,0},{2,3},{3,2},{4,5},{5,4},{6,7},{7,6},{8,9},{9,8},{10,11... | collective-permute-start | bytes 245768 | tf_op jit(solution)/shard_map/ppermute | solution.py:414
  99.1 1.3 %project_own.1 = (f32[32,384]{1,0:T(8,128)S(1)}, f32[32,128]{1,0:T(8,128)S(1)}, bf16[1152,384]{1,0:T(8,128)(2,1)S(1)}) custom-call(s32[1]{0:T(128)} %bitcast.5.place_ref, bf16[32,1280]{1,0:T(8,128)(2,1)S(1)} %add_chips.1.own_ref, f32[2,1,1280]{2,1,0:T(1,128)S(1)} %reshape.62.gain_ref, bf16[1152,384]{1,0:T(8,128)(2,1)S(1)} %get-tuple-element.43.front_ref, ...), custom_call_target="tpu_custom_call" | custom-call | tf_op jit(solution)/shard_map/project_own/pallas_call | solution.py:365
  100.3 0.0 collective-permute-done.12.other_ref
  100.3 1.7 %project_other.1 = (bf16[32,320]{1,0:T(8,128)(2,1)}, bf16[32,384]{1,0:T(8,128)(2,1)}) custom-call(s32[1]{0:T(128)} %bitcast.5.place_ref, bf16[32,1280]{1,0:T(8,128)(2,1)S(1)} %add_chips.1.own_ref, bf16[32,1280]{1,0:T(8,128)(2,1)S(1)} %collective-permute-done.12.other_ref, f32[2,1,1280]{2,1,0:T(1,128)S(1)} %reshape.62.gain_ref, ...), custom_call_target="tpu_custom_call" | custom-call | tf_op jit(solution)/shard_map/project_other/pallas_call | solution.py:365
  (20 shorter events, 0.1 us)
Async XLA Ops:
  0.6 17.0 %copy-start = (s32[256,128]{1,0:T(8,128)S(1)}, s32[256,128]{1,0:T(8,128)}, u32[]{:S(2)}) copy-start(s32[256,128]{1,0:T(8,128)} %param.17) | copy-start | bytes 393220
  2.3 28.3 %all-to-all-start = ((bf16[32,4,2560]{2,1,0:T(4,128)(2,1)}), bf16[32,4,2560]{2,1,0:T(4,128)(2,1)S(1)}, u32[]{:S(2)}, u32[]{:S(2)}) async-start(bf16[32,4,2560]{2,1,0:T(4,128)(2,1)} %copy_queries.1.refs_0_), calls=%async_computation | async-start | bytes 1310720 | tf_op jit(solution)/shard_map/all_to_all | solution.py:409
  30.6 14.9 %copy-start.1 = (bf16[4,2560]{1,0:T(4,128)(2,1)S(1)}, bf16[4,2560]{1,0:T(4,128)(2,1)}, u32[]{:S(2)}) copy-start(bf16[4,2560]{1,0:T(4,128)(2,1)} %queries_ref.3) | copy-start | bytes 61444
  30.6 15.0 %copy-start.3 = (bf16[4,512]{1,0:T(4,128)(2,1)S(1)}, bf16[4,512]{1,0:T(4,128)(2,1)}, u32[]{:S(2)}) copy-start(bf16[4,512]{1,0:T(4,128)(2,1)} %new_ref.1) | copy-start | bytes 12292
  34.5 25.7 %all-to-all-start.1 = ((bf16[32,4,2688]{2,1,0:T(4,128)(2,1)}), bf16[32,4,2688]{2,1,0:T(4,128)(2,1)S(1)}, u32[]{:S(2)}, u32[]{:S(2)}) async-start(bf16[32,4,2688]{2,1,0:T(4,128)(2,1)} %attend_pages.1.refs_0_), calls=%async_computation.1 | async-start | bytes 1376256 | tf_op jit(solution)/shard_map/all_to_all | solution.py:409
  60.4 6.0 %collective-permute-start = (bf16[4,2560]{1,0:T(4,128)(2,1)S(1)}, bf16[4,2560]{1,0:T(4,128)(2,1)S(1)}, u32[]{:S(2)}, u32[]{:S(2)}) collective-permute-start(bf16[4,2560]{1,0:T(4,128)(2,1)S(1)} %merge_new.1.refs_4_.first_ref), channel_id=1, source_target_pairs={{0,2},{1,3},{2,0},{3,1},{4,6},{5,7},{6,4},{7,5},{8,10},{9,11},{10,... | collective-permute-start | bytes 61448 | tf_op jit(solution)/shard_map/ppermute | solution.py:414
  61.8 4.6 %collective-permute-start.1 = (bf16[4,2560]{1,0:T(4,128)(2,1)S(1)}, bf16[4,2560]{1,0:T(4,128)(2,1)S(1)}, u32[]{:S(2)}, u32[]{:S(2)}) collective-permute-start(bf16[4,2560]{1,0:T(4,128)(2,1)S(1)} %merge_new.1.refs_4_.first_ref), channel_id=1, source_target_pairs={{0,6},{1,7},{2,4},{3,5},{4,2},{5,3},{6,0},{7,1},{8,14},{9,15},{10,... | collective-permute-start | bytes 61448 | tf_op jit(solution)/shard_map/ppermute | solution.py:414
  63.7 4.1 %collective-permute-start.2 = (bf16[4,2560]{1,0:T(4,128)(2,1)S(1)}, bf16[4,2560]{1,0:T(4,128)(2,1)S(1)}, u32[]{:S(2)}, u32[]{:S(2)}) collective-permute-start(bf16[4,2560]{1,0:T(4,128)(2,1)S(1)} %merge_new.1.refs_4_.first_ref), channel_id=1, source_target_pairs={{0,4},{1,5},{2,6},{3,7},{4,0},{5,1},{6,2},{7,3},{8,12},{9,13},{10,... | collective-permute-start | bytes 61448 | tf_op jit(solution)/shard_map/ppermute | solution.py:414
  64.4 11.0 %copy-start.2 = (bf16[32,320]{1,0:T(8,128)(2,1)S(1)}, bf16[32,320]{1,0:T(8,128)(2,1)}, u32[]{:S(2)}) copy-start(bf16[32,320]{1,0:T(8,128)(2,1)} %residual_ref.1) | copy-start | bytes 61444
  67.9 7.5 %collective-permute-start.3 = (bf16[4,4,2560]{2,1,0:T(4,128)(2,1)S(1)}, bf16[4,4,2560]{2,1,0:T(4,128)(2,1)S(1)}, u32[]{:S(2)}, u32[]{:S(2)}) collective-permute-start(bf16[4,4,2560]{2,1,0:T(4,128)(2,1)S(1)} %stack_blocks.2.mine_ref), channel_id=1, source_target_pairs={{0,1},{1,0},{2,3},{3,2},{4,5},{5,4},{6,7},{7,6},{8,9},{9,8},{10,11... | collective-permute-start | bytes 245768 | tf_op jit(solution)/shard_map/ppermute | solution.py:414
  76.0 5.5 %collective-permute-start.4 = (bf16[32,320]{1,0:T(8,128)(2,1)S(1)}, bf16[32,320]{1,0:T(8,128)(2,1)S(1)}, u32[]{:S(2)}, u32[]{:S(2)}) collective-permute-start(bf16[32,320]{1,0:T(8,128)(2,1)S(1)} %project_out.1.first_ref), channel_id=1, source_target_pairs={{0,2},{1,3},{2,0},{3,1},{4,6},{5,7},{6,4},{7,5},{8,10},{9,11},{10,... | collective-permute-start | bytes 61448 | tf_op jit(solution)/shard_map/ppermute | solution.py:414
  76.5 5.0 %collective-permute-start.5 = (bf16[32,320]{1,0:T(8,128)(2,1)S(1)}, bf16[32,320]{1,0:T(8,128)(2,1)S(1)}, u32[]{:S(2)}, u32[]{:S(2)}) collective-permute-start(bf16[32,320]{1,0:T(8,128)(2,1)S(1)} %project_out.1.first_ref), channel_id=1, source_target_pairs={{0,6},{1,7},{2,4},{3,5},{4,2},{5,3},{6,0},{7,1},{8,14},{9,15},{10,... | collective-permute-start | bytes 61448 | tf_op jit(solution)/shard_map/ppermute | solution.py:414
  77.0 4.5 %collective-permute-start.6 = (bf16[32,320]{1,0:T(8,128)(2,1)S(1)}, bf16[32,320]{1,0:T(8,128)(2,1)S(1)}, u32[]{:S(2)}, u32[]{:S(2)}) collective-permute-start(bf16[32,320]{1,0:T(8,128)(2,1)S(1)} %project_out.1.first_ref), channel_id=1, source_target_pairs={{0,4},{1,5},{2,6},{3,7},{4,0},{5,1},{6,2},{7,3},{8,12},{9,13},{10,... | collective-permute-start | bytes 61448 | tf_op jit(solution)/shard_map/ppermute | solution.py:414
  79.4 3.8 %copy-start.4 = (f32[2560]{0:T(1024)S(1)}, f32[2560]{0:T(1024)}, u32[]{:S(2)}) copy-start(f32[2560]{0:T(1024)} %param.20) | copy-start | bytes 30724
  81.6 2.6 %collective-permute-start.7 = (bf16[4,32,320]{2,1,0:T(8,128)(2,1)S(1)}, bf16[4,32,320]{2,1,0:T(8,128)(2,1)S(1)}, u32[]{:S(2)}, u32[]{:S(2)}) collective-permute-start(bf16[4,32,320]{2,1,0:T(8,128)(2,1)S(1)} %stack_blocks.3.refs_0_), channel_id=1, source_target_pairs={{0,1},{1,0},{2,3},{3,2},{4,5},{5,4},{6,7},{7,6},{8,9},{9,8},{10,11... | collective-permute-start | bytes 245768 | tf_op jit(solution)/shard_map/ppermute | solution.py:414
  87.8 11.2 %copy-start.5 = (f32[2560]{0:T(1024)S(1)}, f32[2560]{0:T(1024)}, u32[]{:S(2)}) copy-start(f32[2560]{0:T(1024)} %param.24) | copy-start | bytes 30724
  87.8 1.4 %collective-permute-start.8 = (bf16[32,1280]{1,0:T(8,128)(2,1)S(1)}, bf16[32,1280]{1,0:T(8,128)(2,1)S(1)}, u32[]{:S(2)}, u32[]{:S(2)}) collective-permute-start(bf16[32,1280]{1,0:T(8,128)(2,1)S(1)} %get-tuple-element.40), channel_id=1, source_target_pairs={{0,1},{1,0},{2,3},{3,2},{4,5},{5,4},{6,7},{7,6},{8,9},{9,8},{10,11... | collective-permute-start | bytes 245768 | tf_op jit(solution)/shard_map/ppermute | solution.py:414
  89.2 5.1 %collective-permute-start.10 = (bf16[32,1280]{1,0:T(8,128)(2,1)S(1)}, bf16[32,1280]{1,0:T(8,128)(2,1)S(1)}, u32[]{:S(2)}, u32[]{:S(2)}) collective-permute-start(bf16[32,1280]{1,0:T(8,128)(2,1)S(1)} %add_pair.1), channel_id=1, source_target_pairs={{0,6},{1,7},{2,4},{3,5},{4,2},{5,3},{6,0},{7,1},{8,14},{9,15},{10,... | collective-permute-start | bytes 245768 | tf_op jit(solution)/shard_map/ppermute | solution.py:414
  91.7 4.8 %collective-permute-start.11 = (bf16[32,1280]{1,0:T(8,128)(2,1)S(1)}, bf16[32,1280]{1,0:T(8,128)(2,1)S(1)}, u32[]{:S(2)}, u32[]{:S(2)}) collective-permute-start(bf16[32,1280]{1,0:T(8,128)(2,1)S(1)} %add_pair.1), channel_id=1, source_target_pairs={{0,4},{1,5},{2,6},{3,7},{4,0},{5,1},{6,2},{7,3},{8,12},{9,13},{10,... | collective-permute-start | bytes 245768 | tf_op jit(solution)/shard_map/ppermute | solution.py:414
  92.0 4.5 %collective-permute-start.9 = (bf16[32,1280]{1,0:T(8,128)(2,1)S(1)}, bf16[32,1280]{1,0:T(8,128)(2,1)S(1)}, u32[]{:S(2)}, u32[]{:S(2)}) collective-permute-start(bf16[32,1280]{1,0:T(8,128)(2,1)S(1)} %add_pair.1), channel_id=1, source_target_pairs={{0,2},{1,3},{2,0},{3,1},{4,6},{5,7},{6,4},{7,5},{8,10},{9,11},{10,... | collective-permute-start | bytes 245768 | tf_op jit(solution)/shard_map/ppermute | solution.py:414
  96.5 3.8 %collective-permute-start.12 = (bf16[32,1280]{1,0:T(8,128)(2,1)S(1)}, bf16[32,1280]{1,0:T(8,128)(2,1)S(1)}, u32[]{:S(2)}, u32[]{:S(2)}) collective-permute-start(bf16[32,1280]{1,0:T(8,128)(2,1)S(1)} %add_chips.1.own_ref), channel_id=1, source_target_pairs={{0,1},{1,0},{2,3},{3,2},{4,5},{5,4},{6,7},{7,6},{8,9},{9,8},{10,11... | collective-permute-start | bytes 245768 | tf_op jit(solution)/shard_map/ppermute | solution.py:414

commit v8 on v7

--- a/solution.py
+++ b/solution.py
@@ -276,33 +276,39 @@
     far_ref,
     acc_ref,
     square_ref,
-    other_weight_ref,
+    first_ref,
+    second_ref,
     rest_ref,
     copied,
 ):
     half = own_ref.shape[1]
     core = place_ref[0] % 2
-    near_rows = other_weight_ref.shape[0]
-    copy = pltpu.make_async_copy(
-        far_ref.at[pl.ds(pl.multiple_of((1 - core) * half, 128), near_rows)],
-        other_weight_ref,
-        copied.at[0],
-    )
+    quarter = half // 2
+    copies = [
+        pltpu.make_async_copy(
+            far_ref.at[pl.ds(pl.multiple_of((1 - core) * half + index * quarter, 128), quarter)],
+            ref,
+            copied.at[index],
+        )
+        for index, ref in enumerate((first_ref, second_ref))
+    ]
     own_rows = front_ref.shape[0]
     rest = pltpu.make_async_copy(
         far_ref.at[pl.ds(pl.multiple_of(core * half + own_rows, 128), half - own_rows)],
         rest_ref,
-        copied.at[1],
+        copied.at[2],
     )
     rest.start()
-    copy.start()
+    for copy in copies:
+        copy.start()
     own = own_ref[...].astype(F32)
     square_ref[...] = jnp.broadcast_to(jnp.sum(own * own, axis=1, keepdims=True), square_ref.shape)
     scaled = (own * gain_ref[core]).astype(BF16)
     acc = jnp.dot(scaled[:, :own_rows], front_ref[...], preferred_element_type=F32)
     rest.wait()
     acc_ref[...] = acc + jnp.dot(scaled[:, own_rows:], rest_ref[...], preferred_element_type=F32)
-    copy.wait()
+    for copy in copies:
+        copy.wait()
 
 
 def project_other(
@@ -312,22 +318,14 @@
     gain_ref,
     acc_ref,
     square_ref,
-    front_ref,
-    far_ref,
+    first_ref,
+    second_ref,
     shard_ref,
     out_ref,
-    rest_ref,
-    copied,
 ):
     half = own_ref.shape[1]
     core = place_ref[0] % 2
-    near_rows = front_ref.shape[0]
-    copy = pltpu.make_async_copy(
-        far_ref.at[pl.ds(pl.multiple_of((1 - core) * half + near_rows, 128), half - near_rows)],
-        rest_ref,
-        copied.at[0],
-    )
-    copy.start()
+    quarter = half // 2
     part = shard_ref.shape[1]
     parts = half // part
     for place in range(2 * parts):
@@ -341,9 +339,8 @@
     other = other_ref[...].astype(F32)
     square = square_ref[:, :1] + jnp.sum(other * other, axis=1, keepdims=True)
     scaled = (other * gain_ref[1 - core]).astype(BF16)
-    acc = acc_ref[...] + jnp.dot(scaled[:, :near_rows], front_ref[...], preferred_element_type=F32)
-    copy.wait()
-    acc = acc + jnp.dot(scaled[:, near_rows:], rest_ref[...], preferred_element_type=F32)
+    acc = acc_ref[...] + jnp.dot(scaled[:, :quarter], first_ref[...], preferred_element_type=F32)
+    acc = acc + jnp.dot(scaled[:, quarter:], second_ref[...], preferred_element_type=F32)
     out_ref[...] = (acc * lax.rsqrt(square / (2 * half) + 1e-06)).astype(BF16)
 
 
@@ -537,7 +534,6 @@
     others = [partner(chip_half, distance) for distance in DISTANCES[1:]]
     columns = qkv_weight.shape[1]
     own_rows = 1152
-    near_rows = 1152
     own_weight, fetched = pl.pallas_call(
         fetch_half,
         out_shape=[pltpu.VMEM((own_rows, columns), BF16), jax.ShapeDtypeStruct((8, 128), F32)],
@@ -551,23 +547,21 @@
     )
     other_half = partner(after_half, 1)
     gains = next_gain.reshape(2, 1, half)
-    acc, square, other_weight = call(
+    acc, square, *other_weights = call(
         project_own,
-        [((row_count, columns), F32, True), ((row_count, 128), F32, True), ((near_rows, columns), BF16, True)],
+        [((row_count, columns), F32, True), ((row_count, 128), F32, True)]
+        + [((half // 2, columns), BF16, True)] * 2,
         [place],
         [after_half, gains, own_weight],
         [qkv_weight],
         [((half - own_rows, columns), BF16)],
-        2,
+        3,
     )
     shard_after, next_qkv = call(
         project_other,
         [((row_count, part_width), BF16, False), ((row_count, columns), BF16, False)],
         [place],
-        [after_half, other_half, gains, acc, square, other_weight],
-        [qkv_weight],
-        [((half - near_rows, columns), BF16)],
-        1,
+        [after_half, other_half, gains, acc, square, *other_weights],
     )
     return (attended_out, shard_after, next_qkv)
 

time: 103 us -> 102 us (level)
  no operation moved by 1% of the time
where the time goes in v8:
time: 102 us; the launch traced here: 101 us
  starting transfers between devices  42.2 us (41%)
  waiting for transfers between devices  32.5 us (32%)
  Pallas kernels  20.6 us (20%)
  between operations  2.83 us (3%)
  other arithmetic  1.72 us (2%)
  local copies, waits for them, and re-layouts  1.52 us (1%)
    all_to_all x2, waiting for transfers between devices, exchange(): return lax.all_to_all(copies, axis, split_axis=0, concat_axis=0, tiled=True)  26.2 us
    ppermute x13, starting transfers between devices, partner(): return lax.ppermute(block, 'mlp', [(i, i ^ distance) for i in range(count)])  21.9 us
    all_to_all x2, starting transfers between devices, exchange(): return lax.all_to_all(copies, axis, split_axis=0, concat_axis=0, tiled=True)  20.3 us
    pallas_call x11, Pallas kernels, call(): pl.pallas_call(body, out_shape=[pltpu.VMEM(shape, dtype) if stays else ja...  11.1 us
    ppermute x13, waiting for transfers between devices, partner(): return lax.ppermute(block, 'mlp', [(i, i ^ distance) for i in range(count)])  6.29 us
    pallas_call x3, Pallas kernels, fetch(): pl.pallas_call(fetch_rows, out_shape=[pltpu.VMEM((rows,) + far.shape[1:],...  6.09 us
  transfers between devices with their start and end apart: 15, of which 7 were waited for; matrix products, arithmetic and copies ran while one was open for 3% of the time, Pallas kernels for 9%

profile of v8, /device:TPU:1, one launch (start us, length us, event | category | flops | bytes accessed | tf_op | source)
XLA Modules:
  0.0 101.3 jit_solution(172099885865028578)
XLA Ops:
  0.6 0.0 copy-start
  0.6 1.7 %copy_queries.1.refs_0_ = bf16[32,4,2560]{2,1,0:T(4,128)(2,1)} custom-call(bf16[4,2560]{1,0:T(4,128)(2,1)} %queries_ref.3), custom_call_target="tpu_custom_call" | custom-call | tf_op jit(solution)/shard_map/copy_queries/pallas_call | solution.py:450
  2.3 11.9 %all-to-all-start = ((bf16[32,4,2560]{2,1,0:T(4,128)(2,1)}), bf16[32,4,2560]{2,1,0:T(4,128)(2,1)S(1)}, u32[]{:S(2)}, u32[]{:S(2)}) async-start(bf16[32,4,2560]{2,1,0:T(4,128)(2,1)} %copy_queries.1.refs_0_), calls=%async_computation | async-start | bytes 1310720 | tf_op jit(solution)/shard_map/all_to_all | solution.py:406
  14.2 0.8 reshape.58
  15.0 2.0 %fetch_rows.3 = (bf16[11,128,512]{2,1,0:T(8,128)(2,1)S(1)}, f32[8,128]{1,0:T(8,128)}) custom-call(bf16[32,4,2560]{2,1,0:T(4,128)(2,1)} %copy_queries.1.refs_0_, bf16[17,128,512]{2,1,0:T(8,128)(2,1)} %far_ref.3), custom_call_target="tpu_custom_call" | custom-call | tf_op jit(solution)/shard_map/fetch_rows/pallas_call | solution.py:393
  16.9 0.7 dynamic-slice_reduce_fusion.length_ref
  17.7 0.1 add_add_fusion
  17.7 1.0 select_reduce_fusion.code_ref
  18.7 11.8 %all-to-all-done.rows_ref = bf16[32,4,2560]{2,1,0:T(4,128)(2,1)S(1)} async-done(((bf16[32,4,2560]{2,1,0:T(4,128)(2,1)}), bf16[32,4,2560]{2,1,0:T(4,128)(2,1)S(1)}, u32[]{:S(2)}, u32[]{:S(2)}) %all-to-all-start) | async-done | bytes 655392 | tf_op jit(solution)/shard_map/all_to_all | solution.py:406
  30.6 3.9 %attend_pages.1.refs_0_ = bf16[32,4,2688]{2,1,0:T(4,128)(2,1)} custom-call(s32[17]{0:T(128)} %select_reduce_fusion.code_ref, s32[32]{0:T(128)} %dynamic-slice_reduce_fusion.length_ref, bf16[32,4,2560]{2,1,0:T(4,128)(2,1)S(1)} %all-to-all-done.rows_ref, bf16[11,128,512]{2,1,0:T(8,128)(2,1)S(1)} %get-tuple-element.27.front_ref, bf16[17,128,512]{2,1,0:T(8,128)(2,1)} %far_ref.3), custom_call_target="tpu_custom_call" | custom-call | tf_op jit(solution)/shard_map/attend_pages/pallas_call | solution.py:362
  34.5 8.4 %all-to-all-start.1 = ((bf16[32,4,2688]{2,1,0:T(4,128)(2,1)}), bf16[32,4,2688]{2,1,0:T(4,128)(2,1)S(1)}, u32[]{:S(2)}, u32[]{:S(2)}) async-start(bf16[32,4,2688]{2,1,0:T(4,128)(2,1)} %attend_pages.1.refs_0_), calls=%async_computation.1 | async-start | bytes 1376256 | tf_op jit(solution)/shard_map/all_to_all | solution.py:406
  42.9 0.6 fusion
  45.5 0.3 attend_new.1
  45.9 14.4 %all-to-all-done.1.got_ref = bf16[32,4,2688]{2,1,0:T(4,128)(2,1)S(1)} async-done(((bf16[32,4,2688]{2,1,0:T(4,128)(2,1)}), bf16[32,4,2688]{2,1,0:T(4,128)(2,1)S(1)}, u32[]{:S(2)}, u32[]{:S(2)}) %all-to-all-start.1) | async-done | bytes 688160 | tf_op jit(solution)/shard_map/all_to_all | solution.py:406
  60.2 0.2 merge_new.1.refs_4_.first_ref
  60.4 1.4 %collective-permute-start = (bf16[4,2560]{1,0:T(4,128)(2,1)S(1)}, bf16[4,2560]{1,0:T(4,128)(2,1)S(1)}, u32[]{:S(2)}, u32[]{:S(2)}) collective-permute-start(bf16[4,2560]{1,0:T(4,128)(2,1)S(1)} %merge_new.1.refs_4_.first_ref), channel_id=1, source_target_pairs={{0,2},{1,3},{2,0},{3,1},{4,6},{5,7},{6,4},{7,5},{8,10},{9,11},{10,... | collective-permute-start | bytes 61448 | tf_op jit(solution)/shard_map/ppermute | solution.py:411
  61.8 1.9 %collective-permute-start.1 = (bf16[4,2560]{1,0:T(4,128)(2,1)S(1)}, bf16[4,2560]{1,0:T(4,128)(2,1)S(1)}, u32[]{:S(2)}, u32[]{:S(2)}) collective-permute-start(bf16[4,2560]{1,0:T(4,128)(2,1)S(1)} %merge_new.1.refs_4_.first_ref), channel_id=1, source_target_pairs={{0,6},{1,7},{2,4},{3,5},{4,2},{5,3},{6,0},{7,1},{8,14},{9,15},{10,... | collective-permute-start | bytes 61448 | tf_op jit(solution)/shard_map/ppermute | solution.py:411
  63.7 0.7 collective-permute-start.2
  64.4 2.0 %fetch_rows.5 = (bf16[128,2560]{1,0:T(8,128)(2,1)S(1)}, bf16[128,2560]{1,0:T(8,128)(2,1)S(1)}, bf16[64,2560]{1,0:T(8,128)(2,1)S(1)}, f32[8,128]{1,0:T(8,128)}) custom-call(bf16[32,4,2688]{2,1,0:T(4,128)(2,1)} %attend_pages.1.refs_0_, bf16[320,2560]{1,0:T(8,128)(2,1)} %bitcast.9, bf16[320,2560]{1,0:T(8,128)(2,1)} %bitcast.10, bf16[320,2560]{1,0:T(8,128)(2,1)} %bitcast.11), custom_call_target="tpu_custom_call" | custom-call | tf_op jit(solution)/shard_map/fetch_rows/pallas_call | solution.py:393
  66.4 0.0 collective-permute-done.second_ref
  66.4 0.0 collective-permute-done.1.third_ref
  66.5 1.4 %collective-permute-done.2.fourth_ref = bf16[4,2560]{1,0:T(4,128)(2,1)S(1)} collective-permute-done((bf16[4,2560]{1,0:T(4,128)(2,1)S(1)}, bf16[4,2560]{1,0:T(4,128)(2,1)S(1)}, u32[]{:S(2)}, u32[]{:S(2)}) %collective-permute-start.2) | collective-permute-done | bytes 20512 | tf_op jit(solution)/shard_map/ppermute | solution.py:411
  67.8 6.6 %collective-permute-start.3 = (bf16[4,4,2560]{2,1,0:T(4,128)(2,1)S(1)}, bf16[4,4,2560]{2,1,0:T(4,128)(2,1)S(1)}, u32[]{:S(2)}, u32[]{:S(2)}) collective-permute-start(bf16[4,4,2560]{2,1,0:T(4,128)(2,1)S(1)} %stack_blocks.2.mine_ref), channel_id=1, source_target_pairs={{0,1},{1,0},{2,3},{3,2},{4,5},{5,4},{6,7},{7,6},{8,9},{9,8},{10,11... | collective-permute-start | bytes 245768 | tf_op jit(solution)/shard_map/ppermute | solution.py:411
  74.5 0.9 collective-permute-done.3.theirs_ref
  75.4 0.6 project_out.1.first_ref
  76.0 0.5 collective-permute-start.4
  76.5 0.5 collective-permute-start.5
  77.0 2.4 %collective-permute-start.6 = (bf16[32,320]{1,0:T(8,128)(2,1)S(1)}, bf16[32,320]{1,0:T(8,128)(2,1)S(1)}, u32[]{:S(2)}, u32[]{:S(2)}) collective-permute-start(bf16[32,320]{1,0:T(8,128)(2,1)S(1)} %project_out.1.first_ref), channel_id=1, source_target_pairs={{0,4},{1,5},{2,6},{3,7},{4,0},{5,1},{6,2},{7,3},{8,12},{9,13},{10,... | collective-permute-start | bytes 61448 | tf_op jit(solution)/shard_map/ppermute | solution.py:411
  79.4 2.1 %fetch_rows.4 = (bf16[128,2560]{1,0:T(8,128)(2,1)S(1)}, bf16[128,2560]{1,0:T(8,128)(2,1)S(1)}, bf16[128,2560]{1,0:T(8,128)(2,1)S(1)}, f32[8,128]{1,0:T(8,128)}, bf16[4,2560]{1,0:T(4,128)(2,1)}) custom-call(bf16[32,4,2688]{2,1,0:T(4,128)(2,1)} %attend_pages.1.refs_0_, bf16[480,2560]{1,0:T(8,128)(2,1)} %bitcast.12, bf16[480,2560]{1,0:T(8,128)(2,1)} %bitcast.14, ...), custom_call_target="tpu_custom_call" | custom-call | tf_op jit(solution)/shard_map/fetch_rows/pallas_call | solution.py:393
  81.5 0.0 collective-permute-done.4.second_ref
  81.5 0.0 collective-permute-done.6.fourth_ref
  81.6 1.6 %collective-permute-start.7 = (bf16[4,32,320]{2,1,0:T(8,128)(2,1)S(1)}, bf16[4,32,320]{2,1,0:T(8,128)(2,1)S(1)}, u32[]{:S(2)}, u32[]{:S(2)}) collective-permute-start(bf16[4,32,320]{2,1,0:T(8,128)(2,1)S(1)} %stack_blocks.3.refs_0_), channel_id=1, source_target_pairs={{0,1},{1,0},{2,3},{3,2},{4,5},{5,4},{6,7},{7,6},{8,9},{9,8},{10,11... | collective-permute-start | bytes 245768 | tf_op jit(solution)/shard_map/ppermute | solution.py:411
  83.2 0.9 collective-permute-done.7.refs_1_
  84.2 3.7 %feed_forward.1 = (f32[32,1280]{1,0:T(8,128)S(1)}, bf16[32,1280]{1,0:T(8,128)(2,1)S(1)}, bf16[32,1280]{1,0:T(8,128)(2,1)S(1)}) custom-call(s32[1]{0:T(128)} %bitcast.5.place_ref, bf16[4,32,320]{2,1,0:T(8,128)(2,1)S(1)} %stack_blocks.3.refs_0_, bf16[4,32,320]{2,1,0:T(8,128)(2,1)S(1)} %collective-permute-done.7.refs_1_, f32[1,2560]{1,0:T(1,128)S(1)} %reshape.61.refs_2_, ...), custom_call_target="tpu_custom_call" | custom-call | tf_op jit(solution)/shard_map/feed_forward/pallas_call | solution.py:362
  87.8 0.0 copy-start.5
  87.8 0.4 collective-permute-start.8
  88.3 0.9 collective-permute-done.8.got_ref
  89.2 2.4 %collective-permute-start.10 = (bf16[32,1280]{1,0:T(8,128)(2,1)S(1)}, bf16[32,1280]{1,0:T(8,128)(2,1)S(1)}, u32[]{:S(2)}, u32[]{:S(2)}) collective-permute-start(bf16[32,1280]{1,0:T(8,128)(2,1)S(1)} %add_pair.1), channel_id=1, source_target_pairs={{0,6},{1,7},{2,4},{3,5},{4,2},{5,3},{6,0},{7,1},{8,14},{9,15},{10,... | collective-permute-start | bytes 245768 | tf_op jit(solution)/shard_map/ppermute | solution.py:411
  91.7 0.3 collective-permute-start.11
  92.0 0.6 collective-permute-start.9
  92.6 1.8 %fetch_half.1 = (bf16[1152,384]{1,0:T(8,128)(2,1)S(1)}, f32[8,128]{1,0:T(8,128)}) custom-call(s32[1]{0:T(128)} %bitcast.5.place_ref, bf16[2560,384]{1,0:T(8,128)(2,1)} %far_ref.5), custom_call_target="tpu_custom_call" | custom-call | tf_op jit(solution)/shard_map/fetch_half/pallas_call | solution.py:537
  94.3 0.0 collective-permute-done.10.second_ref
  94.3 2.1 %collective-permute-done.11.third_ref = bf16[32,1280]{1,0:T(8,128)(2,1)S(1)} collective-permute-done((bf16[32,1280]{1,0:T(8,128)(2,1)S(1)}, bf16[32,1280]{1,0:T(8,128)(2,1)S(1)}, u32[]{:S(2)}, u32[]{:S(2)}) %collective-permute-start.11) | collective-permute-done | bytes 81952 | tf_op jit(solution)/shard_map/ppermute | solution.py:411
  96.4 0.0 collective-permute-done.9.first_ref
  96.5 0.1 add_chips.1.own_ref
  96.5 2.5 %collective-permute-start.12 = (bf16[32,1280]{1,0:T(8,128)(2,1)S(1)}, bf16[32,1280]{1,0:T(8,128)(2,1)S(1)}, u32[]{:S(2)}, u32[]{:S(2)}) collective-permute-start(bf16[32,1280]{1,0:T(8,128)(2,1)S(1)} %add_chips.1.own_ref), channel_id=1, source_target_pairs={{0,1},{1,0},{2,3},{3,2},{4,5},{5,4},{6,7},{7,6},{8,9},{9,8},{10,11... | collective-permute-start | bytes 245768 | tf_op jit(solution)/shard_map/ppermute | solution.py:411
  99.1 1.3 %project_own.1 = (f32[32,384]{1,0:T(8,128)S(1)}, f32[32,128]{1,0:T(8,128)S(1)}, bf16[640,384]{1,0:T(8,128)(2,1)S(1)}, bf16[640,384]{1,0:T(8,128)(2,1)S(1)}) custom-call(s32[1]{0:T(128)} %bitcast.5.place_ref, bf16[32,1280]{1,0:T(8,128)(2,1)S(1)} %add_chips.1.own_ref, f32[2,1,1280]{2,1,0:T(1,128)S(1)} %reshape.62.gain_ref, ...), custom_call_target="tpu_custom_call" | custom-call | tf_op jit(solution)/shard_map/project_own/pallas_call | solution.py:362
  100.4 1.0 project_other.1
  (20 shorter events, 0.1 us)
Async XLA Ops:
  0.6 17.0 %copy-start = (s32[256,128]{1,0:T(8,128)S(1)}, s32[256,128]{1,0:T(8,128)}, u32[]{:S(2)}) copy-start(s32[256,128]{1,0:T(8,128)} %param.17) | copy-start | bytes 393220
  2.3 28.3 %all-to-all-start = ((bf16[32,4,2560]{2,1,0:T(4,128)(2,1)}), bf16[32,4,2560]{2,1,0:T(4,128)(2,1)S(1)}, u32[]{:S(2)}, u32[]{:S(2)}) async-start(bf16[32,4,2560]{2,1,0:T(4,128)(2,1)} %copy_queries.1.refs_0_), calls=%async_computation | async-start | bytes 1310720 | tf_op jit(solution)/shard_map/all_to_all | solution.py:406
  30.6 14.9 %copy-start.1 = (bf16[4,2560]{1,0:T(4,128)(2,1)S(1)}, bf16[4,2560]{1,0:T(4,128)(2,1)}, u32[]{:S(2)}) copy-start(bf16[4,2560]{1,0:T(4,128)(2,1)} %queries_ref.3) | copy-start | bytes 61444
  30.6 15.0 %copy-start.3 = (bf16[4,512]{1,0:T(4,128)(2,1)S(1)}, bf16[4,512]{1,0:T(4,128)(2,1)}, u32[]{:S(2)}) copy-start(bf16[4,512]{1,0:T(4,128)(2,1)} %new_ref.1) | copy-start | bytes 12292
  34.5 25.7 %all-to-all-start.1 = ((bf16[32,4,2688]{2,1,0:T(4,128)(2,1)}), bf16[32,4,2688]{2,1,0:T(4,128)(2,1)S(1)}, u32[]{:S(2)}, u32[]{:S(2)}) async-start(bf16[32,4,2688]{2,1,0:T(4,128)(2,1)} %attend_pages.1.refs_0_), calls=%async_computation.1 | async-start | bytes 1376256 | tf_op jit(solution)/shard_map/all_to_all | solution.py:406
  60.4 6.0 %collective-permute-start = (bf16[4,2560]{1,0:T(4,128)(2,1)S(1)}, bf16[4,2560]{1,0:T(4,128)(2,1)S(1)}, u32[]{:S(2)}, u32[]{:S(2)}) collective-permute-start(bf16[4,2560]{1,0:T(4,128)(2,1)S(1)} %merge_new.1.refs_4_.first_ref), channel_id=1, source_target_pairs={{0,2},{1,3},{2,0},{3,1},{4,6},{5,7},{6,4},{7,5},{8,10},{9,11},{10,... | collective-permute-start | bytes 61448 | tf_op jit(solution)/shard_map/ppermute | solution.py:411
  61.8 4.6 %collective-permute-start.1 = (bf16[4,2560]{1,0:T(4,128)(2,1)S(1)}, bf16[4,2560]{1,0:T(4,128)(2,1)S(1)}, u32[]{:S(2)}, u32[]{:S(2)}) collective-permute-start(bf16[4,2560]{1,0:T(4,128)(2,1)S(1)} %merge_new.1.refs_4_.first_ref), channel_id=1, source_target_pairs={{0,6},{1,7},{2,4},{3,5},{4,2},{5,3},{6,0},{7,1},{8,14},{9,15},{10,... | collective-permute-start | bytes 61448 | tf_op jit(solution)/shard_map/ppermute | solution.py:411
  63.7 4.1 %collective-permute-start.2 = (bf16[4,2560]{1,0:T(4,128)(2,1)S(1)}, bf16[4,2560]{1,0:T(4,128)(2,1)S(1)}, u32[]{:S(2)}, u32[]{:S(2)}) collective-permute-start(bf16[4,2560]{1,0:T(4,128)(2,1)S(1)} %merge_new.1.refs_4_.first_ref), channel_id=1, source_target_pairs={{0,4},{1,5},{2,6},{3,7},{4,0},{5,1},{6,2},{7,3},{8,12},{9,13},{10,... | collective-permute-start | bytes 61448 | tf_op jit(solution)/shard_map/ppermute | solution.py:411
  64.4 11.0 %copy-start.2 = (bf16[32,320]{1,0:T(8,128)(2,1)S(1)}, bf16[32,320]{1,0:T(8,128)(2,1)}, u32[]{:S(2)}) copy-start(bf16[32,320]{1,0:T(8,128)(2,1)} %residual_ref.1) | copy-start | bytes 61444
  67.8 7.5 %collective-permute-start.3 = (bf16[4,4,2560]{2,1,0:T(4,128)(2,1)S(1)}, bf16[4,4,2560]{2,1,0:T(4,128)(2,1)S(1)}, u32[]{:S(2)}, u32[]{:S(2)}) collective-permute-start(bf16[4,4,2560]{2,1,0:T(4,128)(2,1)S(1)} %stack_blocks.2.mine_ref), channel_id=1, source_target_pairs={{0,1},{1,0},{2,3},{3,2},{4,5},{5,4},{6,7},{7,6},{8,9},{9,8},{10,11... | collective-permute-start | bytes 245768 | tf_op jit(solution)/shard_map/ppermute | solution.py:411
  76.0 5.5 %collective-permute-start.4 = (bf16[32,320]{1,0:T(8,128)(2,1)S(1)}, bf16[32,320]{1,0:T(8,128)(2,1)S(1)}, u32[]{:S(2)}, u32[]{:S(2)}) collective-permute-start(bf16[32,320]{1,0:T(8,128)(2,1)S(1)} %project_out.1.first_ref), channel_id=1, source_target_pairs={{0,2},{1,3},{2,0},{3,1},{4,6},{5,7},{6,4},{7,5},{8,10},{9,11},{10,... | collective-permute-start | bytes 61448 | tf_op jit(solution)/shard_map/ppermute | solution.py:411
  76.5 5.0 %collective-permute-start.5 = (bf16[32,320]{1,0:T(8,128)(2,1)S(1)}, bf16[32,320]{1,0:T(8,128)(2,1)S(1)}, u32[]{:S(2)}, u32[]{:S(2)}) collective-permute-start(bf16[32,320]{1,0:T(8,128)(2,1)S(1)} %project_out.1.first_ref), channel_id=1, source_target_pairs={{0,6},{1,7},{2,4},{3,5},{4,2},{5,3},{6,0},{7,1},{8,14},{9,15},{10,... | collective-permute-start | bytes 61448 | tf_op jit(solution)/shard_map/ppermute | solution.py:411
  77.0 4.5 %collective-permute-start.6 = (bf16[32,320]{1,0:T(8,128)(2,1)S(1)}, bf16[32,320]{1,0:T(8,128)(2,1)S(1)}, u32[]{:S(2)}, u32[]{:S(2)}) collective-permute-start(bf16[32,320]{1,0:T(8,128)(2,1)S(1)} %project_out.1.first_ref), channel_id=1, source_target_pairs={{0,4},{1,5},{2,6},{3,7},{4,0},{5,1},{6,2},{7,3},{8,12},{9,13},{10,... | collective-permute-start | bytes 61448 | tf_op jit(solution)/shard_map/ppermute | solution.py:411
  79.4 3.8 %copy-start.4 = (f32[2560]{0:T(1024)S(1)}, f32[2560]{0:T(1024)}, u32[]{:S(2)}) copy-start(f32[2560]{0:T(1024)} %param.20) | copy-start | bytes 30724
  81.6 2.6 %collective-permute-start.7 = (bf16[4,32,320]{2,1,0:T(8,128)(2,1)S(1)}, bf16[4,32,320]{2,1,0:T(8,128)(2,1)S(1)}, u32[]{:S(2)}, u32[]{:S(2)}) collective-permute-start(bf16[4,32,320]{2,1,0:T(8,128)(2,1)S(1)} %stack_blocks.3.refs_0_), channel_id=1, source_target_pairs={{0,1},{1,0},{2,3},{3,2},{4,5},{5,4},{6,7},{7,6},{8,9},{9,8},{10,11... | collective-permute-start | bytes 245768 | tf_op jit(solution)/shard_map/ppermute | solution.py:411
  87.8 11.2 %copy-start.5 = (f32[2560]{0:T(1024)S(1)}, f32[2560]{0:T(1024)}, u32[]{:S(2)}) copy-start(f32[2560]{0:T(1024)} %param.24) | copy-start | bytes 30724
  87.8 1.4 %collective-permute-start.8 = (bf16[32,1280]{1,0:T(8,128)(2,1)S(1)}, bf16[32,1280]{1,0:T(8,128)(2,1)S(1)}, u32[]{:S(2)}, u32[]{:S(2)}) collective-permute-start(bf16[32,1280]{1,0:T(8,128)(2,1)S(1)} %get-tuple-element.41), channel_id=1, source_target_pairs={{0,1},{1,0},{2,3},{3,2},{4,5},{5,4},{6,7},{7,6},{8,9},{9,8},{10,11... | collective-permute-start | bytes 245768 | tf_op jit(solution)/shard_map/ppermute | solution.py:411
  89.2 5.1 %collective-permute-start.10 = (bf16[32,1280]{1,0:T(8,128)(2,1)S(1)}, bf16[32,1280]{1,0:T(8,128)(2,1)S(1)}, u32[]{:S(2)}, u32[]{:S(2)}) collective-permute-start(bf16[32,1280]{1,0:T(8,128)(2,1)S(1)} %add_pair.1), channel_id=1, source_target_pairs={{0,6},{1,7},{2,4},{3,5},{4,2},{5,3},{6,0},{7,1},{8,14},{9,15},{10,... | collective-permute-start | bytes 245768 | tf_op jit(solution)/shard_map/ppermute | solution.py:411
  91.7 4.8 %collective-permute-start.11 = (bf16[32,1280]{1,0:T(8,128)(2,1)S(1)}, bf16[32,1280]{1,0:T(8,128)(2,1)S(1)}, u32[]{:S(2)}, u32[]{:S(2)}) collective-permute-start(bf16[32,1280]{1,0:T(8,128)(2,1)S(1)} %add_pair.1), channel_id=1, source_target_pairs={{0,4},{1,5},{2,6},{3,7},{4,0},{5,1},{6,2},{7,3},{8,12},{9,13},{10,... | collective-permute-start | bytes 245768 | tf_op jit(solution)/shard_map/ppermute | solution.py:411
  92.0 4.5 %collective-permute-start.9 = (bf16[32,1280]{1,0:T(8,128)(2,1)S(1)}, bf16[32,1280]{1,0:T(8,128)(2,1)S(1)}, u32[]{:S(2)}, u32[]{:S(2)}) collective-permute-start(bf16[32,1280]{1,0:T(8,128)(2,1)S(1)} %add_pair.1), channel_id=1, source_target_pairs={{0,2},{1,3},{2,0},{3,1},{4,6},{5,7},{6,4},{7,5},{8,10},{9,11},{10,... | collective-permute-start | bytes 245768 | tf_op jit(solution)/shard_map/ppermute | solution.py:411
  96.5 3.8 %collective-permute-start.12 = (bf16[32,1280]{1,0:T(8,128)(2,1)S(1)}, bf16[32,1280]{1,0:T(8,128)(2,1)S(1)}, u32[]{:S(2)}, u32[]{:S(2)}) collective-permute-start(bf16[32,1280]{1,0:T(8,128)(2,1)S(1)} %add_chips.1.own_ref), channel_id=1, source_target_pairs={{0,1},{1,0},{2,3},{3,2},{4,5},{5,4},{6,7},{7,6},{8,9},{9,8},{10,11... | collective-permute-start | bytes 245768 | tf_op jit(solution)/shard_map/ppermute | solution.py:411
